TPU v7x, 512 devices: a whole 4x8x8 slice. The times are simulated.
512 devices in a mesh: grp: 64 (over y, z), tp: 8 (over x, core).
Axes of the slice: x: 4, y: 8, z: 8, core: 2. Of those that a mesh axis runs over, the one named last changes fastest.
Arguments:
- queries: bfloat16 [512, 2048], P('grp', 'tp'), may hold values from -8 to 8
- new_kv: bfloat16 [512, 2, 512], P('grp', None, 'tp'), may hold values from -6 to 6
- home_cache: bfloat16 [512, 2, 8, 512, 128], P('grp', None, 'tp'), may hold values from -28 to 28
- help_cache: bfloat16 [256, 2, 8, 512, 128], P('grp', None, 'tp'), may hold values from -6 to 6
- lengths: int32 [512], P('grp'), may hold values from 2 to 2048, as said below
- split_at: int32 [512], P('grp'), may hold values from 1 to 1024, as said below
- helper_req: int32 [256], P('grp'), may hold values from 0 to 511, as said below
- out_weight: bfloat16 [2048, 2048], P('tp'), may hold values from -0.125 to 0.125
Outputs:
- attn_out: bfloat16 [512, 2048], P('grp', 'tp')
Inputs may be any that keep to these rules, and one draw needn't show every extreme that they name: `lengths`: in each aligned block of 8 requests exactly 4 have more than 1024 cached positions. `split_at`: equal to the length for requests of 1024 positions or fewer; otherwise between length - 1024 and min(1024, length - 1). `helper_req`: groups come in pairs; the 4 helper slots of a group serve, in increasing order, the requests of its partner group that have more than 1024 positions, so each such request has exactly one helper slot and all values are distinct.
All inputs are finite; a program needn't handle non-finite values.
Results may differ from a plain program's by a relative error of at most 0.007.
Values may be sent and summed in bfloat16 or wider, within the bound.
A program may use at most 192 MiB of HBM per device.

v0:
```python
import jax
import jax.numpy as jnp
from jax import lax
from jax.sharding import PartitionSpec as P


def attend(queries, cache, count, fresh):
    row_count = queries.shape[0]
    kv_heads = cache.shape[2]
    head_width = cache.shape[4] // 2
    context = cache.shape[3] * 2
    group_size = queries.shape[1] // (kv_heads * head_width)
    score_scale = head_width ** (-0.5)
    head_rows = queries.reshape(row_count, kv_heads, group_size, head_width)
    key_rows = cache[:, 0].reshape(row_count, kv_heads, context, head_width)
    value_rows = cache[:, 1].reshape(row_count, kv_heads, context, head_width)
    scores = (
        jnp.einsum("nkgd,nkpd->nkgp", head_rows, key_rows, preferred_element_type=jnp.float32)
        * score_scale
    )
    inside = (jnp.arange(context)[None, :] < count[:, None])[:, None, None, :]
    top_score = jnp.max(jnp.where(inside, scores, -1e30), axis=-1)
    if fresh is not None:
        fresh_key = fresh[:, 0].reshape(row_count, kv_heads, head_width)
        fresh_score = (
            jnp.einsum("nkgd,nkd->nkg", head_rows, fresh_key, preferred_element_type=jnp.float32)
            * score_scale
        )
        top_score = jnp.maximum(top_score, fresh_score)
    weights = jnp.where(inside, jnp.exp(scores - top_score[..., None]), 0.0).astype(jnp.bfloat16)
    weight_sum = jnp.sum(weights.astype(jnp.float32), axis=-1)
    mixed_sum = jnp.einsum(
        "nkgp,nkpd->nkgd", weights, value_rows, preferred_element_type=jnp.float32
    )
    if fresh is not None:
        fresh_weight = lax.optimization_barrier(
            jnp.exp(fresh_score - top_score).astype(jnp.bfloat16)
        ).astype(jnp.float32)
        weight_sum = weight_sum + fresh_weight
        fresh_value = fresh[:, 1].reshape(row_count, kv_heads, 1, head_width).astype(jnp.float32)
        mixed_sum = mixed_sum + fresh_weight[..., None] * fresh_value
    return (
        top_score.reshape(row_count, -1),
        weight_sum.reshape(row_count, -1),
        mixed_sum.reshape(row_count, -1, head_width),
    )


def per_device(queries, new_kv, home_cache, help_cache, lengths, split_at, helper_req, out_weight):
    row_count = queries.shape[0]
    total_rows = row_count * lax.axis_size("grp")
    row_ids = jnp.arange(total_rows)
    help_sel = helper_req[:, None] == row_ids[None, :]
    everyone, all_lengths, all_splits = (
        lax.all_gather(queries, "grp", axis=0, tiled=True),
        lax.all_gather(lengths, "grp", axis=0, tiled=True),
        lax.all_gather(split_at, "grp", axis=0, tiled=True),
    )
    help_queries = jnp.dot(
        help_sel.astype(jnp.bfloat16), everyone, preferred_element_type=jnp.float32
    ).astype(jnp.bfloat16)
    help_count = jnp.sum(jnp.where(help_sel, (all_lengths - all_splits)[None, :], 0), axis=1)
    home_m, home_l, home_u = attend(queries, home_cache, split_at, new_kv)
    help_m, help_l, help_u = attend(help_queries, help_cache, help_count, None)
    row_start = lax.axis_index("grp") * row_count
    all_m, all_l, all_u, all_req = (
        lax.all_gather(help_m, "grp", axis=0, tiled=True),
        lax.all_gather(help_l, "grp", axis=0, tiled=True),
        lax.all_gather(help_u, "grp", axis=0, tiled=True),
        lax.all_gather(helper_req, "grp", axis=0, tiled=True),
    )
    own_ids = row_start + jnp.arange(row_count)
    own_sel = own_ids[:, None] == all_req[None, :]
    far_m = jnp.max(jnp.where(own_sel[:, :, None], all_m[None], -1e30), axis=1)
    far_l = jnp.sum(jnp.where(own_sel[:, :, None], all_l[None], 0.0), axis=1)
    far_u = jnp.sum(jnp.where(own_sel[:, :, None, None], all_u[None], 0.0), axis=1)
    top_score = jnp.maximum(home_m, far_m)
    home_e = jnp.exp(home_m - top_score)
    far_e = jnp.exp(far_m - top_score)
    numerator = home_u * home_e[..., None] + far_u * far_e[..., None]
    denominator = home_l * home_e + far_l * far_e
    heads_out = numerator / denominator[..., None]
    mix = heads_out.reshape(row_count, -1).astype(jnp.bfloat16)
    partial_out = jnp.dot(mix, out_weight, preferred_element_type=jnp.float32)
    return lax.psum_scatter(partial_out, "tp", scatter_dimension=1, tiled=True).astype(jnp.bfloat16)


def solution(mesh):
    return jax.shard_map(
        per_device,
        mesh=mesh,
        in_specs=(
            P("grp", "tp"),
            P("grp", None, "tp"),
            P("grp", None, "tp", None, None),
            P("grp", None, "tp", None, None),
            P("grp"),
            P("grp"),
            P("grp"),
            P("tp", None),
        ),
        out_specs=P("grp", "tp"),
        check_vma=False,
    )
```

profile of v0, /device:TPU:1, one launch (start us, length us, event | category | flops | bytes accessed | tf_op | source)
XLA Modules:
  0.0 292.1 jit_solution(9021844830264315112)
XLA Ops:
  6.5 0.9 reshape.232
  7.4 45.1 %all_gather.24 = bf16[512,256]{1,0:T(8,128)(2,1)S(1)} all-gather(bf16[8,256]{1,0:T(8,128)(2,1)} %param.8), channel_id=1, replica_groups=mesh['grp'=64,'tp'=8] {'grp'}, dimensions={0}, use_global_device_ids=true | all-gather | bytes 266240 | tf_op jit(solution)/shard_map/all_gather | solution.py:55
  52.5 1.3 dynamic-slice
  55.1 0.7 iota_compare_fusion
  55.8 0.8 dynamic-update-slice.2
  56.7 0.8 dynamic-update-slice.1
  57.5 0.8 dynamic-update-slice
  58.4 17.1 %all-reduce.3 = (s32[512]{0:T(512)S(1)}, s32[512]{0:T(512)S(1)}, s32[256]{0:T(256)S(1)}) all-reduce(s32[512]{0:T(512)S(1)} %dynamic-update-slice.1, s32[512]{0:T(512)S(1)} %dynamic-update-slice.2, s32[256]{0:T(256)S(1)} %dynamic-update-slice), channel_id=1, replica_groups=mesh['grp'=64,'tp'=8] {'grp'}, use_global_device_ids=true, to_apply=%add.1 | all-reduce | flops 1280 | bytes 10240
  75.4 0.8 select_reduce_fusion.5
  76.3 0.8 slice_convert_fusion
  77.1 0.8 convolution_convert_fusion
  78.0 1.3 fusion.14
  79.3 0.4 reshape.237
  79.7 0.5 select_reduce_fusion.2
  80.2 0.2 convert_reduce_fusion.1
  80.4 35.5 %all-gather.1 = f32[64,4,4]{2,1,0:T(4,128)S(1)} all-gather(f32[1,4,4]{2,1,0:T(4,128)S(1)} %bitcast.43), channel_id=1, replica_groups=mesh['grp'=64,'tp'=8] {'grp'}, dimensions={0}, use_global_device_ids=true | all-gather | bytes 4160 | tf_op jit(solution)/shard_map/all_gather | solution.py:68
  116.0 34.9 %all-gather = f32[64,4,4]{2,1,0:T(4,128)S(1)} all-gather(f32[1,4,4]{2,1,0:T(4,128)S(1)} %bitcast.40), channel_id=1, replica_groups=mesh['grp'=64,'tp'=8] {'grp'}, dimensions={0}, use_global_device_ids=true | all-gather | bytes 4160 | tf_op jit(solution)/shard_map/all_gather | solution.py:67
  151.4 0.4 reshape.238
  151.8 0.3 fusion.10
  152.1 35.8 %all_gather.26 = f32[256,4,64]{2,1,0:T(4,128)S(1)} all-gather(f32[4,4,64]{2,1,0:T(4,128)S(1)} %fusion.10), channel_id=1, replica_groups=mesh['grp'=64,'tp'=8] {'grp'}, dimensions={0}, use_global_device_ids=true | all-gather | bytes 266240 | tf_op jit(solution)/shard_map/all_gather | solution.py:69
  187.9 0.2 copy.42
  188.1 0.4 select_reduce_fusion
  188.5 3.1 %fusion.13 = (bf16[8,1,1,512,128]{4,3,2,1,0:T(8,128)(2,1)}, bf16[8,1,1,512,128]{4,3,2,1,0:T(8,128)(2,1)}) fusion(bf16[8,2,1,512,128]{4,3,2,1,0:T(8,128)(2,1)} %param.10), kind=kLoop, calls=%fused_computation.39 | loop fusion | bytes 4194304 | tf_op jit(solution)/shard_map/slice | solution.py:15
  191.6 2.7 reshape.233
  194.3 0.1 fusion.7
  194.5 0.7 select_reduce_fusion.1
  195.4 0.2 convert_reduce_fusion
  195.8 2.7 reshape.235
  198.6 0.4 fusion.3
  199.1 0.9 fusion.15
  200.0 84.0 %reduce-scatter.2.cloned.1.call-done = f32[8,256]{1,0:T(8,128)} async-done(((f32[8,2048]{1,0:T(8,128)}), f32[8,256]{1,0:T(8,128)}) %reduce-scatter.2.cloned.1.call-update) | async-done | bytes 8208 | tf_op jit(solution)/shard_map/reduce_scatter | solution.py:85
  284.0 1.3 convert_element_type.61
  (27 shorter events, 1.2 us)
Async XLA Ops:
  6.5 192.6 %copy-start = (bf16[256,2048]{1,0:T(8,128)(2,1)S(1)}, bf16[256,2048]{1,0:T(8,128)(2,1)}, u32[]{:S(2)}) copy-start(bf16[256,2048]{1,0:T(8,128)(2,1)} %param.15) | copy-start | bytes 3145732
  6.5 277.5 %reduce-scatter.2.cloned.1.call-start = ((), (), s32[]{:S(2)}) async-start(), calls=%async_computation.1 | async-start | bytes 73728 | tf_op jit(solution)/shard_map/reduce_scatter | solution.py:85
Sparse Core Ops, SparseCore 0:
  200.1 83.8 reduce-scatter.1
where the time goes:
time: 293 us; the launch traced here: 292 us
  blocking collectives  168 us (57%)
  waiting for transfers between devices  84 us (29%)
  local copies, waits for them, and re-layouts  16.4 us (6%)
  between operations  14.8 us (5%)
  other arithmetic  4.71 us (2%)
  matrix products  3.79 us (1%)
    reduce_scatter x1, waiting for transfers between devices, per_device(): lax.psum_scatter(partial_out, 'tp', scatter_dimension=1, tiled=True)  84 us
    all_gather x1, blocking collectives, per_device(): lax.all_gather(queries, 'grp', axis=0, tiled=True)  45.1 us
    all_gather x1, blocking collectives, per_device(): lax.all_gather(help_u, 'grp', axis=0, tiled=True)  35.8 us
    all_gather x1, blocking collectives, per_device(): lax.all_gather(help_l, 'grp', axis=0, tiled=True)  35.5 us
    all_gather x1, blocking collectives, per_device(): lax.all_gather(help_m, 'grp', axis=0, tiled=True)  34.9 us
    unnamed x1, blocking collectives  17.1 us
    another operation x6, local copies, waits for them, and re-layouts  7.24 us
  transfers between devices with their start and end apart: 1, of which 1 were waited for; matrix products, arithmetic and copies ran while one was open for 0% of the time, Pallas kernels for 0%

commit v1 on v0

--- a/solution.py
+++ b/solution.py
@@ -1,7 +1,14 @@
+import functools
+
 import jax
 import jax.numpy as jnp
 from jax import lax
+from jax.experimental import pallas as pl
+from jax.experimental.pallas import tpu as pltpu
 from jax.sharding import PartitionSpec as P
+
+MESH = pl.DeviceIdType.MESH
+LONG_AT = 1024
 
 
 def attend(queries, cache, count, fresh):
@@ -46,34 +53,172 @@
     )
 
 
+def gather_kernel(n, x_ref, out_ref, held, send_sem, recv_sem):
+    me = lax.axis_index("grp")
+    col = lax.axis_index("tp")
+
+    barrier = pltpu.get_barrier_semaphore()
+
+    def greet(k, carry):
+        peer = lax.rem(me + k, n)
+        pl.semaphore_signal(barrier, inc=1, device_id=(peer, col), device_id_type=MESH)
+        return carry
+
+    lax.fori_loop(1, n, greet, 0)
+    pl.semaphore_wait(barrier, n - 1)
+
+    def copy_to(k):
+        peer = lax.rem(me + k, n)
+        return pltpu.make_async_remote_copy(
+            src_ref=x_ref,
+            dst_ref=held.at[me],
+            send_sem=send_sem.at[k],
+            recv_sem=recv_sem.at[k],
+            device_id=(peer, col),
+            device_id_type=MESH,
+        )
+
+    def copy_from(k):
+        source = lax.rem(me + n - k, n)
+        return pltpu.make_async_remote_copy(
+            src_ref=x_ref,
+            dst_ref=held.at[source],
+            send_sem=send_sem.at[k],
+            recv_sem=recv_sem.at[k],
+            device_id=(source, col),
+            device_id_type=MESH,
+        )
+
+    def start(k, carry):
+        copy_to(k).start()
+        return carry
+
+    lax.fori_loop(1, n, start, 0)
+
+    def finish(k, carry):
+        copy_to(k).wait_send()
+        copy_from(k).wait_recv()
+        return carry
+
+    lax.fori_loop(1, n, finish, 0)
+    held[me] = x_ref[...]
+    out_ref[...] = held[...]
+
+
+def gather_grp(x, n, cid):
+    return pl.pallas_call(
+        functools.partial(gather_kernel, n),
+        out_shape=jax.ShapeDtypeStruct((n,) + x.shape, x.dtype),
+        in_specs=[pl.BlockSpec(memory_space=pltpu.VMEM)],
+        out_specs=pl.BlockSpec(memory_space=pltpu.VMEM),
+        scratch_shapes=[
+            pltpu.VMEM((n,) + x.shape, x.dtype),
+            pltpu.SemaphoreType.DMA((n,)),
+            pltpu.SemaphoreType.DMA((n,)),
+        ],
+        compiler_params=pltpu.CompilerParams(collective_id=cid, has_side_effects=True),
+    )(x)
+
+
+def scatter_kernel(n, x_ref, out_ref, held, send_sem, recv_sem):
+    me = lax.axis_index("tp")
+    row = lax.axis_index("grp")
+    width = out_ref.shape[1]
+
+    barrier = pltpu.get_barrier_semaphore()
+    for k in range(1, n):
+        peer = lax.rem(me + k, n)
+        pl.semaphore_signal(barrier, inc=1, device_id=(row, peer), device_id_type=MESH)
+    pl.semaphore_wait(barrier, n - 1)
+
+    copies = []
+    for k in range(1, n):
+        peer = lax.rem(me + k, n)
+        cols = pl.ds(pl.multiple_of(peer * width, width), width)
+        copy = pltpu.make_async_remote_copy(
+            src_ref=x_ref.at[:, cols],
+            dst_ref=held.at[k],
+            send_sem=send_sem.at[k],
+            recv_sem=recv_sem.at[k],
+            device_id=(row, peer),
+            device_id_type=MESH,
+        )
+        copy.start()
+        copies.append(copy)
+    own = pl.ds(pl.multiple_of(me * width, width), width)
+    total = x_ref[:, own]
+    for copy in copies:
+        copy.wait_send()
+        copy.wait_recv()
+    for k in range(1, n):
+        total = total + held[k]
+    out_ref[...] = total.astype(out_ref.dtype)
+
+
+def scatter_tp(x, n, cid):
+    rows, cols = x.shape
+    width = cols // n
+    return pl.pallas_call(
+        functools.partial(scatter_kernel, n),
+        out_shape=jax.ShapeDtypeStruct((rows, width), jnp.bfloat16),
+        in_specs=[pl.BlockSpec(memory_space=pltpu.VMEM)],
+        out_specs=pl.BlockSpec(memory_space=pltpu.VMEM),
+        scratch_shapes=[
+            pltpu.VMEM((n, rows, width), jnp.float32),
+            pltpu.SemaphoreType.DMA((n,)),
+            pltpu.SemaphoreType.DMA((n,)),
+        ],
+        compiler_params=pltpu.CompilerParams(collective_id=cid, has_side_effects=True),
+    )(x)
+
+
 def per_device(queries, new_kv, home_cache, help_cache, lengths, split_at, helper_req, out_weight):
-    row_count = queries.shape[0]
-    total_rows = row_count * lax.axis_size("grp")
-    row_ids = jnp.arange(total_rows)
-    help_sel = helper_req[:, None] == row_ids[None, :]
-    everyone, all_lengths, all_splits = (
-        lax.all_gather(queries, "grp", axis=0, tiled=True),
-        lax.all_gather(lengths, "grp", axis=0, tiled=True),
-        lax.all_gather(split_at, "grp", axis=0, tiled=True),
-    )
-    help_queries = jnp.dot(
-        help_sel.astype(jnp.bfloat16), everyone, preferred_element_type=jnp.float32
-    ).astype(jnp.bfloat16)
-    help_count = jnp.sum(jnp.where(help_sel, (all_lengths - all_splits)[None, :], 0), axis=1)
+    n_grp = lax.axis_size("grp")
+    n_tp = lax.axis_size("tp")
+    row_count, width = queries.shape
+    slots = help_cache.shape[0]
+    heads = width // 64
+    head_width = 64
+
+    is_long = lengths > LONG_AT
+    order = jnp.argsort(jnp.where(is_long, 0, 1), stable=True)[:slots]
+    long_count = (lengths - split_at)[order]
+    hi = (long_count // 32).astype(jnp.bfloat16)
+    lo = (long_count % 32).astype(jnp.bfloat16)
+    pad = 128
+    extra = jnp.zeros((slots, pad), jnp.bfloat16).at[:, 0].set(hi).at[:, 1].set(lo)
+    sent = jnp.concatenate([queries[order], extra], axis=1)
+
+    partner = helper_req[0] // row_count
+    got = gather_grp(sent, n_grp, 0)
+    mine = lax.dynamic_index_in_dim(got, partner, axis=0, keepdims=False)
+    help_queries = mine[:, :width]
+    help_count = (
+        mine[:, width].astype(jnp.int32) * 32 + mine[:, width + 1].astype(jnp.int32)
+    )
+
     home_m, home_l, home_u = attend(queries, home_cache, split_at, new_kv)
     help_m, help_l, help_u = attend(help_queries, help_cache, help_count, None)
-    row_start = lax.axis_index("grp") * row_count
-    all_m, all_l, all_u, all_req = (
-        lax.all_gather(help_m, "grp", axis=0, tiled=True),
-        lax.all_gather(help_l, "grp", axis=0, tiled=True),
-        lax.all_gather(help_u, "grp", axis=0, tiled=True),
-        lax.all_gather(helper_req, "grp", axis=0, tiled=True),
-    )
-    own_ids = row_start + jnp.arange(row_count)
-    own_sel = own_ids[:, None] == all_req[None, :]
-    far_m = jnp.max(jnp.where(own_sel[:, :, None], all_m[None], -1e30), axis=1)
-    far_l = jnp.sum(jnp.where(own_sel[:, :, None], all_l[None], 0.0), axis=1)
-    far_u = jnp.sum(jnp.where(own_sel[:, :, None, None], all_u[None], 0.0), axis=1)
+
+    back = jnp.concatenate(
+        [
+            help_u.reshape(slots, heads * head_width),
+            help_m,
+            help_l,
+            jnp.zeros((slots, pad - 2 * heads), jnp.float32),
+        ],
+        axis=1,
+    )
+    got_back = gather_grp(back, n_grp, 1)
+    theirs = lax.dynamic_index_in_dim(got_back, partner, axis=0, keepdims=False)
+    t_u = theirs[:, : heads * head_width].reshape(slots, heads, head_width)
+    t_m = theirs[:, heads * head_width : heads * head_width + heads]
+    t_l = theirs[:, heads * head_width + heads : heads * head_width + 2 * heads]
+
+    own_sel = (jnp.arange(row_count)[:, None] == order[None, :]) & is_long[order][None, :]
+    far_m = jnp.max(jnp.where(own_sel[:, :, None], t_m[None], -1e30), axis=1)
+    far_l = jnp.sum(jnp.where(own_sel[:, :, None], t_l[None], 0.0), axis=1)
+    far_u = jnp.sum(jnp.where(own_sel[:, :, None, None], t_u[None], 0.0), axis=1)
     top_score = jnp.maximum(home_m, far_m)
     home_e = jnp.exp(home_m - top_score)
     far_e = jnp.exp(far_m - top_score)
@@ -82,7 +227,7 @@
     heads_out = numerator / denominator[..., None]
     mix = heads_out.reshape(row_count, -1).astype(jnp.bfloat16)
     partial_out = jnp.dot(mix, out_weight, preferred_element_type=jnp.float32)
-    return lax.psum_scatter(partial_out, "tp", scatter_dimension=1, tiled=True).astype(jnp.bfloat16)
+    return scatter_tp(partial_out, n_tp, 2)
 
 
 def solution(mesh):

time: 293 us -> 87.3 us (0.30)
  blocking collectives: 168 us -> 0 us
  waiting for transfers between devices: 84 us -> 0 us
  Pallas kernels: 0 us -> 57 us
  between operations: 14.8 us -> 2.85 us
    all_gather x4 -> x0, blocking collectives: 151 us -> none  [the longest x1 45.1 us: per_device(): lax.all_gather(queries, 'grp', axis=0, tiled=True)]
    reduce_scatter x1 -> x0, waiting for transfers between devices: 84 us -> none  [per_device(): lax.psum_scatter(partial_out, 'tp', scatter_dimension=1, tiled=True)]
    pallas_call x0 -> x3, Pallas kernels: none -> 57 us  [the longest x2 44 us: gather_grp(): pl.pallas_call(functools.partial(gather_kernel, n), out_shape=jax.ShapeDt...]
    unnamed x1 -> x0, blocking collectives: 17.1 us -> none
    another operation x6 -> x7, local copies, waits for them, and re-layouts: 7.24 us -> 6.57 us
  transfers between devices with their start and end apart: 1 -> 0, of which waited for: 1 -> 0; matrix products, arithmetic and copies ran while one was open for 0% -> 0% of each run, Pallas kernels for 0% -> 0%
where the time goes in v1:
time: 87.3 us; the launch traced here: 86.7 us
  Pallas kernels  57 us (65%)
  local copies, waits for them, and re-layouts  17.2 us (20%)
  other arithmetic  6.64 us (8%)
  matrix products  2.94 us (3%)
  between operations  2.85 us (3%)
    pallas_call x2, Pallas kernels, gather_grp(): pl.pallas_call(functools.partial(gather_kernel, n), out_shape=jax.ShapeDt...  44 us
    pallas_call x1, Pallas kernels, scatter_tp(): pl.pallas_call(functools.partial(scatter_kernel, n), out_shape=jax.ShapeD...  13 us
    another operation x6, local copies, waits for them, and re-layouts  6.48 us
    slice x1, local copies, waits for them, and re-layouts, attend(): key_rows = cache[:, 0].reshape(row_count, kv_heads, context, head_width)  3.1 us
    another operation x3, other arithmetic  2.7 us

profile of v1, /device:TPU:1, one launch (start us, length us, event | category | flops | bytes accessed | tf_op | source)
XLA Modules:
  0.0 86.7 jit_solution(4371803562402553395)
XLA Ops:
  2.7 0.7 broadcast_select_fusion.1
  3.4 1.0 %sort.17 = (s32[8]{0:T(128)}, s32[8]{0:T(128)S(1)}) sort(s32[8]{0:T(128)S(1)} %get-tuple-element.50, s32[8]{0:T(128)S(1)} %iota.37), dimensions={0}, to_apply=%region_1.2 | sort | flops 24 | bytes 128 | tf_op jit(solution)/shard_map/jit(argsort)/sort | solution.py:184
  4.4 0.6 gather_fusion.2
  5.1 0.6 compare_reduce_fusion
  5.7 0.7 compare_reduce_fusion.1
  6.5 1.3 %fusion.13 = (bf16[4,1]{1,0:T(4,128)(2,1)S(1)}, bf16[4,1]{1,0:T(4,128)(2,1)S(1)}) fusion(pred[]{:T(512)} %compare_reduce_fusion, s32[4,1]{1,0:T(4,128)S(1)} %copy.50, pred[]{:T(512)} %compare_reduce_fusion.1), kind=kLoop, calls=%fused_computation.56 | loop fusion | flops 92 | bytes 34 | tf_op jit(solution)/shard_map/select.44
  7.8 0.1 scatter.9
  7.9 1.3 %gather_fusion.1 = bf16[4,256]{1,0:T(4,128)(2,1)S(1)} fusion(bf16[8,256]{1,0:T(8,128)(2,1)} %param.12, s32[1024]{0:T(1024)S(1)} %pad_clamp_fusion), kind=kCustom, calls=%fused_computation.1 | custom fusion | bytes 4112 | tf_op jit(solution)/shard_map/gather | solution.py:190
  9.2 0.6 pad_maximum_fusion.x_ref
  9.8 24.9 %shard_map.82 = bf16[64,4,384]{2,1,0:T(4,128)(2,1)} custom-call(bf16[4,384]{1,0:T(4,128)(2,1)} %pad_maximum_fusion.x_ref), custom_call_target="tpu_custom_call" | custom-call | tf_op jit(solution)/shard_map/pallas_call | solution.py:109
  34.7 0.7 dynamic-slice_bitcast_fusion.1
  35.5 0.2 add_reduce_fusion
  35.7 1.3 %fusion.18 = (bf16[4,1,1,512,128]{4,3,2,1,0:T(8,128)(2,1)S(1)}, bf16[4,1,1,512,128]{4,3,2,1,0:T(8,128)(2,1)S(1)}) fusion(bf16[4,2,1,512,128]{4,3,2,1,0:T(8,128)(2,1)} %param.15), kind=kLoop, calls=%fused_computation.64 | loop fusion | bytes 2097152 | tf_op jit(solution)/shard_map/slice | solution.py:23
  37.0 0.4 reshape.337
  37.4 0.5 select_reduce_fusion.2
  37.9 0.4 reshape.338
  38.3 0.3 fusion.14
  38.7 0.2 convert_reduce_fusion.1
  39.0 0.7 maximum_maximum_fusion.x_ref
  39.6 19.2 %shard_map.83 = f32[64,4,384]{2,1,0:T(4,128)} custom-call(f32[4,384]{1,0:T(4,128)} %maximum_maximum_fusion.x_ref), custom_call_target="tpu_custom_call" | custom-call | tf_op jit(solution)/shard_map/pallas_call | solution.py:109
  58.8 0.7 dynamic-slice_bitcast_fusion
  59.6 0.6 gather_fusion
  60.6 3.1 %fusion.17 = (bf16[8,1,1,512,128]{4,3,2,1,0:T(8,128)(2,1)}, bf16[8,1,1,512,128]{4,3,2,1,0:T(8,128)(2,1)}) fusion(bf16[8,2,1,512,128]{4,3,2,1,0:T(8,128)(2,1)} %param.14), kind=kLoop, calls=%fused_computation.63 | loop fusion | bytes 4194304 | tf_op jit(solution)/shard_map/slice | solution.py:22
  63.7 2.8 %reshape.333 = bf16[8,1024,64]{2,1,0:T(8,128)(2,1)S(1)} reshape(bf16[8,1,1,512,128]{4,3,2,1,0:T(8,128)(2,1)} %get-tuple-element.38) | data formatting | bytes 2097152 | tf_op jit(solution)/shard_map/reshape.48
  66.6 0.7 select_reduce_fusion
  67.4 0.1 fusion.6
  67.5 0.2 convert_reduce_fusion
  68.3 2.7 %reshape.335 = bf16[8,1024,64]{2,1,0:T(8,128)(2,1)S(1)} reshape(bf16[8,1,1,512,128]{4,3,2,1,0:T(8,128)(2,1)} %get-tuple-element.39) | data formatting | bytes 2097152 | tf_op jit(solution)/shard_map/reshape.56
  71.0 0.4 fusion.3
  71.5 0.9 %fusion.21.x_ref = f32[8,2048]{1,0:T(8,128)} fusion(bf16[8,256]{1,0:T(8,128)(2,1)S(1)} %convert_element_type.80, bf16[256,2048]{1,0:T(8,128)(2,1)S(1)} %copy-done), kind=kOutput, calls=%fused_computation.67 | convolution fusion | flops 8388608 | bytes 1118208 | tf_op jit(solution)/shard_map/dot_general | solution.py:229
  72.4 13.0 %shard_map.84 = bf16[8,256]{1,0:T(8,128)(2,1)} custom-call(f32[8,2048]{1,0:T(8,128)} %fusion.21.x_ref), custom_call_target="tpu_custom_call" | custom-call | tf_op jit(solution)/shard_map/pallas_call | solution.py:161
  85.4 1.3 %copy.78 = bf16[8,256]{1,0:T(8,128)(2,1)} copy(bf16[8,256]{1,0:T(8,128)(2,1)} %shard_map.84) | data formatting | bytes 8192
  (43 shorter events, 1.7 us)
Async XLA Ops:
  0.0 71.5 %copy-start = (bf16[256,2048]{1,0:T(8,128)(2,1)S(1)}, bf16[256,2048]{1,0:T(8,128)(2,1)}, u32[]{:S(2)}) copy-start(bf16[256,2048]{1,0:T(8,128)(2,1)} %param.19) | copy-start | bytes 3145732
  37.4 22.2 %copy-start.4 = (s32[8]{0:T(128)S(1)}, s32[8]{0:T(128)}, u32[]{:S(2)}) copy-start(s32[8]{0:T(128)} %param.16) | copy-start | bytes 100
  37.9 22.7 %copy-start.3 = (s32[8]{0:T(128)S(1)}, s32[8]{0:T(128)}, u32[]{:S(2)}) copy-start(s32[8]{0:T(128)} %param.17) | copy-start | bytes 100
  63.7 2.8 %copy-start.1 = (bf16[8,256]{1,0:T(8,128)(2,1)S(1)}, bf16[8,256]{1,0:T(8,128)(2,1)}, u32[]{:S(2)}) copy-start(bf16[8,256]{1,0:T(8,128)(2,1)} %param.12) | copy-start | bytes 12292
  63.7 3.6 %copy-start.2 = (bf16[8,2,64]{2,1,0:T(2,128)(2,1)S(1)}, bf16[8,2,64]{2,1,0:T(2,128)(2,1)}, u32[]{:S(2)}) copy-start(bf16[8,2,64]{2,1,0:T(2,128)(2,1)} %param.13) | copy-start | bytes 6148

commit v2 on v1

--- a/solution.py
+++ b/solution.py
@@ -53,71 +53,93 @@
     )
 
 
-def gather_kernel(n, x_ref, out_ref, held, send_sem, recv_sem):
+def gather_kernel(ny, nz, x_ref, out_ref, held, copy_sem, send1, recv1, send2, recv2):
     me = lax.axis_index("grp")
     col = lax.axis_index("tp")
+    my_y = me // nz
+    my_z = me % nz
 
     barrier = pltpu.get_barrier_semaphore()
-
-    def greet(k, carry):
-        peer = lax.rem(me + k, n)
+    for k in range(1, nz):
+        peer = my_y * nz + lax.rem(my_z + k, nz)
         pl.semaphore_signal(barrier, inc=1, device_id=(peer, col), device_id_type=MESH)
-        return carry
-
-    lax.fori_loop(1, n, greet, 0)
-    pl.semaphore_wait(barrier, n - 1)
-
-    def copy_to(k):
-        peer = lax.rem(me + k, n)
-        return pltpu.make_async_remote_copy(
+    for k in range(1, ny):
+        peer = lax.rem(my_y + k, ny) * nz + my_z
+        pl.semaphore_signal(barrier, inc=1, device_id=(peer, col), device_id_type=MESH)
+    pl.semaphore_wait(barrier, (nz - 1) + (ny - 1))
+
+    local = pltpu.make_async_copy(x_ref, held.at[my_y, my_z], copy_sem)
+    local.start()
+    first = []
+    for k in range(1, nz):
+        peer_z = lax.rem(my_z + k, nz)
+        copy = pltpu.make_async_remote_copy(
             src_ref=x_ref,
-            dst_ref=held.at[me],
-            send_sem=send_sem.at[k],
-            recv_sem=recv_sem.at[k],
-            device_id=(peer, col),
-            device_id_type=MESH,
-        )
-
-    def copy_from(k):
-        source = lax.rem(me + n - k, n)
-        return pltpu.make_async_remote_copy(
+            dst_ref=held.at[my_y, my_z],
+            send_sem=send1.at[k],
+            recv_sem=recv1.at[k],
+            device_id=(my_y * nz + peer_z, col),
+            device_id_type=MESH,
+        )
+        copy.start()
+        first.append(copy)
+    for k in range(1, nz):
+        first[k - 1].wait_send()
+        src_z = lax.rem(my_z + nz - k, nz)
+        pltpu.make_async_remote_copy(
             src_ref=x_ref,
-            dst_ref=held.at[source],
-            send_sem=send_sem.at[k],
-            recv_sem=recv_sem.at[k],
-            device_id=(source, col),
-            device_id_type=MESH,
-        )
-
-    def start(k, carry):
-        copy_to(k).start()
-        return carry
-
-    lax.fori_loop(1, n, start, 0)
-
-    def finish(k, carry):
-        copy_to(k).wait_send()
-        copy_from(k).wait_recv()
-        return carry
-
-    lax.fori_loop(1, n, finish, 0)
-    held[me] = x_ref[...]
+            dst_ref=held.at[my_y, src_z],
+            send_sem=send1.at[k],
+            recv_sem=recv1.at[k],
+            device_id=(my_y * nz + src_z, col),
+            device_id_type=MESH,
+        ).wait_recv()
+    local.wait()
+
+    second = []
+    for k in range(1, ny):
+        peer_y = lax.rem(my_y + k, ny)
+        copy = pltpu.make_async_remote_copy(
+            src_ref=held.at[my_y],
+            dst_ref=held.at[my_y],
+            send_sem=send2.at[k],
+            recv_sem=recv2.at[k],
+            device_id=(peer_y * nz + my_z, col),
+            device_id_type=MESH,
+        )
+        copy.start()
+        second.append(copy)
+    for k in range(1, ny):
+        second[k - 1].wait_send()
+        src_y = lax.rem(my_y + ny - k, ny)
+        pltpu.make_async_remote_copy(
+            src_ref=held.at[src_y],
+            dst_ref=held.at[src_y],
+            send_sem=send2.at[k],
+            recv_sem=recv2.at[k],
+            device_id=(src_y * nz + my_z, col),
+            device_id_type=MESH,
+        ).wait_recv()
     out_ref[...] = held[...]
 
 
-def gather_grp(x, n, cid):
-    return pl.pallas_call(
-        functools.partial(gather_kernel, n),
-        out_shape=jax.ShapeDtypeStruct((n,) + x.shape, x.dtype),
+def gather_grp(x, ny, nz, cid):
+    out = pl.pallas_call(
+        functools.partial(gather_kernel, ny, nz),
+        out_shape=jax.ShapeDtypeStruct((ny, nz) + x.shape, x.dtype),
         in_specs=[pl.BlockSpec(memory_space=pltpu.VMEM)],
         out_specs=pl.BlockSpec(memory_space=pltpu.VMEM),
         scratch_shapes=[
-            pltpu.VMEM((n,) + x.shape, x.dtype),
-            pltpu.SemaphoreType.DMA((n,)),
-            pltpu.SemaphoreType.DMA((n,)),
+            pltpu.VMEM((ny, nz) + x.shape, x.dtype),
+            pltpu.SemaphoreType.DMA(()),
+            pltpu.SemaphoreType.DMA((nz,)),
+            pltpu.SemaphoreType.DMA((nz,)),
+            pltpu.SemaphoreType.DMA((ny,)),
+            pltpu.SemaphoreType.DMA((ny,)),
         ],
         compiler_params=pltpu.CompilerParams(collective_id=cid, has_side_effects=True),
     )(x)
+    return out.reshape((ny * nz,) + x.shape)
 
 
 def scatter_kernel(n, x_ref, out_ref, held, send_sem, recv_sem):
@@ -172,7 +194,7 @@
     )(x)
 
 
-def per_device(queries, new_kv, home_cache, help_cache, lengths, split_at, helper_req, out_weight):
+def per_device(ny, nz, queries, new_kv, home_cache, help_cache, lengths, split_at, helper_req, out_weight):
     n_grp = lax.axis_size("grp")
     n_tp = lax.axis_size("tp")
     row_count, width = queries.shape
@@ -190,7 +212,7 @@
     sent = jnp.concatenate([queries[order], extra], axis=1)
 
     partner = helper_req[0] // row_count
-    got = gather_grp(sent, n_grp, 0)
+    got = gather_grp(sent, ny, nz, 0)
     mine = lax.dynamic_index_in_dim(got, partner, axis=0, keepdims=False)
     help_queries = mine[:, :width]
     help_count = (
@@ -209,7 +231,7 @@
         ],
         axis=1,
     )
-    got_back = gather_grp(back, n_grp, 1)
+    got_back = gather_grp(back, ny, nz, 1)
     theirs = lax.dynamic_index_in_dim(got_back, partner, axis=0, keepdims=False)
     t_u = theirs[:, : heads * head_width].reshape(slots, heads, head_width)
     t_m = theirs[:, heads * head_width : heads * head_width + heads]
@@ -230,9 +252,25 @@
     return scatter_tp(partial_out, n_tp, 2)
 
 
+def grp_rows(mesh):
+    column = list(mesh.devices[:, 0])
+    n = len(column)
+    coords = [getattr(d, "coords", None) for d in column]
+    if coords[0] is not None:
+        nz = 1
+        while nz < n and coords[nz][1] == coords[0][1]:
+            nz += 1
+    else:
+        nz = 1
+        while nz * nz < n:
+            nz *= 2
+    return n // nz, nz
+
+
 def solution(mesh):
+    ny, nz = grp_rows(mesh)
     return jax.shard_map(
-        per_device,
+        functools.partial(per_device, ny, nz),
         mesh=mesh,
         in_specs=(
             P("grp", "tp"),

time: 87.3 us -> 85.6 us (0.981)
  Pallas kernels: 57 us -> 55.3 us
    pallas_call x1, Pallas kernels: 13 us -> 10.7 us  [scatter_tp(): pl.pallas_call(functools.partial(scatter_kernel, n), out_shape=jax.ShapeD...]
where the time goes in v2:
time: 85.6 us; the launch traced here: 84.9 us
  Pallas kernels  55.3 us (65%)
  local copies, waits for them, and re-layouts  17.2 us (20%)
  other arithmetic  6.64 us (8%)
  matrix products  2.94 us (3%)
  between operations  2.85 us (3%)
    pallas_call x2, Pallas kernels, gather_grp(): pl.pallas_call(functools.partial(gather_kernel, ny, nz), out_shape=jax.Sh...  44.5 us
    pallas_call x1, Pallas kernels, scatter_tp(): pl.pallas_call(functools.partial(scatter_kernel, n), out_shape=jax.ShapeD...  10.7 us
    another operation x6, local copies, waits for them, and re-layouts  6.48 us
    slice x1, local copies, waits for them, and re-layouts, attend(): key_rows = cache[:, 0].reshape(row_count, kv_heads, context, head_width)  3.1 us
    another operation x3, other arithmetic  2.7 us

profile of v2, /device:TPU:1, one launch (start us, length us, event | category | flops | bytes accessed | tf_op | source)
XLA Modules:
  0.0 84.9 jit_solution(5385119892987169181)
XLA Ops:
  2.7 0.7 broadcast_select_fusion.1
  3.4 1.0 %sort.17 = (s32[8]{0:T(128)}, s32[8]{0:T(128)S(1)}) sort(s32[8]{0:T(128)S(1)} %get-tuple-element.50, s32[8]{0:T(128)S(1)} %iota.37), dimensions={0}, to_apply=%region_1.2 | sort | flops 24 | bytes 128 | tf_op jit(solution)/shard_map/jit(argsort)/sort | solution.py:206
  4.4 0.6 gather_fusion.2
  5.1 0.6 compare_reduce_fusion
  5.7 0.7 compare_reduce_fusion.1
  6.5 1.3 %fusion.13 = (bf16[4,1]{1,0:T(4,128)(2,1)S(1)}, bf16[4,1]{1,0:T(4,128)(2,1)S(1)}) fusion(pred[]{:T(512)} %compare_reduce_fusion, s32[4,1]{1,0:T(4,128)S(1)} %copy.50, pred[]{:T(512)} %compare_reduce_fusion.1), kind=kLoop, calls=%fused_computation.56 | loop fusion | flops 92 | bytes 34 | tf_op jit(solution)/shard_map/select.44
  7.8 0.1 scatter.9
  7.9 1.3 %gather_fusion.1 = bf16[4,256]{1,0:T(4,128)(2,1)S(1)} fusion(bf16[8,256]{1,0:T(8,128)(2,1)} %param.12, s32[1024]{0:T(1024)S(1)} %pad_clamp_fusion), kind=kCustom, calls=%fused_computation.1 | custom fusion | bytes 4112 | tf_op jit(solution)/shard_map/gather | solution.py:212
  9.2 0.6 pad_maximum_fusion.x_ref
  9.8 25.5 %shard_map.82 = bf16[8,8,4,384]{3,2,1,0:T(4,128)(2,1)} custom-call(bf16[4,384]{1,0:T(4,128)(2,1)} %pad_maximum_fusion.x_ref), custom_call_target="tpu_custom_call" | custom-call | tf_op jit(solution)/shard_map/pallas_call | solution.py:127
  35.3 0.7 dynamic-slice_bitcast_fusion.1
  36.0 0.2 add_reduce_fusion
  36.3 1.3 %fusion.18 = (bf16[4,1,1,512,128]{4,3,2,1,0:T(8,128)(2,1)S(1)}, bf16[4,1,1,512,128]{4,3,2,1,0:T(8,128)(2,1)S(1)}) fusion(bf16[4,2,1,512,128]{4,3,2,1,0:T(8,128)(2,1)} %param.15), kind=kLoop, calls=%fused_computation.64 | loop fusion | bytes 2097152 | tf_op jit(solution)/shard_map/slice | solution.py:23
  37.6 0.4 reshape.344
  38.0 0.5 select_reduce_fusion.2
  38.5 0.4 reshape.345
  38.9 0.3 fusion.14
  39.3 0.2 convert_reduce_fusion.1
  39.6 0.7 maximum_maximum_fusion.x_ref
  40.2 19.1 %shard_map.83 = f32[8,8,4,384]{3,2,1,0:T(4,128)} custom-call(f32[4,384]{1,0:T(4,128)} %maximum_maximum_fusion.x_ref), custom_call_target="tpu_custom_call" | custom-call | tf_op jit(solution)/shard_map/pallas_call | solution.py:127
  59.3 0.7 dynamic-slice_bitcast_fusion
  60.1 0.6 gather_fusion
  61.1 3.1 %fusion.17 = (bf16[8,1,1,512,128]{4,3,2,1,0:T(8,128)(2,1)}, bf16[8,1,1,512,128]{4,3,2,1,0:T(8,128)(2,1)}) fusion(bf16[8,2,1,512,128]{4,3,2,1,0:T(8,128)(2,1)} %param.14), kind=kLoop, calls=%fused_computation.63 | loop fusion | bytes 4194304 | tf_op jit(solution)/shard_map/slice | solution.py:22
  64.2 2.8 %reshape.339 = bf16[8,1024,64]{2,1,0:T(8,128)(2,1)S(1)} reshape(bf16[8,1,1,512,128]{4,3,2,1,0:T(8,128)(2,1)} %get-tuple-element.38) | data formatting | bytes 2097152 | tf_op jit(solution)/shard_map/reshape.50
  67.1 0.7 select_reduce_fusion
  67.9 0.1 fusion.6
  68.0 0.2 convert_reduce_fusion
  68.8 2.7 %reshape.341 = bf16[8,1024,64]{2,1,0:T(8,128)(2,1)S(1)} reshape(bf16[8,1,1,512,128]{4,3,2,1,0:T(8,128)(2,1)} %get-tuple-element.39) | data formatting | bytes 2097152 | tf_op jit(solution)/shard_map/reshape.58
  71.5 0.4 fusion.3
  72.0 0.9 %fusion.21.x_ref = f32[8,2048]{1,0:T(8,128)} fusion(bf16[8,256]{1,0:T(8,128)(2,1)S(1)} %convert_element_type.80, bf16[256,2048]{1,0:T(8,128)(2,1)S(1)} %copy-done), kind=kOutput, calls=%fused_computation.67 | convolution fusion | flops 8388608 | bytes 1118208 | tf_op jit(solution)/shard_map/dot_general | solution.py:251
  72.9 10.7 %shard_map.84 = bf16[8,256]{1,0:T(8,128)(2,1)} custom-call(f32[8,2048]{1,0:T(8,128)} %fusion.21.x_ref), custom_call_target="tpu_custom_call" | custom-call | tf_op jit(solution)/shard_map/pallas_call | solution.py:183
  83.6 1.3 %copy.78 = bf16[8,256]{1,0:T(8,128)(2,1)} copy(bf16[8,256]{1,0:T(8,128)(2,1)} %shard_map.84) | data formatting | bytes 8192
  (43 shorter events, 1.7 us)
Async XLA Ops:
  0.0 72.0 %copy-start = (bf16[256,2048]{1,0:T(8,128)(2,1)S(1)}, bf16[256,2048]{1,0:T(8,128)(2,1)}, u32[]{:S(2)}) copy-start(bf16[256,2048]{1,0:T(8,128)(2,1)} %param.19) | copy-start | bytes 3145732
  38.0 22.1 %copy-start.4 = (s32[8]{0:T(128)S(1)}, s32[8]{0:T(128)}, u32[]{:S(2)}) copy-start(s32[8]{0:T(128)} %param.16) | copy-start | bytes 100
  38.5 22.6 %copy-start.3 = (s32[8]{0:T(128)S(1)}, s32[8]{0:T(128)}, u32[]{:S(2)}) copy-start(s32[8]{0:T(128)} %param.17) | copy-start | bytes 100
  64.2 2.8 %copy-start.1 = (bf16[8,256]{1,0:T(8,128)(2,1)S(1)}, bf16[8,256]{1,0:T(8,128)(2,1)}, u32[]{:S(2)}) copy-start(bf16[8,256]{1,0:T(8,128)(2,1)} %param.12) | copy-start | bytes 12292
  64.2 3.6 %copy-start.2 = (bf16[8,2,64]{2,1,0:T(2,128)(2,1)S(1)}, bf16[8,2,64]{2,1,0:T(2,128)(2,1)}, u32[]{:S(2)}) copy-start(bf16[8,2,64]{2,1,0:T(2,128)(2,1)} %param.13) | copy-start | bytes 6148

commit v3 on v2

--- a/solution.py
+++ b/solution.py
@@ -15,18 +15,27 @@
     row_count = queries.shape[0]
     kv_heads = cache.shape[2]
     head_width = cache.shape[4] // 2
-    context = cache.shape[3] * 2
+    half = cache.shape[3]
     group_size = queries.shape[1] // (kv_heads * head_width)
     score_scale = head_width ** (-0.5)
     head_rows = queries.reshape(row_count, kv_heads, group_size, head_width)
-    key_rows = cache[:, 0].reshape(row_count, kv_heads, context, head_width)
-    value_rows = cache[:, 1].reshape(row_count, kv_heads, context, head_width)
+    blank = jnp.zeros_like(head_rows)
+    wide_rows = jnp.stack(
+        [
+            jnp.concatenate([head_rows, blank], axis=-1),
+            jnp.concatenate([blank, head_rows], axis=-1),
+        ],
+        axis=3,
+    )
+    key_rows = cache[:, 0]
+    value_rows = cache[:, 1]
     scores = (
-        jnp.einsum("nkgd,nkpd->nkgp", head_rows, key_rows, preferred_element_type=jnp.float32)
+        jnp.einsum("nkgjc,nkpc->nkgjp", wide_rows, key_rows, preferred_element_type=jnp.float32)
         * score_scale
     )
-    inside = (jnp.arange(context)[None, :] < count[:, None])[:, None, None, :]
-    top_score = jnp.max(jnp.where(inside, scores, -1e30), axis=-1)
+    position = 2 * jnp.arange(half)[None, :] + jnp.arange(2)[:, None]
+    inside = (position[None] < count[:, None, None])[:, None, None]
+    top_score = jnp.max(jnp.where(inside, scores, -1e30), axis=(-2, -1))
     if fresh is not None:
         fresh_key = fresh[:, 0].reshape(row_count, kv_heads, head_width)
         fresh_score = (
@@ -34,11 +43,14 @@
             * score_scale
         )
         top_score = jnp.maximum(top_score, fresh_score)
-    weights = jnp.where(inside, jnp.exp(scores - top_score[..., None]), 0.0).astype(jnp.bfloat16)
-    weight_sum = jnp.sum(weights.astype(jnp.float32), axis=-1)
-    mixed_sum = jnp.einsum(
-        "nkgp,nkpd->nkgd", weights, value_rows, preferred_element_type=jnp.float32
-    )
+    weights = jnp.where(
+        inside, jnp.exp(scores - top_score[..., None, None]), 0.0
+    ).astype(jnp.bfloat16)
+    weight_sum = jnp.sum(weights.astype(jnp.float32), axis=(-2, -1))
+    both = jnp.einsum(
+        "nkgjp,nkpc->nkgjc", weights, value_rows, preferred_element_type=jnp.float32
+    )
+    mixed_sum = both[..., 0, :head_width] + both[..., 1, head_width:]
     if fresh is not None:
         fresh_weight = lax.optimization_barrier(
             jnp.exp(fresh_score - top_score).astype(jnp.bfloat16)

time: 85.6 us -> 77.6 us (0.907)
  local copies, waits for them, and re-layouts: 17.2 us -> 7.38 us
  matrix products: 2.94 us -> 4.51 us
    another operation x7 -> x3, local copies, waits for them, and re-layouts: 6.57 us -> 0.25 us  [the longest x2 0.16 us: attend(): jnp.stack([jnp.concatenate([head_rows, blank], axis=-1), jnp.concatenate(...]
    slice x2 -> x0, local copies, waits for them, and re-layouts: 4.37 us -> none  [the longest x1 3.1 us: attend(): key_rows = cache[:, 0].reshape(row_count, kv_heads, context, head_width)]
    dot_general x4, matrix products: 1.94 us -> 3.5 us  [the longest x2 1.86 us: attend(): jnp.einsum('nkgjc,nkpc->nkgjp', wide_rows, key_rows, preferred_element_ty...]
    pallas_call x1, Pallas kernels: 10.7 us -> 12.1 us  [scatter_tp(): pl.pallas_call(functools.partial(scatter_kernel, n), out_shape=jax.ShapeD...]
    pallas_call x2, Pallas kernels: 44.5 us -> 43.1 us  [gather_grp(): pl.pallas_call(functools.partial(gather_kernel, ny, nz), out_shape=jax.Sh...]
where the time goes in v3:
time: 77.6 us; the launch traced here: 77.1 us
  Pallas kernels  55.3 us (71%)
  local copies, waits for them, and re-layouts  7.38 us (10%)
  other arithmetic  6.96 us (9%)
  matrix products  4.51 us (6%)
  between operations  2.95 us (4%)
    pallas_call x2, Pallas kernels, gather_grp(): pl.pallas_call(functools.partial(gather_kernel, ny, nz), out_shape=jax.Sh...  43.1 us
    pallas_call x1, Pallas kernels, scatter_tp(): pl.pallas_call(functools.partial(scatter_kernel, n), out_shape=jax.ShapeD...  12.1 us
    another operation x3, other arithmetic  2.7 us
    dot_general x2, matrix products, attend(): jnp.einsum('nkgjc,nkpc->nkgjp', wide_rows, key_rows, preferred_element_ty...  1.86 us
    dot_general x2, matrix products, attend(): jnp.einsum('nkgjp,nkpc->nkgjc', weights, value_rows, preferred_element_ty...  1.64 us

profile of v3, /device:TPU:1, one launch (start us, length us, event | category | flops | bytes accessed | tf_op | source)
XLA Modules:
  0.0 77.1 jit_solution(9373416647026231883)
XLA Ops:
  2.9 0.7 broadcast_select_fusion.1
  3.5 1.0 %sort.17 = (s32[8]{0:T(128)}, s32[8]{0:T(128)S(1)}) sort(s32[8]{0:T(128)S(1)} %get-tuple-element.50, s32[8]{0:T(128)S(1)} %iota.42), dimensions={0}, to_apply=%region_1.2 | sort | flops 24 | bytes 128 | tf_op jit(solution)/shard_map/jit(argsort)/sort | solution.py:218
  4.5 0.6 gather_fusion.2
  5.1 0.1 copy.80
  5.2 0.6 compare_reduce_fusion
  5.9 0.7 compare_reduce_fusion.1
  6.6 1.3 %fusion.22 = (bf16[4,1]{1,0:T(4,128)(2,1)S(1)}, bf16[4,1]{1,0:T(4,128)(2,1)S(1)}) fusion(pred[]{:T(512)} %compare_reduce_fusion, s32[4,1]{1,0:T(4,128)S(1)} %copy.80, pred[]{:T(512)} %compare_reduce_fusion.1), kind=kLoop, calls=%fused_computation.78 | loop fusion | flops 92 | bytes 34 | tf_op jit(solution)/shard_map/select.44
  8.0 0.1 scatter.9
  8.1 1.3 %gather_fusion.1 = bf16[4,256]{1,0:T(4,128)(2,1)S(1)} fusion(bf16[8,256]{1,0:T(8,128)(2,1)} %param.12, s32[1024]{0:T(1024)S(1)} %pad_clamp_fusion), kind=kCustom, calls=%fused_computation.1 | custom fusion | bytes 4112 | tf_op jit(solution)/shard_map/gather | solution.py:224
  9.3 0.6 pad_maximum_fusion.x_ref
  9.9 25.5 %shard_map.82 = bf16[8,8,4,384]{3,2,1,0:T(4,128)(2,1)} custom-call(bf16[4,384]{1,0:T(4,128)(2,1)} %pad_maximum_fusion.x_ref), custom_call_target="tpu_custom_call" | custom-call | tf_op jit(solution)/shard_map/pallas_call | solution.py:139
  35.4 0.7 dynamic-slice_bitcast_fusion.1
  36.3 0.2 add_reduce_fusion
  36.6 1.4 %select_reduce_fusion.2 = (f32[4,4]{1,0:T(4,128)S(1)}, f32[4,4,2,512]{3,1,2,0:T(4,128)S(1)}) fusion(pred[4,2,512]{2,1,0:T(4,128)(4,1)S(1)} %broadcast_compare_fusion.1, bf16[4,2,1,512,128]{4,3,2,1,0:T(8,128)(2,1)} %param.15, bf16[4,1,4,1,128]{4,2,3,0,1:T(4,128)(2,1)S(1)} %get-tuple-element.45, bf16[4,1,4,1,128]{4,2,3,0,1:T(4,128)(2,1)S(1)} %get-tuple-element.44), kind=kOutput, calls=%fused_computation.21 | convolution fusion | flops 4259824 | bytes 602176 | tf_op jit(solution)/shard_map/nkgjc,nkpc->nkgjp/dot_general | solution.py:33
  38.0 1.3 %convolution_bitcast_fusion.1 = f32[4,1,4,2,128]{4,2,3,0,1:T(4,128)S(1)} fusion(bf16[4,2,1,512,128]{4,3,2,1,0:T(8,128)(2,1)} %param.15, f32[4,4,2,512]{3,1,2,0:T(4,128)S(1)} %get-tuple-element.53, f32[4,4]{1,0:T(4,128)S(1)} %get-tuple-element.52, pred[4,2,512]{2,1,0:T(4,128)(4,1)S(1)} %broadcast_compare_fusion.1), kind=kOutput, calls=%fused_computation.6 | convolution fusion | flops 4243456 | bytes 610368 | tf_op jit(solution)/shard_map/nkgjp,nkpc->nkgjc/dot_general | solution.py:50
  39.4 0.2 convert_reduce_fusion.1
  39.7 0.7 maximum_maximum_fusion.x_ref
  40.4 17.7 %shard_map.83 = f32[8,8,4,384]{3,2,1,0:T(4,128)} custom-call(f32[4,384]{1,0:T(4,128)} %maximum_maximum_fusion.x_ref), custom_call_target="tpu_custom_call" | custom-call | tf_op jit(solution)/shard_map/pallas_call | solution.py:139
  58.0 0.7 dynamic-slice_bitcast_fusion
  58.8 0.6 gather_fusion
  60.1 0.5 select_reduce_fusion
  60.6 0.1 fusion.15
  60.8 0.2 convert_reduce_fusion
  61.1 0.1 copy.78
  61.8 0.1 div.39
  61.9 0.1 mul.109
  62.0 0.3 convolution_bitcast_fusion
  62.4 0.1 add.125
  62.7 0.1 mul.104
  62.8 0.9 %fusion.14.x_ref = f32[8,2048]{1,0:T(8,128)} fusion(bf16[256,2048]{1,0:T(8,128)(2,1)S(1)} %copy-done, f32[8,256]{1,0:T(8,128)S(1)} %div.39, f32[8,256]{1,0:T(8,128)S(1)} %mul.113, f32[8,256]{1,0:T(8,128)S(1)} %mul.109, f32[8,256]{1,0:T(8,128)S(1)} %add.125, f32[8,256]{1,0:T(8,128)S(1)} %mul.104), kind=kOutput, calls=%fused_computation.45 | convolution fusion | flops 8398848 | bytes 1155072 | tf_op jit(solution)/shard_map/dot_general | solution.py:263
  63.7 12.1 %shard_map.84 = bf16[8,256]{1,0:T(8,128)(2,1)} custom-call(f32[8,2048]{1,0:T(8,128)} %fusion.14.x_ref), custom_call_target="tpu_custom_call" | custom-call | tf_op jit(solution)/shard_map/pallas_call | solution.py:195
  75.8 1.3 %copy.111 = bf16[8,256]{1,0:T(8,128)(2,1)} copy(bf16[8,256]{1,0:T(8,128)(2,1)} %shard_map.84) | data formatting | bytes 8192
  (56 shorter events, 2.3 us)
Async XLA Ops:
  0.0 62.8 %copy-start = (bf16[256,2048]{1,0:T(8,128)(2,1)S(1)}, bf16[256,2048]{1,0:T(8,128)(2,1)}, u32[]{:S(2)}) copy-start(bf16[256,2048]{1,0:T(8,128)(2,1)} %param.19) | copy-start | bytes 3145732
  0.0 58.8 %copy-start.4 = (s32[8]{0:T(128)S(1)}, s32[8]{0:T(128)}, u32[]{:S(2)}) copy-start(s32[8]{0:T(128)} %param.16) | copy-start | bytes 100
  0.0 59.8 %copy-start.3 = (s32[8]{0:T(128)S(1)}, s32[8]{0:T(128)}, u32[]{:S(2)}) copy-start(s32[8]{0:T(128)} %param.17) | copy-start | bytes 100
  0.0 59.9 %copy-start.1 = (bf16[8,256]{1,0:T(8,128)(2,1)S(1)}, bf16[8,256]{1,0:T(8,128)(2,1)}, u32[]{:S(2)}) copy-start(bf16[8,256]{1,0:T(8,128)(2,1)} %param.12) | copy-start | bytes 12292
  0.0 60.0 %copy-start.5 = (bf16[8,2,1,512,128]{4,3,2,1,0:T(8,128)(2,1)S(1)}, bf16[8,2,1,512,128]{4,3,2,1,0:T(8,128)(2,1)}, u32[]{:S(2)}) copy-start(bf16[8,2,1,512,128]{4,3,2,1,0:T(8,128)(2,1)} %param.14) | copy-start | bytes 6291460
  5.1 55.4 %copy-start.2 = (bf16[8,2,64]{2,1,0:T(2,128)(2,1)S(1)}, bf16[8,2,64]{2,1,0:T(2,128)(2,1)}, u32[]{:S(2)}) copy-start(bf16[8,2,64]{2,1,0:T(2,128)(2,1)} %param.13) | copy-start | bytes 6148

commit v4 on v3

--- a/solution.py
+++ b/solution.py
@@ -154,114 +154,179 @@
     return out.reshape((ny * nz,) + x.shape)
 
 
-def scatter_kernel(n, x_ref, out_ref, held, send_sem, recv_sem):
-    me = lax.axis_index("tp")
-    row = lax.axis_index("grp")
+def final_kernel(n, n_tp, partner_ref, back_ref, home_ref, fsel_ref, w_ref, out_ref,
+                 got, part, held, send2, recv2, send3, recv3):
+    me = lax.axis_index("grp")
+    col = lax.axis_index("tp")
+    heads, slots = back_ref.shape[0], back_ref.shape[1]
+    head_width = w_ref.shape[0] // heads
     width = out_ref.shape[1]
 
     barrier = pltpu.get_barrier_semaphore()
-    for k in range(1, n):
+
+    def greet(k, carry):
         peer = lax.rem(me + k, n)
-        pl.semaphore_signal(barrier, inc=1, device_id=(row, peer), device_id_type=MESH)
-    pl.semaphore_wait(barrier, n - 1)
-
-    copies = []
-    for k in range(1, n):
+        pl.semaphore_signal(barrier, inc=1, device_id=(peer, col), device_id_type=MESH)
+        return carry
+
+    lax.fori_loop(1, n, greet, 0)
+    for k in range(1, n_tp):
+        peer = lax.rem(col + k, n_tp)
+        pl.semaphore_signal(barrier, inc=1, device_id=(me, peer), device_id_type=MESH)
+    pl.semaphore_wait(barrier, (n - 1) + (n_tp - 1))
+
+    def copy_to(k):
         peer = lax.rem(me + k, n)
+        return pltpu.make_async_remote_copy(
+            src_ref=back_ref,
+            dst_ref=got.at[me],
+            send_sem=send2.at[k],
+            recv_sem=recv2.at[k],
+            device_id=(peer, col),
+            device_id_type=MESH,
+        )
+
+    def copy_from(k):
+        source = lax.rem(me + n - k, n)
+        return pltpu.make_async_remote_copy(
+            src_ref=back_ref,
+            dst_ref=got.at[source],
+            send_sem=send2.at[k],
+            recv_sem=recv2.at[k],
+            device_id=(source, col),
+            device_id_type=MESH,
+        )
+
+    def start(k, carry):
+        copy_to(k).start()
+        return carry
+
+    lax.fori_loop(1, n, start, 0)
+
+    def finish(k, carry):
+        copy_to(k).wait_send()
+        copy_from(k).wait_recv()
+        return carry
+
+    lax.fori_loop(1, n, finish, 0)
+
+    block = got[partner_ref[0]]
+    fsel = fsel_ref[...]
+    has = fsel[:, 0:1]
+    for k in range(1, slots):
+        has = has + fsel[:, k : k + 1]
+    acc = jnp.zeros(part.shape, jnp.float32)
+    for g in range(heads):
+        theirs = block[g]
+        far = fsel[:, 0:1] * theirs[0:1, :]
+        for k in range(1, slots):
+            far = far + fsel[:, k : k + 1] * theirs[k : k + 1, :]
+        home = home_ref[g]
+        home_m = home[:, head_width : head_width + 1]
+        home_l = home[:, head_width + 1 : head_width + 2]
+        far_m = jnp.where(has > 0.0, far[:, head_width : head_width + 1], -1e30)
+        far_l = far[:, head_width + 1 : head_width + 2]
+        top = jnp.maximum(home_m, far_m)
+        home_e = jnp.exp(home_m - top)
+        far_e = jnp.exp(far_m - top)
+        mix = (home * home_e + far * far_e) / (home_l * home_e + far_l * far_e)
+        acc = acc + jnp.dot(
+            mix[:, :head_width].astype(jnp.bfloat16),
+            w_ref[g * head_width : (g + 1) * head_width, :],
+            preferred_element_type=jnp.float32,
+        )
+    part[...] = acc
+
+    sends = []
+    for k in range(1, n_tp):
+        peer = lax.rem(col + k, n_tp)
         cols = pl.ds(pl.multiple_of(peer * width, width), width)
         copy = pltpu.make_async_remote_copy(
-            src_ref=x_ref.at[:, cols],
+            src_ref=part.at[:, cols],
             dst_ref=held.at[k],
-            send_sem=send_sem.at[k],
-            recv_sem=recv_sem.at[k],
-            device_id=(row, peer),
+            send_sem=send3.at[k],
+            recv_sem=recv3.at[k],
+            device_id=(me, peer),
             device_id_type=MESH,
         )
         copy.start()
-        copies.append(copy)
-    own = pl.ds(pl.multiple_of(me * width, width), width)
-    total = x_ref[:, own]
-    for copy in copies:
+        sends.append(copy)
+    own = pl.ds(pl.multiple_of(col * width, width), width)
+    total = part[:, own]
+    for copy in sends:
         copy.wait_send()
         copy.wait_recv()
-    for k in range(1, n):
+    for k in range(1, n_tp):
         total = total + held[k]
     out_ref[...] = total.astype(out_ref.dtype)
 
 
-def scatter_tp(x, n, cid):
-    rows, cols = x.shape
-    width = cols // n
+def finish_call(n, n_tp, partner, back, home, fsel, out_weight, cid):
+    rows = home.shape[1]
+    width = out_weight.shape[1] // n_tp
+    vmem = pl.BlockSpec(memory_space=pltpu.VMEM)
     return pl.pallas_call(
-        functools.partial(scatter_kernel, n),
+        functools.partial(final_kernel, n, n_tp),
         out_shape=jax.ShapeDtypeStruct((rows, width), jnp.bfloat16),
-        in_specs=[pl.BlockSpec(memory_space=pltpu.VMEM)],
-        out_specs=pl.BlockSpec(memory_space=pltpu.VMEM),
+        in_specs=[pl.BlockSpec(memory_space=pltpu.SMEM), vmem, vmem, vmem, vmem],
+        out_specs=vmem,
         scratch_shapes=[
-            pltpu.VMEM((n, rows, width), jnp.float32),
+            pltpu.VMEM((n,) + back.shape, jnp.float32),
+            pltpu.VMEM((rows, out_weight.shape[1]), jnp.float32),
+            pltpu.VMEM((n_tp, rows, width), jnp.float32),
             pltpu.SemaphoreType.DMA((n,)),
             pltpu.SemaphoreType.DMA((n,)),
+            pltpu.SemaphoreType.DMA((n_tp,)),
+            pltpu.SemaphoreType.DMA((n_tp,)),
         ],
         compiler_params=pltpu.CompilerParams(collective_id=cid, has_side_effects=True),
-    )(x)
+    )(partner, back, home, fsel, out_weight)
+
+
+def pack(m, l, u):
+    rows, heads, hw = u.shape
+    lanes = 128
+    packed = jnp.concatenate(
+        [u, m[..., None], l[..., None], jnp.zeros((rows, heads, lanes - hw - 2), jnp.float32)],
+        axis=-1,
+    )
+    return packed.transpose(1, 0, 2)
 
 
 def per_device(ny, nz, queries, new_kv, home_cache, help_cache, lengths, split_at, helper_req, out_weight):
     n_grp = lax.axis_size("grp")
     n_tp = lax.axis_size("tp")
     row_count, width = queries.shape
+
+    count = lengths - split_at
+    lanes = 128
+    extra = (
+        jnp.zeros((row_count, lanes), jnp.bfloat16)
+        .at[:, 0]
+        .set((count // 32).astype(jnp.bfloat16))
+        .at[:, 1]
+        .set((count % 32).astype(jnp.bfloat16))
+    )
+    sent = jnp.concatenate([queries, extra], axis=1)
+    got = gather_grp(sent, ny, nz, 0).reshape(n_grp * row_count, width + lanes)
+    picked = got[helper_req]
+    help_queries = picked[:, :width]
+    help_count = (
+        picked[:, width].astype(jnp.int32) * 32 + picked[:, width + 1].astype(jnp.int32)
+    )
+    help_m, help_l, help_u = attend(help_queries, help_cache, help_count, None)
+    back = pack(help_m, help_l, help_u)
+
+    home_m, home_l, home_u = attend(queries, home_cache, split_at, new_kv)
+    home = pack(home_m, home_l, home_u)
+
     slots = help_cache.shape[0]
-    heads = width // 64
-    head_width = 64
-
     is_long = lengths > LONG_AT
-    order = jnp.argsort(jnp.where(is_long, 0, 1), stable=True)[:slots]
-    long_count = (lengths - split_at)[order]
-    hi = (long_count // 32).astype(jnp.bfloat16)
-    lo = (long_count % 32).astype(jnp.bfloat16)
-    pad = 128
-    extra = jnp.zeros((slots, pad), jnp.bfloat16).at[:, 0].set(hi).at[:, 1].set(lo)
-    sent = jnp.concatenate([queries[order], extra], axis=1)
-
-    partner = helper_req[0] // row_count
-    got = gather_grp(sent, ny, nz, 0)
-    mine = lax.dynamic_index_in_dim(got, partner, axis=0, keepdims=False)
-    help_queries = mine[:, :width]
-    help_count = (
-        mine[:, width].astype(jnp.int32) * 32 + mine[:, width + 1].astype(jnp.int32)
-    )
-
-    home_m, home_l, home_u = attend(queries, home_cache, split_at, new_kv)
-    help_m, help_l, help_u = attend(help_queries, help_cache, help_count, None)
-
-    back = jnp.concatenate(
-        [
-            help_u.reshape(slots, heads * head_width),
-            help_m,
-            help_l,
-            jnp.zeros((slots, pad - 2 * heads), jnp.float32),
-        ],
-        axis=1,
-    )
-    got_back = gather_grp(back, ny, nz, 1)
-    theirs = lax.dynamic_index_in_dim(got_back, partner, axis=0, keepdims=False)
-    t_u = theirs[:, : heads * head_width].reshape(slots, heads, head_width)
-    t_m = theirs[:, heads * head_width : heads * head_width + heads]
-    t_l = theirs[:, heads * head_width + heads : heads * head_width + 2 * heads]
-
-    own_sel = (jnp.arange(row_count)[:, None] == order[None, :]) & is_long[order][None, :]
-    far_m = jnp.max(jnp.where(own_sel[:, :, None], t_m[None], -1e30), axis=1)
-    far_l = jnp.sum(jnp.where(own_sel[:, :, None], t_l[None], 0.0), axis=1)
-    far_u = jnp.sum(jnp.where(own_sel[:, :, None, None], t_u[None], 0.0), axis=1)
-    top_score = jnp.maximum(home_m, far_m)
-    home_e = jnp.exp(home_m - top_score)
-    far_e = jnp.exp(far_m - top_score)
-    numerator = home_u * home_e[..., None] + far_u * far_e[..., None]
-    denominator = home_l * home_e + far_l * far_e
-    heads_out = numerator / denominator[..., None]
-    mix = heads_out.reshape(row_count, -1).astype(jnp.bfloat16)
-    partial_out = jnp.dot(mix, out_weight, preferred_element_type=jnp.float32)
-    return scatter_tp(partial_out, n_tp, 2)
+    before = jnp.arange(row_count)[None, :] < jnp.arange(row_count)[:, None]
+    rank = jnp.sum(jnp.where(before, is_long[None, :], False), axis=1)
+    fsel = (is_long[:, None] & (rank[:, None] == jnp.arange(slots)[None, :])).astype(jnp.float32)
+    partner = (helper_req[:1] // row_count).astype(jnp.int32)
+    return finish_call(n_grp, n_tp, partner, back, home, fsel, out_weight, 1)
 
 
 def grp_rows(mesh):

time: 77.6 us -> 83.3 us (1.073)
  Pallas kernels: 55.3 us -> 63 us
  local copies, waits for them, and re-layouts: 7.38 us -> 4.35 us
  other arithmetic: 6.96 us -> 9.07 us
  matrix products: 4.51 us -> 3.63 us
    pallas_call x1, Pallas kernels: 12.1 us -> 32.1 us  [finish_call(): pl.pallas_call(functools.partial(final_kernel, n, n_tp), out_shape=jax.Sh...]
    pallas_call x2 -> x1, Pallas kernels: 43.1 us -> 30.9 us  [gather_grp(): pl.pallas_call(functools.partial(gather_kernel, ny, nz), out_shape=jax.Sh...]
    squeeze x2 -> x0, local copies, waits for them, and re-layouts: 1.38 us -> none  [the longest x1 0.7 us: per_device(): theirs = lax.dynamic_index_in_dim(got_back, partner, axis=0, keepdims=False)]
    transpose x0 -> x2, other arithmetic: none -> 1.36 us  [pack(): return packed.transpose(1, 0, 2)]
    gather x4 -> x1, local copies, waits for them, and re-layouts: 2.63 us -> 1.61 us  [per_device(): picked = got[helper_req]]
    sort x1 -> x0, other arithmetic: 0.96 us -> none  [per_device(): order = jnp.argsort(jnp.where(is_long, 0, 1), stable=True)[:slots]]
    dot_general x1 -> x0, matrix products: 0.88 us -> none  [per_device(): partial_out = jnp.dot(mix, out_weight, preferred_element_type=jnp.float32)]
    another operation x3 -> x4, other arithmetic: 2.7 us -> 3.38 us
where the time goes in v4:
time: 83.3 us; the launch traced here: 82.9 us
  Pallas kernels  63 us (76%)
  other arithmetic  9.07 us (11%)
  local copies, waits for them, and re-layouts  4.35 us (5%)
  matrix products  3.63 us (4%)
  between operations  2.85 us (3%)
    pallas_call x1, Pallas kernels, finish_call(): pl.pallas_call(functools.partial(final_kernel, n, n_tp), out_shape=jax.Sh...  32.1 us
    pallas_call x1, Pallas kernels, gather_grp(): pl.pallas_call(functools.partial(gather_kernel, ny, nz), out_shape=jax.Sh...  30.9 us
    another operation x3, other arithmetic  3.38 us
    dot_general x2, matrix products, attend(): jnp.einsum('nkgjc,nkpc->nkgjp', wide_rows, key_rows, preferred_element_ty...  1.86 us

profile of v4, /device:TPU:1, one launch (start us, length us, event | category | flops | bytes accessed | tf_op | source)
XLA Modules:
  0.0 82.9 jit_solution(17365673118645550909)
XLA Ops:
  2.8 0.6 compare_reduce_fusion
  3.4 0.7 compare_reduce_fusion.1
  4.1 2.0 %fusion.24 = (bf16[8,1]{0,1:T(2,128)(2,1)S(1)}, bf16[8,1]{0,1:T(2,128)(2,1)S(1)}) fusion(pred[]{:T(512)} %compare_reduce_fusion, s32[8]{0:T(128)} %param.16, s32[8]{0:T(128)} %param.17, pred[]{:T(512)} %compare_reduce_fusion.1), kind=kLoop, calls=%fused_computation.71 | loop fusion | flops 192 | bytes 98 | tf_op jit(solution)/shard_map/reshape.189
  6.1 0.1 copy.58
  6.2 0.1 copy.59
  6.3 0.1 scatter.9
  6.4 1.3 %pad_maximum_fusion.x_ref = bf16[8,384]{1,0:T(8,128)(2,1)} fusion(bf16[8,128]{1,0:T(8,128)(2,1)S(1)} %scatter.9, bf16[8,256]{1,0:T(8,128)(2,1)} %param.12), kind=kLoop, calls=%fused_computation.38 | loop fusion | flops 12288 | bytes 12288 | tf_op jit(solution)/shard_map/concatenate | solution.py:310
  7.7 30.9 %shard_map.82 = bf16[8,8,8,384]{3,2,1,0:T(8,128)(2,1)} custom-call(bf16[8,384]{1,0:T(8,128)(2,1)} %pad_maximum_fusion.x_ref), custom_call_target="tpu_custom_call" | custom-call | tf_op jit(solution)/shard_map/pallas_call | solution.py:139
  38.6 0.7 compare_select_fusion
  39.3 1.6 %gather_fusion = bf16[4,384]{1,0:T(4,128)(2,1)S(1)} fusion(bf16[512,384]{1,0:T(8,128)(2,1)} %bitcast.102, s32[1024]{0:T(1024)S(1)} %pad_clamp_fusion), kind=kCustom, calls=%fused_computation | custom fusion | bytes 6160 | tf_op jit(solution)/shard_map/gather | solution.py:312
  40.9 0.2 add_reduce_fusion
  41.3 1.4 %select_reduce_fusion.1 = (f32[4,4]{1,0:T(4,128)S(1)}, f32[4,4,2,512]{3,1,2,0:T(4,128)S(1)}) fusion(pred[4,2,512]{2,1,0:T(4,128)(4,1)S(1)} %broadcast_compare_fusion.1, bf16[4,2,1,512,128]{4,3,2,1,0:T(8,128)(2,1)} %param.15, bf16[4,1,4,1,128]{4,2,3,0,1:T(4,128)(2,1)S(1)} %get-tuple-element.36, bf16[4,1,4,1,128]{4,2,3,0,1:T(4,128)(2,1)S(1)} %get-tuple-element.35), kind=kOutput, calls=%fused_computation.18 | convolution fusion | flops 4259824 | bytes 602176 | tf_op jit(solution)/shard_map/nkgjc,nkpc->nkgjp/dot_general | solution.py:33
  42.7 1.3 %fusion.5 = f32[4,4,2,128]{3,1,2,0:T(4,128)S(1)} fusion(bf16[4,2,1,512,128]{4,3,2,1,0:T(8,128)(2,1)} %param.15, f32[4,4,2,512]{3,1,2,0:T(4,128)S(1)} %get-tuple-element.40, f32[4,4]{1,0:T(4,128)S(1)} %get-tuple-element.39, pred[4,2,512]{2,1,0:T(4,128)(4,1)S(1)} %broadcast_compare_fusion.1), kind=kOutput, calls=%fused_computation.8 | convolution fusion | flops 4243456 | bytes 610368 | tf_op jit(solution)/shard_map/nkgjp,nkpc->nkgjc/dot_general | solution.py:50
  44.1 0.2 convert_reduce_fusion.1
  44.3 0.1 copy.65
  44.4 0.1 copy.64
  44.6 0.7 maximum_bitcast_fusion.5.back_ref
  45.3 0.7 broadcast_compare_fusion
  46.0 0.1 reshape.229
  46.2 0.5 select_reduce_fusion
  46.7 0.1 reshape.232
  46.8 0.1 fusion.20
  46.9 0.3 fusion
  47.3 0.1 copy.71
  47.5 0.2 convert_reduce_fusion
  47.8 0.1 copy.75
  47.9 0.1 copy.74
  48.0 0.7 maximum_bitcast_fusion.2.home_ref
  48.7 0.1 convert_reduce_fusion.2
  48.8 0.7 fusion.19.fsel_ref
  49.5 32.1 %shard_map.83 = bf16[8,256]{1,0:T(8,128)(2,1)} custom-call(s32[1]{0:T(128)S(6)} %select_n.42.partner_ref, f32[4,4,128]{2,1,0:T(4,128)} %maximum_bitcast_fusion.5.back_ref, f32[4,8,128]{2,1,0:T(8,128)} %maximum_bitcast_fusion.2.home_ref, f32[8,4]{1,0:T(8,128)} %fusion.19.fsel_ref, bf16[256,2048]{1,0:T(8,128)(2,1)} %w_ref.1), custom_call_target="tpu_custom_call" | custom-call | tf_op jit(solution)/shard_map/pallas_call | solution.py:268
  81.6 1.3 %copy.99 = bf16[8,256]{1,0:T(8,128)(2,1)} copy(bf16[8,256]{1,0:T(8,128)(2,1)} %shard_map.83) | data formatting | bytes 8192
  (30 shorter events, 0.8 us)
Async XLA Ops:
  0.0 46.0 %copy-start = (bf16[8,256]{1,0:T(8,128)(2,1)S(1)}, bf16[8,256]{1,0:T(8,128)(2,1)}, u32[]{:S(2)}) copy-start(bf16[8,256]{1,0:T(8,128)(2,1)} %param.12) | copy-start | bytes 12292
  0.0 46.2 %copy-start.3 = (bf16[8,2,1,512,128]{4,3,2,1,0:T(8,128)(2,1)S(1)}, bf16[8,2,1,512,128]{4,3,2,1,0:T(8,128)(2,1)}, u32[]{:S(2)}) copy-start(bf16[8,2,1,512,128]{4,3,2,1,0:T(8,128)(2,1)} %param.14) | copy-start | bytes 6291460
  0.0 46.7 %copy-start.1 = (bf16[8,2,64]{2,1,0:T(2,128)(2,1)S(1)}, bf16[8,2,64]{2,1,0:T(2,128)(2,1)}, u32[]{:S(2)}) copy-start(bf16[8,2,64]{2,1,0:T(2,128)(2,1)} %param.13) | copy-start | bytes 6148
  42.7 6.0 %copy-start.2 = (s32[8]{0:T(128)S(1)}, s32[8]{0:T(128)}, u32[]{:S(2)}) copy-start(s32[8]{0:T(128)} %param.16) | copy-start | bytes 100

commit v5 on v4

v5 whole, which is shorter than its diff:
```python
import functools

import jax
import jax.numpy as jnp
from jax import lax
from jax.experimental import pallas as pl
from jax.experimental.pallas import tpu as pltpu
from jax.sharding import PartitionSpec as P

MESH = pl.DeviceIdType.MESH
LONG_AT = 1024


def attend(queries, cache, count, fresh):
    row_count = queries.shape[0]
    kv_heads = cache.shape[2]
    head_width = cache.shape[4] // 2
    half = cache.shape[3]
    group_size = queries.shape[1] // (kv_heads * head_width)
    score_scale = head_width ** (-0.5)
    head_rows = queries.reshape(row_count, kv_heads, group_size, head_width)
    blank = jnp.zeros_like(head_rows)
    wide_rows = jnp.stack(
        [
            jnp.concatenate([head_rows, blank], axis=-1),
            jnp.concatenate([blank, head_rows], axis=-1),
        ],
        axis=3,
    )
    key_rows = cache[:, 0]
    value_rows = cache[:, 1]
    scores = (
        jnp.einsum("nkgjc,nkpc->nkgjp", wide_rows, key_rows, preferred_element_type=jnp.float32)
        * score_scale
    )
    position = 2 * jnp.arange(half)[None, :] + jnp.arange(2)[:, None]
    inside = (position[None] < count[:, None, None])[:, None, None]
    top_score = jnp.max(jnp.where(inside, scores, -1e30), axis=(-2, -1))
    if fresh is not None:
        fresh_key = fresh[:, 0].reshape(row_count, kv_heads, head_width)
        fresh_score = (
            jnp.einsum("nkgd,nkd->nkg", head_rows, fresh_key, preferred_element_type=jnp.float32)
            * score_scale
        )
        top_score = jnp.maximum(top_score, fresh_score)
    weights = jnp.where(
        inside, jnp.exp(scores - top_score[..., None, None]), 0.0
    ).astype(jnp.bfloat16)
    weight_sum = jnp.sum(weights.astype(jnp.float32), axis=(-2, -1))
    both = jnp.einsum(
        "nkgjp,nkpc->nkgjc", weights, value_rows, preferred_element_type=jnp.float32
    )
    mixed_sum = both[..., 0, :head_width] + both[..., 1, head_width:]
    if fresh is not None:
        fresh_weight = lax.optimization_barrier(
            jnp.exp(fresh_score - top_score).astype(jnp.bfloat16)
        ).astype(jnp.float32)
        weight_sum = weight_sum + fresh_weight
        fresh_value = fresh[:, 1].reshape(row_count, kv_heads, 1, head_width).astype(jnp.float32)
        mixed_sum = mixed_sum + fresh_weight[..., None] * fresh_value
    return (
        top_score.reshape(row_count, -1),
        weight_sum.reshape(row_count, -1),
        mixed_sum.reshape(row_count, -1, head_width),
    )


def gather_kernel(n, x_ref, out_ref, held, send_sem, recv_sem):
    me = lax.axis_index("grp")
    col = lax.axis_index("tp")

    barrier = pltpu.get_barrier_semaphore()

    def greet(k, carry):
        peer = lax.rem(me + k, n)
        pl.semaphore_signal(barrier, inc=1, device_id=(peer, col), device_id_type=MESH)
        return carry

    lax.fori_loop(1, n, greet, 0)
    pl.semaphore_wait(barrier, n - 1)

    def copy_to(k):
        peer = lax.rem(me + k, n)
        return pltpu.make_async_remote_copy(
            src_ref=x_ref,
            dst_ref=held.at[me],
            send_sem=send_sem.at[k],
            recv_sem=recv_sem.at[k],
            device_id=(peer, col),
            device_id_type=MESH,
        )

    def copy_from(k):
        source = lax.rem(me + n - k, n)
        return pltpu.make_async_remote_copy(
            src_ref=x_ref,
            dst_ref=held.at[source],
            send_sem=send_sem.at[k],
            recv_sem=recv_sem.at[k],
            device_id=(source, col),
            device_id_type=MESH,
        )

    def start(k, carry):
        copy_to(k).start()
        return carry

    lax.fori_loop(1, n, start, 0)

    def finish(k, carry):
        copy_to(k).wait_send()
        copy_from(k).wait_recv()
        return carry

    lax.fori_loop(1, n, finish, 0)
    held[me] = x_ref[...]
    out_ref[...] = held[...]


def gather_grp(x, n, cid):
    return pl.pallas_call(
        functools.partial(gather_kernel, n),
        out_shape=jax.ShapeDtypeStruct((n,) + x.shape, x.dtype),
        in_specs=[pl.BlockSpec(memory_space=pltpu.VMEM)],
        out_specs=pl.BlockSpec(memory_space=pltpu.VMEM),
        scratch_shapes=[
            pltpu.VMEM((n,) + x.shape, x.dtype),
            pltpu.SemaphoreType.DMA((n,)),
            pltpu.SemaphoreType.DMA((n,)),
        ],
        compiler_params=pltpu.CompilerParams(collective_id=cid, has_side_effects=True),
    )(x)


def final_kernel(n, n_tp, heads, slots, stat_row, partner_ref, back_ref, home_ref, hm_ref, hl_ref,
                 fsel_ref, fwide_ref, w_ref, out_ref, got, part, held, send2, recv2, send3, recv3):
    me = lax.axis_index("grp")
    col = lax.axis_index("tp")
    head_width = w_ref.shape[0] // heads
    width = out_ref.shape[1]

    barrier = pltpu.get_barrier_semaphore()

    def greet(k, carry):
        peer = lax.rem(me + k, n)
        pl.semaphore_signal(barrier, inc=1, device_id=(peer, col), device_id_type=MESH)
        return carry

    lax.fori_loop(1, n, greet, 0)
    for k in range(1, n_tp):
        peer = lax.rem(col + k, n_tp)
        pl.semaphore_signal(barrier, inc=1, device_id=(me, peer), device_id_type=MESH)
    pl.semaphore_wait(barrier, (n - 1) + (n_tp - 1))

    def copy_to(k):
        peer = lax.rem(me + k, n)
        return pltpu.make_async_remote_copy(
            src_ref=back_ref,
            dst_ref=got.at[me],
            send_sem=send2.at[k],
            recv_sem=recv2.at[k],
            device_id=(peer, col),
            device_id_type=MESH,
        )

    def copy_from(k):
        source = lax.rem(me + n - k, n)
        return pltpu.make_async_remote_copy(
            src_ref=back_ref,
            dst_ref=got.at[source],
            send_sem=send2.at[k],
            recv_sem=recv2.at[k],
            device_id=(source, col),
            device_id_type=MESH,
        )

    def start(k, carry):
        copy_to(k).start()
        return carry

    lax.fori_loop(1, n, start, 0)

    def finish(k, carry):
        copy_to(k).wait_send()
        copy_from(k).wait_recv()
        return carry

    lax.fori_loop(1, n, finish, 0)

    block = got[partner_ref[0]].astype(jnp.float32)
    fsel = fsel_ref[...]
    wide = fwide_ref[...]
    stats = block[stat_row : stat_row + 1, :]
    n_st = slots * heads

    def parts(base):
        return (
            stats[:, base : base + n_st]
            + stats[:, base + n_st : base + 2 * n_st]
            + stats[:, base + 2 * n_st : base + 3 * n_st]
        )

    def per_head(x):
        y = x[:, 0:heads]
        for k in range(1, slots):
            y = y + x[:, k * heads : (k + 1) * heads]
        return y

    has = per_head(wide)[:, 0:1] * 0.0
    for k in range(slots):
        has = has + fsel[:, k : k + 1]
    far_m = jnp.where(has > 0.0, per_head(wide * parts(0)), -1e30)
    far_l = per_head(wide * parts(3 * n_st))
    home_m_all = hm_ref[...]
    home_l_all = hl_ref[...]
    lane = lax.broadcasted_iota(jnp.int32, (fsel.shape[0], 2 * head_width), 1)
    left = lane < head_width

    def spread(x, h):
        return jnp.where(left, x[:, 2 * h : 2 * h + 1], x[:, 2 * h + 1 : 2 * h + 2])

    acc = jnp.zeros(part.shape, jnp.float32)
    for h in range(heads // 2):
        far = fsel[:, 0:1] * block[h : h + 1, :]
        for k in range(1, slots):
            far = far + fsel[:, k : k + 1] * block[2 * k + h : 2 * k + h + 1, :]
        home = home_ref[h]
        home_m = spread(home_m_all, h)
        home_l = spread(home_l_all, h)
        fm = spread(far_m, h)
        fl = spread(far_l, h)
        top = jnp.maximum(home_m, fm)
        home_e = jnp.exp(home_m - top)
        far_e = jnp.exp(fm - top)
        mix = (home * home_e + far * far_e) / (home_l * home_e + fl * far_e)
        acc = acc + jnp.dot(
            mix.astype(jnp.bfloat16),
            w_ref[h * 2 * head_width : (h + 1) * 2 * head_width, :],
            preferred_element_type=jnp.float32,
        )
    part[...] = acc

    sends = []
    for k in range(1, n_tp):
        peer = lax.rem(col + k, n_tp)
        cols = pl.ds(pl.multiple_of(peer * width, width), width)
        copy = pltpu.make_async_remote_copy(
            src_ref=part.at[:, cols],
            dst_ref=held.at[k],
            send_sem=send3.at[k],
            recv_sem=recv3.at[k],
            device_id=(me, peer),
            device_id_type=MESH,
        )
        copy.start()
        sends.append(copy)
    own = pl.ds(pl.multiple_of(col * width, width), width)
    total = part[:, own]
    for copy in sends:
        copy.wait_send()
        copy.wait_recv()
    for k in range(1, n_tp):
        total = total + held[k]
    out_ref[...] = total.astype(out_ref.dtype)


def finish_call(n, n_tp, heads, slots, stat_row, partner, back, home, home_m, home_l, fsel, fwide,
                out_weight, cid):
    rows = home.shape[1]
    width = out_weight.shape[1] // n_tp
    vmem = pl.BlockSpec(memory_space=pltpu.VMEM)
    return pl.pallas_call(
        functools.partial(final_kernel, n, n_tp, heads, slots, stat_row),
        out_shape=jax.ShapeDtypeStruct((rows, width), jnp.bfloat16),
        in_specs=[pl.BlockSpec(memory_space=pltpu.SMEM)] + [vmem] * 7,
        out_specs=vmem,
        scratch_shapes=[
            pltpu.VMEM((n,) + back.shape, back.dtype),
            pltpu.VMEM((rows, out_weight.shape[1]), jnp.float32),
            pltpu.VMEM((n_tp, rows, width), jnp.float32),
            pltpu.SemaphoreType.DMA((n,)),
            pltpu.SemaphoreType.DMA((n,)),
            pltpu.SemaphoreType.DMA((n_tp,)),
            pltpu.SemaphoreType.DMA((n_tp,)),
        ],
        compiler_params=pltpu.CompilerParams(collective_id=cid, has_side_effects=True),
    )(partner, back, home, home_m, home_l, fsel, fwide, out_weight)


def three_way(x):
    hi = x.astype(jnp.bfloat16)
    rest = x - hi.astype(jnp.float32)
    mid = rest.astype(jnp.bfloat16)
    lo = (rest - mid.astype(jnp.float32)).astype(jnp.bfloat16)
    return [hi, mid, lo]


def tile(rows_of, extra):
    lanes = rows_of.shape[1]
    rows = rows_of.shape[0]
    stat = jnp.zeros((1, lanes), jnp.bfloat16).at[0, : extra.shape[0]].set(extra)
    pad = jnp.zeros((16 - rows - 1, lanes), jnp.bfloat16)
    return jnp.concatenate([rows_of, stat, pad], axis=0)


def per_device(ny, nz, queries, new_kv, home_cache, help_cache, lengths, split_at, helper_req, out_weight):
    n_grp = lax.axis_size("grp")
    n_tp = lax.axis_size("tp")
    row_count, width = queries.shape
    slots = help_cache.shape[0]
    heads = width // 64
    lanes = 128

    is_long = lengths > LONG_AT
    before = jnp.arange(row_count)[None, :] < jnp.arange(row_count)[:, None]
    rank = jnp.sum(jnp.where(before, is_long[None, :], False), axis=1)
    pick = is_long[None, :] & (rank[None, :] == jnp.arange(slots)[:, None])
    long_q = jnp.dot(
        pick.astype(jnp.bfloat16), queries, preferred_element_type=jnp.float32
    ).astype(jnp.bfloat16)
    long_count = jnp.sum(jnp.where(pick, (lengths - split_at)[None, :], 0), axis=1)
    counts = jnp.concatenate([long_count // 32, long_count % 32]).astype(jnp.bfloat16)
    stat_row = slots * width // lanes
    sent = tile(long_q.reshape(stat_row, lanes), counts)

    partner = helper_req[0] // row_count
    got = gather_grp(sent, n_grp, 0)
    mine = lax.dynamic_index_in_dim(got, partner, axis=0, keepdims=False)
    help_queries = mine[:stat_row].reshape(slots, width)
    code = mine[stat_row].astype(jnp.int32)
    help_count = code[:slots] * 32 + code[slots : 2 * slots]
    help_m, help_l, help_u = attend(help_queries, help_cache, help_count, None)
    stat_parts = three_way(help_m.reshape(-1)) + three_way(help_l.reshape(-1))
    back = tile(
        help_u.astype(jnp.bfloat16).reshape(stat_row, lanes), jnp.concatenate(stat_parts)
    )

    home_m, home_l, home_u = attend(queries, home_cache, split_at, new_kv)
    home = home_u.reshape(row_count, heads // 2, lanes).transpose(1, 0, 2)
    fsel = (is_long[:, None] & (rank[:, None] == jnp.arange(slots)[None, :])).astype(jnp.float32)
    fwide = jnp.repeat(fsel, heads, axis=1)
    partner_arr = (helper_req[:1] // row_count).astype(jnp.int32)
    return finish_call(
        n_grp, n_tp, heads, slots, stat_row, partner_arr, back, home, home_m, home_l, fsel, fwide,
        out_weight, 1,
    )


def grp_rows(mesh):
    column = list(mesh.devices[:, 0])
    n = len(column)
    coords = [getattr(d, "coords", None) for d in column]
    if coords[0] is not None:
        nz = 1
        while nz < n and coords[nz][1] == coords[0][1]:
            nz += 1
    else:
        nz = 1
        while nz * nz < n:
            nz *= 2
    return n // nz, nz


def solution(mesh):
    ny, nz = grp_rows(mesh)
    return jax.shard_map(
        functools.partial(per_device, ny, nz),
        mesh=mesh,
        in_specs=(
            P("grp", "tp"),
            P("grp", None, "tp"),
            P("grp", None, "tp", None, None),
            P("grp", None, "tp", None, None),
            P("grp"),
            P("grp"),
            P("grp"),
            P("tp", None),
        ),
        out_specs=P("grp", "tp"),
        check_vma=False,
    )
```

time: 83.3 us -> 78.3 us (0.940)
  Pallas kernels: 63 us -> 53.3 us
  between operations: 2.85 us -> 5.48 us
  matrix products: 3.63 us -> 5.65 us
  other arithmetic: 9.07 us -> 7.92 us
  local copies, waits for them, and re-layouts: 4.35 us -> 5.39 us
    pallas_call x2, Pallas kernels: 63 us -> 53.3 us  [the longest x1 27 us: finish_call(): pl.pallas_call(functools.partial(final_kernel, n, n_tp, heads, slots, sta...]
    gather x1 -> x0, local copies, waits for them, and re-layouts: 1.61 us -> none  [per_device(): picked = got[helper_req]]
    reshape x0 -> x3, local copies, waits for them, and re-layouts: none -> 1.34 us  [the longest x1 0.67 us: attend(): weight_sum.reshape(row_count, -1)]
    another operation x4 -> x3, other arithmetic: 3.38 us -> 2.05 us
    dot_general x2, matrix products: 1.86 us -> 3.09 us  [attend(): jnp.einsum('nkgjc,nkpc->nkgjp', wide_rows, key_rows, preferred_element_ty...]
where the time goes in v5:
time: 78.3 us; the launch traced here: 77.7 us
  Pallas kernels  53.3 us (68%)
  other arithmetic  7.92 us (10%)
  matrix products  5.65 us (7%)
  between operations  5.48 us (7%)
  local copies, waits for them, and re-layouts  5.39 us (7%)
    pallas_call x1, Pallas kernels, finish_call(): pl.pallas_call(functools.partial(final_kernel, n, n_tp, heads, slots, sta...  27 us
    pallas_call x1, Pallas kernels, gather_grp(): pl.pallas_call(functools.partial(gather_kernel, n), out_shape=jax.ShapeDt...  26.3 us
    dot_general x2, matrix products, attend(): jnp.einsum('nkgjc,nkpc->nkgjp', wide_rows, key_rows, preferred_element_ty...  3.09 us
    another operation x3, other arithmetic  2.05 us
    dot_general x2, matrix products, attend(): jnp.einsum('nkgjp,nkpc->nkgjc', weights, value_rows, preferred_element_ty...  1.64 us

profile of v5, /device:TPU:1, one launch (start us, length us, event | category | flops | bytes accessed | tf_op | source)
XLA Modules:
  0.0 77.7 jit_solution(17541219792991055896)
XLA Ops:
  2.8 0.7 broadcast_compare_fusion.2
  3.4 0.1 convert_reduce_fusion.2
  3.6 0.7 sub.74
  4.2 0.1 select_reduce_fusion.2
  4.4 0.7 compare_reduce_fusion
  5.1 0.7 broadcast_select_fusion.1
  5.8 0.8 %convolution_convert_fusion = bf16[4,256]{1,0:T(4,128)(2,1)S(1)} fusion(bf16[8,256]{1,0:T(8,128)(2,1)} %param.12, s32[8]{0:T(128)S(1)} %convert_reduce_fusion.2, pred[8]{0:T(512)(128)(4,1)S(1)} %broadcast_compare_fusion.2), kind=kOutput, calls=%fused_computation.4 | convolution fusion | flops 17472 | bytes 6184 | tf_op jit(solution)/shard_map/dot_general | solution.py:318
  6.7 0.7 fusion.18.x_ref
  7.4 26.3 %shard_map.82 = bf16[64,16,128]{2,1,0:T(8,128)(2,1)} custom-call(bf16[16,128]{1,0:T(8,128)(2,1)} %fusion.18.x_ref), custom_call_target="tpu_custom_call" | custom-call | tf_op jit(solution)/shard_map/pallas_call | solution.py:121
  33.7 0.7 constant_dynamic-slice_fusion
  34.5 0.7 dynamic-slice_convert_fusion
  35.4 1.4 %select_reduce_fusion.1 = (f32[4,4]{1,0:T(4,128)S(1)}, f32[4,4,2,512]{3,1,2,0:T(4,128)S(1)}) fusion(pred[4,2,512]{2,1,0:T(4,128)(4,1)S(1)} %broadcast_compare_fusion.1, bf16[4,2,1,512,128]{4,3,2,1,0:T(8,128)(2,1)} %param.15, bf16[4,1,4,1,128]{4,2,3,0,1:T(4,128)(2,1)S(1)} %get-tuple-element.36, bf16[4,1,4,1,128]{4,2,3,0,1:T(4,128)(2,1)S(1)} %get-tuple-element.35), kind=kOutput, calls=%fused_computation.18 | convolution fusion | flops 4259824 | bytes 602176 | tf_op jit(solution)/shard_map/nkgjc,nkpc->nkgjp/dot_general | solution.py:33
  36.8 1.3 %convolution_bitcast_fusion.1 = f32[4,1,4,2,128]{4,2,3,0,1:T(4,128)S(1)} fusion(bf16[4,2,1,512,128]{4,3,2,1,0:T(8,128)(2,1)} %param.15, f32[4,4,2,512]{3,1,2,0:T(4,128)S(1)} %get-tuple-element.46, f32[4,4]{1,0:T(4,128)S(1)} %get-tuple-element.45, pred[4,2,512]{2,1,0:T(4,128)(4,1)S(1)} %broadcast_compare_fusion.1), kind=kOutput, calls=%fused_computation.3 | convolution fusion | flops 4243456 | bytes 610368 | tf_op jit(solution)/shard_map/nkgjp,nkpc->nkgjc/dot_general | solution.py:50
  38.1 0.1 convert_element_type.170
  38.2 0.2 convert_reduce_fusion.1
  38.6 0.1 concatenate.67
  38.7 0.6 broadcast_select_fusion
  39.4 0.7 fusion.20.back_ref
  42.6 0.7 broadcast_compare_fusion
  43.4 0.8 reshape.311
  44.2 1.7 %select_reduce_fusion = (f32[8,4]{1,0:T(8,128)S(1)}, f32[8,4,2,512]{3,1,2,0:T(4,128)S(1)}) fusion(pred[8,2,512]{2,1,0:T(4,128)(4,1)S(1)} %broadcast_compare_fusion, bf16[8,2,1,512,128]{4,3,2,1,0:T(8,128)(2,1)} %param.14, bf16[8,1,4,1,128]{4,2,3,0,1:T(4,128)(2,1)S(1)} %get-tuple-element.32, bf16[8,1,4,1,128]{4,2,3,0,1:T(4,128)(2,1)S(1)} %get-tuple-element.31), kind=kOutput, calls=%fused_computation.15 | convolution fusion | flops 8519648 | bytes 1204352 | tf_op jit(solution)/shard_map/nkgjc,nkpc->nkgjp/dot_general | solution.py:33
  46.1 0.1 fusion.24
  46.2 0.3 convolution_bitcast_fusion
  46.6 0.1 add.108
  46.7 0.1 copy.56
  47.0 0.1 mul.69
  47.1 0.6 fusion.13.home_ref
  47.7 0.2 convert_reduce_fusion
  48.0 0.7 copy.62.hl_ref
  48.8 0.7 copy.63.fwide_ref
  49.5 27.0 %shard_map.83 = bf16[8,256]{1,0:T(8,128)(2,1)} custom-call(s32[1]{0:T(128)S(6)} %select_n.59.partner_ref, bf16[16,128]{1,0:T(8,128)(2,1)} %fusion.20.back_ref, f32[2,8,128]{2,1,0:T(8,128)} %fusion.13.home_ref, f32[8,4]{1,0:T(8,128)} %copy-done, f32[8,4]{1,0:T(8,128)} %copy.62.hl_ref, f32[8,4]{1,0:T(8,128)} %copy-done.1, f32[8,16]{1,0:T(8,128)} %copy.63.fwide_ref, ...), custom_call_target="tpu_custom_call" | custom-call | tf_op jit(solution)/shard_map/pallas_call | solution.py:272
  76.5 1.3 %copy.84 = bf16[8,256]{1,0:T(8,128)(2,1)} copy(bf16[8,256]{1,0:T(8,128)(2,1)} %shard_map.83) | data formatting | bytes 8192
  (39 shorter events, 1.4 us)
Async XLA Ops:
  0.0 46.0 %copy-start.2 = (bf16[8,256]{1,0:T(8,128)(2,1)S(1)}, bf16[8,256]{1,0:T(8,128)(2,1)}, u32[]{:S(2)}) copy-start(bf16[8,256]{1,0:T(8,128)(2,1)} %param.12) | copy-start | bytes 12292
  0.0 46.2 %copy-start.4 = (bf16[8,2,1,512,128]{4,3,2,1,0:T(8,128)(2,1)S(1)}, bf16[8,2,1,512,128]{4,3,2,1,0:T(8,128)(2,1)}, u32[]{:S(2)}) copy-start(bf16[8,2,1,512,128]{4,3,2,1,0:T(8,128)(2,1)} %param.14) | copy-start | bytes 6291460
  0.0 45.9 %copy-start.3 = (bf16[8,2,64]{2,1,0:T(2,128)(2,1)S(1)}, bf16[8,2,64]{2,1,0:T(2,128)(2,1)}, u32[]{:S(2)}) copy-start(bf16[8,2,64]{2,1,0:T(2,128)(2,1)} %param.13) | copy-start | bytes 6148
  46.2 3.3 %copy-start = (f32[8,4]{1,0:T(8,128)}, f32[8,4]{1,0:T(8,128)S(1)}, u32[]{:S(2)}) copy-start(f32[8,4]{1,0:T(8,128)S(1)} %get-tuple-element.29.hm_ref) | copy-start | bytes 388
  48.7 0.8 copy-start.1

commit v6 on v5

--- a/solution.py
+++ b/solution.py
@@ -132,11 +132,81 @@
     )(x)
 
 
-def final_kernel(n, n_tp, heads, slots, stat_row, partner_ref, back_ref, home_ref, hm_ref, hl_ref,
-                 fsel_ref, fwide_ref, w_ref, out_ref, got, part, held, send2, recv2, send3, recv3):
+def fanout(n, me, col, src, dst, send, recv):
+    def copy(k, peer, slot):
+        return pltpu.make_async_remote_copy(
+            src_ref=src,
+            dst_ref=dst.at[slot],
+            send_sem=send.at[k],
+            recv_sem=recv.at[k],
+            device_id=(peer, col),
+            device_id_type=MESH,
+        )
+
+    def start(k, carry):
+        copy(k, lax.rem(me + k, n), me).start()
+        return carry
+
+    lax.fori_loop(1, n, start, 0)
+
+    def finish():
+        def one(k, carry):
+            copy(k, lax.rem(me + k, n), me).wait_send()
+            source = lax.rem(me + n - k, n)
+            copy(k, source, source).wait_recv()
+            return carry
+
+        lax.fori_loop(1, n, one, 0)
+
+    return finish
+
+
+def attend_tile(wide, keys, values, count, fresh_k=None, fresh_v=None):
+    rows = wide.shape[0]
+    scores = lax.dot_general(
+        wide, keys, (((1,), (1,)), ((), ())), preferred_element_type=jnp.float32
+    ) * 0.125
+    half = rows // 2
+    row = lax.broadcasted_iota(jnp.int32, scores.shape, 0)
+    lane = lax.broadcasted_iota(jnp.int32, scores.shape, 1)
+    position = 2 * lane + jnp.where(row >= half, 1, 0)
+    inside = position.astype(jnp.float32) < count
+    top = jnp.max(jnp.where(inside, scores, -1e30), axis=1, keepdims=True)
+    top = jnp.maximum(top, pltpu.roll(top, half, 0))
+    if fresh_k is not None:
+        fresh_score = jnp.sum(
+            wide.astype(jnp.float32) * fresh_k.astype(jnp.float32), axis=1, keepdims=True
+        ) * 0.125
+        top = jnp.maximum(top, fresh_score)
+    weights = jnp.where(inside, jnp.exp(scores - top), 0.0).astype(jnp.bfloat16)
+    total = jnp.sum(weights.astype(jnp.float32), axis=1, keepdims=True)
+    total = total + pltpu.roll(total, half, 0)
+    both = jnp.dot(weights, values, preferred_element_type=jnp.float32)
+    mixed = both + pltpu.roll(pltpu.roll(both, half, 0), 64, 1)
+    if fresh_k is not None:
+        fresh_w = jnp.exp(fresh_score - top).astype(jnp.bfloat16).astype(jnp.float32)
+        total = total + fresh_w
+        mixed = mixed + fresh_w * fresh_v
+    return top, total, mixed
+
+
+def pair_rows(top, total, mixed, h):
+    lane = lax.broadcasted_iota(jnp.int32, (1, mixed.shape[1]), 1)
+    left = lane < 64
+    g = 2 * h
+    u = jnp.where(left, mixed[g : g + 1, :], mixed[g + 5 : g + 6, :])
+    m = jnp.where(left, top[g : g + 1, :], top[g + 1 : g + 2, :])
+    l = jnp.where(left, total[g : g + 1, :], total[g + 1 : g + 2, :])
+    return u, m, l
+
+
+def whole_kernel(n, n_tp, slots, partner_ref, sent_ref, home_wide_ref, home_cnt_ref, fresh_k_ref,
+                 fresh_v_ref, home_ref, help_ref, fsel_ref, w_ref, out_ref,
+                 got1, got2, back, stat, part, held, send1, recv1, send2, recv2, send3, recv3):
     me = lax.axis_index("grp")
     col = lax.axis_index("tp")
-    head_width = w_ref.shape[0] // heads
+    rows = home_wide_ref.shape[0]
+    pairs = w_ref.shape[0] // 128
     width = out_ref.shape[1]
 
     barrier = pltpu.get_barrier_semaphore()
@@ -152,90 +222,67 @@
         pl.semaphore_signal(barrier, inc=1, device_id=(me, peer), device_id_type=MESH)
     pl.semaphore_wait(barrier, (n - 1) + (n_tp - 1))
 
-    def copy_to(k):
-        peer = lax.rem(me + k, n)
-        return pltpu.make_async_remote_copy(
-            src_ref=back_ref,
-            dst_ref=got.at[me],
-            send_sem=send2.at[k],
-            recv_sem=recv2.at[k],
-            device_id=(peer, col),
-            device_id_type=MESH,
-        )
-
-    def copy_from(k):
-        source = lax.rem(me + n - k, n)
-        return pltpu.make_async_remote_copy(
-            src_ref=back_ref,
-            dst_ref=got.at[source],
-            send_sem=send2.at[k],
-            recv_sem=recv2.at[k],
-            device_id=(source, col),
-            device_id_type=MESH,
-        )
-
-    def start(k, carry):
-        copy_to(k).start()
-        return carry
-
-    lax.fori_loop(1, n, start, 0)
-
-    def finish(k, carry):
-        copy_to(k).wait_send()
-        copy_from(k).wait_recv()
-        return carry
-
-    lax.fori_loop(1, n, finish, 0)
-
-    block = got[partner_ref[0]].astype(jnp.float32)
+    wait1 = fanout(n, me, col, sent_ref, got1, send1, recv1)
+    for r in range(rows):
+        top, total, mixed = attend_tile(
+            home_wide_ref[r],
+            home_ref[r, 0, 0],
+            home_ref[r, 1, 0],
+            home_cnt_ref[r : r + 1, 0:1],
+            fresh_k_ref[r : r + 1, :],
+            fresh_v_ref[r : r + 1, :],
+        )
+        for h in range(pairs):
+            u, m, l = pair_rows(top, total, mixed, h)
+            stat[0, h, r : r + 1, :] = u
+            stat[1, h, r : r + 1, :] = m
+            stat[2, h, r : r + 1, :] = l
+    wait1()
+
+    block = got1[partner_ref[0]]
+    code = block[8 * slots : 8 * slots + 1, :].astype(jnp.float32)
+    for k in range(slots):
+        count = code[:, k : k + 1] * 32.0 + code[:, slots + k : slots + k + 1]
+        top, total, mixed = attend_tile(
+            block[8 * k : 8 * k + 8, :], help_ref[k, 0, 0], help_ref[k, 1, 0], count
+        )
+        for h in range(pairs):
+            u, m, l = pair_rows(top, total, mixed, h)
+            back[k * pairs + h : k * pairs + h + 1, :] = u
+            back[(slots + k) * pairs + h : (slots + k) * pairs + h + 1, :] = m
+            back[(2 * slots + k) * pairs + h : (2 * slots + k) * pairs + h + 1, :] = l
+
+    wait2 = fanout(n, me, col, back, got2, send2, recv2)
+    wait2()
+
+    theirs = got2[partner_ref[0]]
     fsel = fsel_ref[...]
-    wide = fwide_ref[...]
-    stats = block[stat_row : stat_row + 1, :]
-    n_st = slots * heads
-
-    def parts(base):
-        return (
-            stats[:, base : base + n_st]
-            + stats[:, base + n_st : base + 2 * n_st]
-            + stats[:, base + 2 * n_st : base + 3 * n_st]
-        )
-
-    def per_head(x):
-        y = x[:, 0:heads]
-        for k in range(1, slots):
-            y = y + x[:, k * heads : (k + 1) * heads]
-        return y
-
-    has = per_head(wide)[:, 0:1] * 0.0
-    for k in range(slots):
+    has = fsel[:, 0:1]
+    for k in range(1, slots):
         has = has + fsel[:, k : k + 1]
-    far_m = jnp.where(has > 0.0, per_head(wide * parts(0)), -1e30)
-    far_l = per_head(wide * parts(3 * n_st))
-    home_m_all = hm_ref[...]
-    home_l_all = hl_ref[...]
-    lane = lax.broadcasted_iota(jnp.int32, (fsel.shape[0], 2 * head_width), 1)
-    left = lane < head_width
-
-    def spread(x, h):
-        return jnp.where(left, x[:, 2 * h : 2 * h + 1], x[:, 2 * h + 1 : 2 * h + 2])
-
     acc = jnp.zeros(part.shape, jnp.float32)
-    for h in range(heads // 2):
-        far = fsel[:, 0:1] * block[h : h + 1, :]
-        for k in range(1, slots):
-            far = far + fsel[:, k : k + 1] * block[2 * k + h : 2 * k + h + 1, :]
-        home = home_ref[h]
-        home_m = spread(home_m_all, h)
-        home_l = spread(home_l_all, h)
-        fm = spread(far_m, h)
-        fl = spread(far_l, h)
-        top = jnp.maximum(home_m, fm)
+    for h in range(pairs):
+
+        def pick(base):
+            x = fsel[:, 0:1] * theirs[base + h : base + h + 1, :]
+            for k in range(1, slots):
+                r0 = base + k * pairs + h
+                x = x + fsel[:, k : k + 1] * theirs[r0 : r0 + 1, :]
+            return x
+
+        far_u = pick(0)
+        far_m = jnp.where(has > 0.0, pick(slots * pairs), -1e30)
+        far_l = pick(2 * slots * pairs)
+        home_u = stat[0, h]
+        home_m = stat[1, h]
+        home_l = stat[2, h]
+        top = jnp.maximum(home_m, far_m)
         home_e = jnp.exp(home_m - top)
-        far_e = jnp.exp(fm - top)
-        mix = (home * home_e + far * far_e) / (home_l * home_e + fl * far_e)
+        far_e = jnp.exp(far_m - top)
+        mix = (home_u * home_e + far_u * far_e) / (home_l * home_e + far_l * far_e)
         acc = acc + jnp.dot(
             mix.astype(jnp.bfloat16),
-            w_ref[h * 2 * head_width : (h + 1) * 2 * head_width, :],
+            w_ref[h * 128 : (h + 1) * 128, :],
             preferred_element_type=jnp.float32,
         )
     part[...] = acc
@@ -264,52 +311,21 @@
     out_ref[...] = total.astype(out_ref.dtype)
 
 
-def finish_call(n, n_tp, heads, slots, stat_row, partner, back, home, home_m, home_l, fsel, fwide,
-                out_weight, cid):
-    rows = home.shape[1]
-    width = out_weight.shape[1] // n_tp
-    vmem = pl.BlockSpec(memory_space=pltpu.VMEM)
-    return pl.pallas_call(
-        functools.partial(final_kernel, n, n_tp, heads, slots, stat_row),
-        out_shape=jax.ShapeDtypeStruct((rows, width), jnp.bfloat16),
-        in_specs=[pl.BlockSpec(memory_space=pltpu.SMEM)] + [vmem] * 7,
-        out_specs=vmem,
-        scratch_shapes=[
-            pltpu.VMEM((n,) + back.shape, back.dtype),
-            pltpu.VMEM((rows, out_weight.shape[1]), jnp.float32),
-            pltpu.VMEM((n_tp, rows, width), jnp.float32),
-            pltpu.SemaphoreType.DMA((n,)),
-            pltpu.SemaphoreType.DMA((n,)),
-            pltpu.SemaphoreType.DMA((n_tp,)),
-            pltpu.SemaphoreType.DMA((n_tp,)),
-        ],
-        compiler_params=pltpu.CompilerParams(collective_id=cid, has_side_effects=True),
-    )(partner, back, home, home_m, home_l, fsel, fwide, out_weight)
-
-
-def three_way(x):
-    hi = x.astype(jnp.bfloat16)
-    rest = x - hi.astype(jnp.float32)
-    mid = rest.astype(jnp.bfloat16)
-    lo = (rest - mid.astype(jnp.float32)).astype(jnp.bfloat16)
-    return [hi, mid, lo]
-
-
-def tile(rows_of, extra):
-    lanes = rows_of.shape[1]
-    rows = rows_of.shape[0]
-    stat = jnp.zeros((1, lanes), jnp.bfloat16).at[0, : extra.shape[0]].set(extra)
-    pad = jnp.zeros((16 - rows - 1, lanes), jnp.bfloat16)
-    return jnp.concatenate([rows_of, stat, pad], axis=0)
-
-
 def per_device(ny, nz, queries, new_kv, home_cache, help_cache, lengths, split_at, helper_req, out_weight):
     n_grp = lax.axis_size("grp")
     n_tp = lax.axis_size("tp")
     row_count, width = queries.shape
     slots = help_cache.shape[0]
     heads = width // 64
+    pairs = heads // 2
     lanes = 128
+
+    def widen(q):
+        q = q.reshape(q.shape[0], heads, 64)
+        blank = jnp.zeros_like(q)
+        return jnp.concatenate(
+            [jnp.concatenate([q, blank], -1), jnp.concatenate([blank, q], -1)], axis=1
+        )
 
     is_long = lengths > LONG_AT
     before = jnp.arange(row_count)[None, :] < jnp.arange(row_count)[:, None]
@@ -319,31 +335,42 @@
         pick.astype(jnp.bfloat16), queries, preferred_element_type=jnp.float32
     ).astype(jnp.bfloat16)
     long_count = jnp.sum(jnp.where(pick, (lengths - split_at)[None, :], 0), axis=1)
-    counts = jnp.concatenate([long_count // 32, long_count % 32]).astype(jnp.bfloat16)
-    stat_row = slots * width // lanes
-    sent = tile(long_q.reshape(stat_row, lanes), counts)
-
-    partner = helper_req[0] // row_count
-    got = gather_grp(sent, n_grp, 0)
-    mine = lax.dynamic_index_in_dim(got, partner, axis=0, keepdims=False)
-    help_queries = mine[:stat_row].reshape(slots, width)
-    code = mine[stat_row].astype(jnp.int32)
-    help_count = code[:slots] * 32 + code[slots : 2 * slots]
-    help_m, help_l, help_u = attend(help_queries, help_cache, help_count, None)
-    stat_parts = three_way(help_m.reshape(-1)) + three_way(help_l.reshape(-1))
-    back = tile(
-        help_u.astype(jnp.bfloat16).reshape(stat_row, lanes), jnp.concatenate(stat_parts)
-    )
-
-    home_m, home_l, home_u = attend(queries, home_cache, split_at, new_kv)
-    home = home_u.reshape(row_count, heads // 2, lanes).transpose(1, 0, 2)
+    code = jnp.zeros((16, lanes), jnp.bfloat16)
+    code = code.at[0, :slots].set((long_count // 32).astype(jnp.bfloat16))
+    code = code.at[0, slots : 2 * slots].set((long_count % 32).astype(jnp.bfloat16))
+    sent = jnp.concatenate([widen(long_q).reshape(slots * 2 * heads, lanes), code], axis=0)
+
+    home_wide = widen(queries)
+    home_cnt = jnp.broadcast_to(split_at.astype(jnp.float32)[:, None], (row_count, lanes))
+    fresh_k = jnp.concatenate([new_kv[:, 0], new_kv[:, 0]], axis=-1)
+    fresh_v = jnp.concatenate([new_kv[:, 1], new_kv[:, 1]], axis=-1).astype(jnp.float32)
     fsel = (is_long[:, None] & (rank[:, None] == jnp.arange(slots)[None, :])).astype(jnp.float32)
-    fwide = jnp.repeat(fsel, heads, axis=1)
-    partner_arr = (helper_req[:1] // row_count).astype(jnp.int32)
-    return finish_call(
-        n_grp, n_tp, heads, slots, stat_row, partner_arr, back, home, home_m, home_l, fsel, fwide,
-        out_weight, 1,
-    )
+    partner = (helper_req[:1] // row_count).astype(jnp.int32)
+
+    out_cols = out_weight.shape[1] // n_tp
+    vmem = pl.BlockSpec(memory_space=pltpu.VMEM)
+    back_rows = 3 * slots * pairs
+    return pl.pallas_call(
+        functools.partial(whole_kernel, n_grp, n_tp, slots),
+        out_shape=jax.ShapeDtypeStruct((row_count, out_cols), jnp.bfloat16),
+        in_specs=[pl.BlockSpec(memory_space=pltpu.SMEM)] + [vmem] * 9,
+        out_specs=vmem,
+        scratch_shapes=[
+            pltpu.VMEM((n_grp,) + sent.shape, jnp.bfloat16),
+            pltpu.VMEM((n_grp, back_rows, lanes), jnp.float32),
+            pltpu.VMEM((back_rows, lanes), jnp.float32),
+            pltpu.VMEM((3, pairs, row_count, lanes), jnp.float32),
+            pltpu.VMEM((row_count, out_weight.shape[1]), jnp.float32),
+            pltpu.VMEM((n_tp, row_count, out_cols), jnp.float32),
+            pltpu.SemaphoreType.DMA((n_grp,)),
+            pltpu.SemaphoreType.DMA((n_grp,)),
+            pltpu.SemaphoreType.DMA((n_grp,)),
+            pltpu.SemaphoreType.DMA((n_grp,)),
+            pltpu.SemaphoreType.DMA((n_tp,)),
+            pltpu.SemaphoreType.DMA((n_tp,)),
+        ],
+        compiler_params=pltpu.CompilerParams(collective_id=0, has_side_effects=True),
+    )(partner, sent, home_wide, home_cnt, fresh_k, fresh_v, home_cache, help_cache, fsel, out_weight)
 
 
 def grp_rows(mesh):

time: 78.3 us -> 89.1 us (1.14)
  Pallas kernels: 53.3 us -> 71.1 us
  matrix products: 5.65 us -> 0.81 us
  between operations: 5.48 us -> 2.65 us
    pallas_call x2 -> x1, Pallas kernels: 53.3 us -> 71.1 us  [per_device(): pl.pallas_call(functools.partial(whole_kernel, n_grp, n_tp, slots), out_s...]
    dot_general x5 -> x0, matrix products: 4.85 us -> none  [the longest x2 3.09 us: attend(): jnp.einsum('nkgjc,nkpc->nkgjp', wide_rows, key_rows, preferred_element_ty...]
    scatter x0 -> x2, local copies, waits for them, and re-layouts: none -> 1.52 us  [the longest x1 1.52 us: per_device(): code.at[0, slots:2 * slots].set((long_count % 32).astype(jnp.bfloat16))]
    reshape x4 -> x2, local copies, waits for them, and re-layouts: 2.12 us -> 0.85 us  [widen(): q = q.reshape(q.shape[0], heads, 64)]
    another operation x3, other arithmetic: 2.05 us -> 3.28 us
    concatenate x5 -> x3, other arithmetic: 1.37 us -> 1.94 us  [the longest x1 0.68 us: widen(): jnp.concatenate([jnp.concatenate([q, blank], -1), jnp.concatenate([blank,...]
where the time goes in v6:
time: 89.1 us; the launch traced here: 88.6 us
  Pallas kernels  71.1 us (80%)
  other arithmetic  8.27 us (9%)
  local copies, waits for them, and re-layouts  5.75 us (6%)
  between operations  2.65 us (3%)
    pallas_call x1, Pallas kernels, per_device(): pl.pallas_call(functools.partial(whole_kernel, n_grp, n_tp, slots), out_s...  71.1 us
    another operation x3, other arithmetic  3.28 us

profile of v6, /device:TPU:1, one launch (start us, length us, event | category | flops | bytes accessed | tf_op | source)
XLA Modules:
  0.0 88.6 jit_solution(9319933766017573543)
XLA Ops:
  2.6 0.7 fusion.17
  3.3 0.7 broadcast_compare_fusion
  4.0 0.1 convert_reduce_fusion
  4.1 0.1 select_reduce_fusion
  4.3 1.3 %and_reduce_fusion = pred[]{:T(512)} fusion(s32[2]{0:T(128)} %constant.104.clone.1), kind=kLoop, calls=%fused_computation.27 | loop fusion | flops 9 | bytes 9 | tf_op jit(solution)/shard_map/reduce.3
  5.6 0.7 fusion.18
  6.2 2.0 %broadcast_select_fusion = bf16[1,4]{1,0:T(2,128)(2,1)S(1)} fusion(pred[]{:T(512)} %and_reduce_fusion, s32[]{:T(128)} %bitcast.2, s32[]{:T(128)} %bitcast.3, bf16[1,4]{1,0:T(2,128)(2,1)S(1)} %fusion.15, s32[4]{0:T(128)S(1)} %select_reduce_fusion), kind=kLoop, calls=%fused_computation.34 | loop fusion | flops 52 | bytes 41 | tf_op jit(solution)/shard_map/select.3
  8.2 1.5 %scatter.9 = bf16[16,128]{1,0:T(8,128)(2,1)S(1)} dynamic-update-slice(bf16[16,128]{1,0:T(8,128)(2,1)S(1)} %scatter.6, bf16[1,4]{1,0:T(2,128)(2,1)S(1)} %broadcast_select_fusion, s32[]{:T(128)} %bitcast.2, s32[]{:T(128)} %bitcast.3) | dynamic-update-slice | bytes 20 | tf_op jit(solution)/shard_map/scatter | solution.py:340
  9.7 0.8 convolution_convert_fusion
  10.5 0.1 reshape.126
  10.6 0.1 fusion.6
  10.7 0.6 pad_maximum_fusion.sent_ref
  11.3 0.8 reshape.130
  12.1 0.7 fusion.2.home_wide_ref
  12.8 0.7 broadcast_in_dim.30.home_cnt_ref
  13.4 0.8 fusion.16
  14.2 0.6 pad_maximum_fusion.1.fresh_k_ref
  14.9 0.7 maximum_convert_fusion.fresh_v_ref
  15.5 0.7 fusion.9.fsel_ref
  16.2 71.1 %shard_map.82 = bf16[8,256]{1,0:T(8,128)(2,1)} custom-call(s32[1]{0:T(128)S(6)} %select_n.35.partner_ref, bf16[48,128]{1,0:T(8,128)(2,1)} %pad_maximum_fusion.sent_ref, bf16[8,8,128]{2,1,0:T(8,128)(2,1)} %fusion.2.home_wide_ref, f32[8,128]{1,0:T(8,128)} %broadcast_in_dim.30.home_cnt_ref, bf16[8,128]{1,0:T(8,128)(2,1)} %pad_maximum_fusion.1.fresh_k_ref, ...), custom_call_target="tpu_custom_call" | custom-call | tf_op jit(solution)/shard_map/pallas_call | solution.py:353
  87.3 1.3 %copy.19 = bf16[8,256]{1,0:T(8,128)(2,1)} copy(bf16[8,256]{1,0:T(8,128)(2,1)} %shard_map.82) | data formatting | bytes 8192
  (4 shorter events, 0.0 us)

commit v7 on v6

--- a/solution.py
+++ b/solution.py
@@ -200,12 +200,29 @@
     return u, m, l
 
 
-def whole_kernel(n, n_tp, slots, partner_ref, sent_ref, home_wide_ref, home_cnt_ref, fresh_k_ref,
-                 fresh_v_ref, home_ref, help_ref, fsel_ref, w_ref, out_ref,
+def widen(q, heads):
+    lane = lax.broadcasted_iota(jnp.int32, (2 * heads, 128), 1)
+    row = lax.broadcasted_iota(jnp.int32, (2 * heads, 128), 0)
+    low = lane < 64
+    wide = jnp.zeros((2 * heads, 128), jnp.float32)
+    for h in range(heads // 2):
+        a = q[:, h * 128 : (h + 1) * 128]
+        turned = pltpu.roll(a, 64, 1)
+        g = 2 * h
+        wide = jnp.where((row == g) & low, a, wide)
+        wide = jnp.where((row == g + 1) & low, turned, wide)
+        wide = jnp.where((row == heads + g) & ~low, turned, wide)
+        wide = jnp.where((row == heads + g + 1) & ~low, a, wide)
+    return wide.astype(jnp.bfloat16)
+
+
+def whole_kernel(n, n_tp, slots, lengths_ref, splits_ref, helpers_ref, sent_ref, queries_ref,
+                 kv_ref, home_ref, help_ref, w_ref, out_ref,
                  got1, got2, back, stat, part, held, send1, recv1, send2, recv2, send3, recv3):
     me = lax.axis_index("grp")
     col = lax.axis_index("tp")
-    rows = home_wide_ref.shape[0]
+    rows = queries_ref.shape[0]
+    heads = queries_ref.shape[1] // 64
     pairs = w_ref.shape[0] // 128
     width = out_ref.shape[1]
 
@@ -223,14 +240,21 @@
     pl.semaphore_wait(barrier, (n - 1) + (n_tp - 1))
 
     wait1 = fanout(n, me, col, sent_ref, got1, send1, recv1)
+    lane = lax.broadcasted_iota(jnp.int32, (1, 128), 1)
+    low = lane < 64
     for r in range(rows):
+        kv = kv_ref[r : r + 1, :].astype(jnp.float32)
+        turned = pltpu.roll(kv, 64, 1)
+        fresh_k = jnp.where(low, kv, turned).astype(jnp.bfloat16)
+        fresh_v = jnp.where(low, turned, kv)
+        count = splits_ref[r].astype(jnp.float32)
         top, total, mixed = attend_tile(
-            home_wide_ref[r],
+            widen(queries_ref[r : r + 1, :].astype(jnp.float32), heads),
             home_ref[r, 0, 0],
             home_ref[r, 1, 0],
-            home_cnt_ref[r : r + 1, 0:1],
-            fresh_k_ref[r : r + 1, :],
-            fresh_v_ref[r : r + 1, :],
+            count,
+            fresh_k,
+            fresh_v,
         )
         for h in range(pairs):
             u, m, l = pair_rows(top, total, mixed, h)
@@ -239,12 +263,19 @@
             stat[2, h, r : r + 1, :] = l
     wait1()
 
-    block = got1[partner_ref[0]]
-    code = block[8 * slots : 8 * slots + 1, :].astype(jnp.float32)
+    partner = helpers_ref[0] // rows
+    block = got1[partner]
+    pick_row = lax.broadcasted_iota(jnp.int32, (slots, rows), 0)
+    pick_col = lax.broadcasted_iota(jnp.int32, (slots, rows), 1)
+    pick = jnp.zeros((slots, rows), jnp.float32)
     for k in range(slots):
-        count = code[:, k : k + 1] * 32.0 + code[:, slots + k : slots + k + 1]
+        pick = jnp.where((pick_row == k) & (pick_col == helpers_ref[k] % rows), 1.0, pick)
+    chosen = jnp.dot(pick.astype(jnp.bfloat16), block, preferred_element_type=jnp.float32)
+    qw = heads * 64
+    for k in range(slots):
+        count = chosen[k : k + 1, qw : qw + 1] * 32.0 + chosen[k : k + 1, qw + 1 : qw + 2]
         top, total, mixed = attend_tile(
-            block[8 * k : 8 * k + 8, :], help_ref[k, 0, 0], help_ref[k, 1, 0], count
+            widen(chosen[k : k + 1, :qw], heads), help_ref[k, 0, 0], help_ref[k, 1, 0], count
         )
         for h in range(pairs):
             u, m, l = pair_rows(top, total, mixed, h)
@@ -253,26 +284,34 @@
             back[(2 * slots + k) * pairs + h : (2 * slots + k) * pairs + h + 1, :] = l
 
     wait2 = fanout(n, me, col, back, got2, send2, recv2)
-    wait2()
-
-    theirs = got2[partner_ref[0]]
-    fsel = fsel_ref[...]
+
+    sel_row = lax.broadcasted_iota(jnp.int32, (rows, slots), 0)
+    sel_col = lax.broadcasted_iota(jnp.int32, (rows, slots), 1)
+    fsel = jnp.zeros((rows, slots), jnp.float32)
+    rank = jnp.int32(0)
+    for r in range(rows):
+        is_long = lengths_ref[r] > LONG_AT
+        fsel = jnp.where((sel_row == r) & (sel_col == rank) & is_long, 1.0, fsel)
+        rank = rank + is_long.astype(jnp.int32)
     has = fsel[:, 0:1]
     for k in range(1, slots):
         has = has + fsel[:, k : k + 1]
+    wait2()
+
+    theirs = got2[partner]
     acc = jnp.zeros(part.shape, jnp.float32)
     for h in range(pairs):
 
-        def pick(base):
+        def pick_far(base):
             x = fsel[:, 0:1] * theirs[base + h : base + h + 1, :]
             for k in range(1, slots):
                 r0 = base + k * pairs + h
                 x = x + fsel[:, k : k + 1] * theirs[r0 : r0 + 1, :]
             return x
 
-        far_u = pick(0)
-        far_m = jnp.where(has > 0.0, pick(slots * pairs), -1e30)
-        far_l = pick(2 * slots * pairs)
+        far_u = pick_far(0)
+        far_m = jnp.where(has > 0.0, pick_far(slots * pairs), -1e30)
+        far_l = pick_far(2 * slots * pairs)
         home_u = stat[0, h]
         home_m = stat[1, h]
         home_l = stat[2, h]
@@ -316,44 +355,25 @@
     n_tp = lax.axis_size("tp")
     row_count, width = queries.shape
     slots = help_cache.shape[0]
-    heads = width // 64
-    pairs = heads // 2
+    pairs = width // 128
     lanes = 128
 
-    def widen(q):
-        q = q.reshape(q.shape[0], heads, 64)
-        blank = jnp.zeros_like(q)
-        return jnp.concatenate(
-            [jnp.concatenate([q, blank], -1), jnp.concatenate([blank, q], -1)], axis=1
-        )
-
-    is_long = lengths > LONG_AT
-    before = jnp.arange(row_count)[None, :] < jnp.arange(row_count)[:, None]
-    rank = jnp.sum(jnp.where(before, is_long[None, :], False), axis=1)
-    pick = is_long[None, :] & (rank[None, :] == jnp.arange(slots)[:, None])
-    long_q = jnp.dot(
-        pick.astype(jnp.bfloat16), queries, preferred_element_type=jnp.float32
+    count = lengths - split_at
+    lane = jnp.arange(lanes)[None, :]
+    code = jnp.where(
+        lane == 0, (count // 32)[:, None], jnp.where(lane == 1, (count % 32)[:, None], 0)
     ).astype(jnp.bfloat16)
-    long_count = jnp.sum(jnp.where(pick, (lengths - split_at)[None, :], 0), axis=1)
-    code = jnp.zeros((16, lanes), jnp.bfloat16)
-    code = code.at[0, :slots].set((long_count // 32).astype(jnp.bfloat16))
-    code = code.at[0, slots : 2 * slots].set((long_count % 32).astype(jnp.bfloat16))
-    sent = jnp.concatenate([widen(long_q).reshape(slots * 2 * heads, lanes), code], axis=0)
-
-    home_wide = widen(queries)
-    home_cnt = jnp.broadcast_to(split_at.astype(jnp.float32)[:, None], (row_count, lanes))
-    fresh_k = jnp.concatenate([new_kv[:, 0], new_kv[:, 0]], axis=-1)
-    fresh_v = jnp.concatenate([new_kv[:, 1], new_kv[:, 1]], axis=-1).astype(jnp.float32)
-    fsel = (is_long[:, None] & (rank[:, None] == jnp.arange(slots)[None, :])).astype(jnp.float32)
-    partner = (helper_req[:1] // row_count).astype(jnp.int32)
+    sent = jnp.concatenate([queries, code], axis=1)
+    kv = new_kv.reshape(row_count, 2 * new_kv.shape[2])
 
     out_cols = out_weight.shape[1] // n_tp
     vmem = pl.BlockSpec(memory_space=pltpu.VMEM)
+    smem = pl.BlockSpec(memory_space=pltpu.SMEM)
     back_rows = 3 * slots * pairs
     return pl.pallas_call(
         functools.partial(whole_kernel, n_grp, n_tp, slots),
         out_shape=jax.ShapeDtypeStruct((row_count, out_cols), jnp.bfloat16),
-        in_specs=[pl.BlockSpec(memory_space=pltpu.SMEM)] + [vmem] * 9,
+        in_specs=[smem] * 3 + [vmem] * 6,
         out_specs=vmem,
         scratch_shapes=[
             pltpu.VMEM((n_grp,) + sent.shape, jnp.bfloat16),
@@ -370,7 +390,7 @@
             pltpu.SemaphoreType.DMA((n_tp,)),
         ],
         compiler_params=pltpu.CompilerParams(collective_id=0, has_side_effects=True),
-    )(partner, sent, home_wide, home_cnt, fresh_k, fresh_v, home_cache, help_cache, fsel, out_weight)
+    )(lengths, split_at, helper_req, sent, queries, kv, home_cache, help_cache, out_weight)
 
 
 def grp_rows(mesh):

time: 89.1 us -> 67.9 us (0.76)
  Pallas kernels: 71.1 us -> 63 us
  other arithmetic: 8.27 us -> 2.04 us
  local copies, waits for them, and re-layouts: 5.75 us -> 2.62 us
  between operations: 2.65 us -> 0.02 us
    pallas_call x1, Pallas kernels: 71.1 us -> 63 us  [per_device(): pl.pallas_call(functools.partial(whole_kernel, n_grp, n_tp, slots), out_s...]
    another operation x3 -> x0, other arithmetic: 3.28 us -> none
    convert_element_type x4 -> x1, other arithmetic: 2.07 us -> 0.08 us  [per_device(): code = jnp.where(lane == 0, (count // 32)[:, None], jnp.where(lane == 1,...]
    scatter x2 -> x0, local copies, waits for them, and re-layouts: 1.52 us -> none  [the longest x1 1.52 us: per_device(): code.at[0, slots:2 * slots].set((long_count % 32).astype(jnp.bfloat16))]
    concatenate x3 -> x1, other arithmetic: 1.94 us -> 1.27 us  [per_device(): sent = jnp.concatenate([queries, code], axis=1)]
where the time goes in v7:
time: 67.9 us; the launch traced here: 67.7 us
  Pallas kernels  63 us (93%)
  local copies, waits for them, and re-layouts  2.62 us (4%)
  other arithmetic  2.04 us (3%)
    pallas_call x1, Pallas kernels, per_device(): pl.pallas_call(functools.partial(whole_kernel, n_grp, n_tp, slots), out_s...  63 us

profile of v7, /device:TPU:1, one launch (start us, length us, event | category | flops | bytes accessed | tf_op | source)
XLA Modules:
  0.0 67.7 jit_solution(6379506372138735499)
XLA Ops:
  0.0 0.7 %and_select_fusion.1 = (s32[8]{0:T(128)S(1)}, s32[8]{0:T(128)S(1)}) fusion(s32[8]{0:T(128)} %lengths_ref.1, s32[8]{0:T(128)} %splits_ref.1), kind=kLoop, calls=%fused_computation.3 | loop fusion | flops 128 | bytes 128 | tf_op jit(solution)/shard_map/jit(floor_divide)/jit(_where)/select_n | solution.py:364
  0.7 0.1 select_convert_fusion
  0.8 1.3 %reshape.15.kv_ref = bf16[8,128]{1,0:T(8,128)(2,1)} reshape(bf16[8,2,64]{2,1,0:T(2,128)(2,1)} %param.9) | data formatting | bytes 4096 | tf_op jit(solution)/shard_map/reshape | solution.py:367
  2.1 1.3 %pad_maximum_fusion.sent_ref = bf16[8,384]{1,0:T(8,128)(2,1)} fusion(bf16[8,128]{1,0:T(8,128)(2,1)S(1)} %select_convert_fusion, bf16[8,256]{1,0:T(8,128)(2,1)} %queries_ref.1), kind=kLoop, calls=%fused_computation | loop fusion | flops 12288 | bytes 12288 | tf_op jit(solution)/shard_map/concatenate | solution.py:366
  3.4 63.0 %shard_map.82 = bf16[8,256]{1,0:T(8,128)(2,1)} custom-call(s32[8]{0:T(128)} %lengths_ref.1, s32[8]{0:T(128)} %splits_ref.1, s32[4]{0:T(128)} %helpers_ref.1, bf16[8,384]{1,0:T(8,128)(2,1)} %pad_maximum_fusion.sent_ref, bf16[8,256]{1,0:T(8,128)(2,1)} %queries_ref.1, bf16[8,128]{1,0:T(8,128)(2,1)} %reshape.15.kv_ref, bf16[8,2,1,512,128]{4,3,2,1,0:T(8,128)(2,1)} %home_ref.1, ...), custom_call_target="tpu_custom_call" | custom-call | tf_op jit(solution)/shard_map/pallas_call | solution.py:373
  66.4 1.3 %copy.10 = bf16[8,256]{1,0:T(8,128)(2,1)} copy(bf16[8,256]{1,0:T(8,128)(2,1)} %shard_map.82) | data formatting | bytes 8192
  (2 shorter events, 0.0 us)

commit v8 on v7

--- a/solution.py
+++ b/solution.py
@@ -132,7 +132,15 @@
     )(x)
 
 
-def fanout(n, me, col, src, dst, send, recv):
+def far_first(i, size):
+    half = size // 2
+    return jnp.where(i % 2 == 0, half + i // 2, half - (i + 1) // 2)
+
+
+def fanout(ny, nz, me, col, src, dst, send, recv):
+    my_y = me // nz
+    my_z = me % nz
+
     def copy(k, peer, slot):
         return pltpu.make_async_remote_copy(
             src_ref=src,
@@ -143,20 +151,33 @@
             device_id_type=MESH,
         )
 
+    def offsets(k):
+        return far_first(k // nz, ny), far_first(k % nz, nz)
+
+    def to(k):
+        dy, dz = offsets(k)
+        return lax.rem(my_y + dy, ny) * nz + lax.rem(my_z + dz, nz)
+
+    def source(k):
+        dy, dz = offsets(k)
+        return lax.rem(my_y + ny - dy, ny) * nz + lax.rem(my_z + nz - dz, nz)
+
+    last = ny * nz - 1
+
     def start(k, carry):
-        copy(k, lax.rem(me + k, n), me).start()
+        copy(k, to(k), me).start()
         return carry
 
-    lax.fori_loop(1, n, start, 0)
+    lax.fori_loop(0, last, start, 0)
 
     def finish():
         def one(k, carry):
-            copy(k, lax.rem(me + k, n), me).wait_send()
-            source = lax.rem(me + n - k, n)
-            copy(k, source, source).wait_recv()
+            copy(k, to(k), me).wait_send()
+            s = source(k)
+            copy(k, s, s).wait_recv()
             return carry
 
-        lax.fori_loop(1, n, one, 0)
+        lax.fori_loop(0, last, one, 0)
 
     return finish
 
@@ -216,9 +237,10 @@
     return wide.astype(jnp.bfloat16)
 
 
-def whole_kernel(n, n_tp, slots, lengths_ref, splits_ref, helpers_ref, sent_ref, queries_ref,
-                 kv_ref, home_ref, help_ref, w_ref, out_ref,
+def whole_kernel(ny, nz, n_tp, slots, lengths_ref, splits_ref, helpers_ref, sent_ref, queries_ref,
+                 kv_ref, home_hbm, help_hbm, w_hbm, out_ref, home_ref, help_ref, w_ref, local,
                  got1, got2, back, stat, part, held, send1, recv1, send2, recv2, send3, recv3):
+    n = ny * nz
     me = lax.axis_index("grp")
     col = lax.axis_index("tp")
     rows = queries_ref.shape[0]
@@ -237,11 +259,20 @@
     for k in range(1, n_tp):
         peer = lax.rem(col + k, n_tp)
         pl.semaphore_signal(barrier, inc=1, device_id=(me, peer), device_id_type=MESH)
+    loads = [
+        pltpu.make_async_copy(hbm, vmem, local.at[i])
+        for i, (hbm, vmem) in enumerate(
+            [(home_hbm, home_ref), (help_hbm, help_ref), (w_hbm, w_ref)]
+        )
+    ]
+    for load in loads:
+        load.start()
     pl.semaphore_wait(barrier, (n - 1) + (n_tp - 1))
 
-    wait1 = fanout(n, me, col, sent_ref, got1, send1, recv1)
+    wait1 = fanout(ny, nz, me, col, sent_ref, got1, send1, recv1)
     lane = lax.broadcasted_iota(jnp.int32, (1, 128), 1)
     low = lane < 64
+    loads[0].wait()
     for r in range(rows):
         kv = kv_ref[r : r + 1, :].astype(jnp.float32)
         turned = pltpu.roll(kv, 64, 1)
@@ -262,6 +293,7 @@
             stat[1, h, r : r + 1, :] = m
             stat[2, h, r : r + 1, :] = l
     wait1()
+    loads[1].wait()
 
     partner = helpers_ref[0] // rows
     block = got1[partner]
@@ -283,7 +315,7 @@
             back[(slots + k) * pairs + h : (slots + k) * pairs + h + 1, :] = m
             back[(2 * slots + k) * pairs + h : (2 * slots + k) * pairs + h + 1, :] = l
 
-    wait2 = fanout(n, me, col, back, got2, send2, recv2)
+    wait2 = fanout(ny, nz, me, col, back, got2, send2, recv2)
 
     sel_row = lax.broadcasted_iota(jnp.int32, (rows, slots), 0)
     sel_col = lax.broadcasted_iota(jnp.int32, (rows, slots), 1)
@@ -298,6 +330,7 @@
         has = has + fsel[:, k : k + 1]
     wait2()
 
+    loads[2].wait()
     theirs = got2[partner]
     acc = jnp.zeros(part.shape, jnp.float32)
     for h in range(pairs):
@@ -371,11 +404,15 @@
     smem = pl.BlockSpec(memory_space=pltpu.SMEM)
     back_rows = 3 * slots * pairs
     return pl.pallas_call(
-        functools.partial(whole_kernel, n_grp, n_tp, slots),
+        functools.partial(whole_kernel, ny, nz, n_tp, slots),
         out_shape=jax.ShapeDtypeStruct((row_count, out_cols), jnp.bfloat16),
-        in_specs=[smem] * 3 + [vmem] * 6,
+        in_specs=[smem] * 3 + [vmem] * 3 + [pl.BlockSpec(memory_space=pl.ANY)] * 3,
         out_specs=vmem,
         scratch_shapes=[
+            pltpu.VMEM(home_cache.shape, home_cache.dtype),
+            pltpu.VMEM(help_cache.shape, help_cache.dtype),
+            pltpu.VMEM(out_weight.shape, out_weight.dtype),
+            pltpu.SemaphoreType.DMA((3,)),
             pltpu.VMEM((n_grp,) + sent.shape, jnp.bfloat16),
             pltpu.VMEM((n_grp, back_rows, lanes), jnp.float32),
             pltpu.VMEM((back_rows, lanes), jnp.float32),

time: 67.9 us -> 65.7 us (0.968)
  Pallas kernels: 63 us -> 60.7 us
    pallas_call x1, Pallas kernels: 63 us -> 60.7 us  [per_device(): pl.pallas_call(functools.partial(whole_kernel, ny, nz, n_tp, slots), out_...]
where the time goes in v8:
time: 65.7 us; the launch traced here: 65.4 us
  Pallas kernels  60.7 us (92%)
  local copies, waits for them, and re-layouts  2.62 us (4%)
  other arithmetic  2.04 us (3%)
    pallas_call x1, Pallas kernels, per_device(): pl.pallas_call(functools.partial(whole_kernel, ny, nz, n_tp, slots), out_...  60.7 us
    reshape x1, local copies, waits for them, and re-layouts, per_device(): kv = new_kv.reshape(row_count, 2 * new_kv.shape[2])  1.35 us

profile of v8, /device:TPU:1, one launch (start us, length us, event | category | flops | bytes accessed | tf_op | source)
XLA Modules:
  0.0 65.4 jit_solution(9296897692869218791)
XLA Ops:
  0.0 0.7 %and_select_fusion.1 = (s32[8]{0:T(128)S(1)}, s32[8]{0:T(128)S(1)}) fusion(s32[8]{0:T(128)} %lengths_ref.1, s32[8]{0:T(128)} %splits_ref.1), kind=kLoop, calls=%fused_computation.3 | loop fusion | flops 128 | bytes 128 | tf_op jit(solution)/shard_map/jit(floor_divide)/jit(_where)/select_n | solution.py:397
  0.7 0.1 select_convert_fusion
  0.8 1.3 %reshape.15.kv_ref = bf16[8,128]{1,0:T(8,128)(2,1)} reshape(bf16[8,2,64]{2,1,0:T(2,128)(2,1)} %param.9) | data formatting | bytes 4096 | tf_op jit(solution)/shard_map/reshape | solution.py:400
  2.1 1.3 %pad_maximum_fusion.sent_ref = bf16[8,384]{1,0:T(8,128)(2,1)} fusion(bf16[8,128]{1,0:T(8,128)(2,1)S(1)} %select_convert_fusion, bf16[8,256]{1,0:T(8,128)(2,1)} %queries_ref.1), kind=kLoop, calls=%fused_computation | loop fusion | flops 12288 | bytes 12288 | tf_op jit(solution)/shard_map/concatenate | solution.py:399
  3.4 60.7 %shard_map.82 = bf16[8,256]{1,0:T(8,128)(2,1)} custom-call(s32[8]{0:T(128)} %lengths_ref.1, s32[8]{0:T(128)} %splits_ref.1, s32[4]{0:T(128)} %helpers_ref.1, bf16[8,384]{1,0:T(8,128)(2,1)} %pad_maximum_fusion.sent_ref, bf16[8,256]{1,0:T(8,128)(2,1)} %queries_ref.1, bf16[8,128]{1,0:T(8,128)(2,1)} %reshape.15.kv_ref, bf16[8,2,1,512,128]{4,3,2,1,0:T(8,128)(2,1)} %home_hbm.1, ...), custom_call_target="tpu_custom_call" | custom-call | tf_op jit(solution)/shard_map/pallas_call | solution.py:406
  64.1 1.3 %copy.10 = bf16[8,256]{1,0:T(8,128)(2,1)} copy(bf16[8,256]{1,0:T(8,128)(2,1)} %shard_map.82) | data formatting | bytes 8192
  (2 shorter events, 0.0 us)

commit v9 on v8

--- a/solution.py
+++ b/solution.py
@@ -237,14 +237,14 @@
     return wide.astype(jnp.bfloat16)
 
 
-def whole_kernel(ny, nz, n_tp, slots, lengths_ref, splits_ref, helpers_ref, sent_ref, queries_ref,
-                 kv_ref, home_hbm, help_hbm, w_hbm, out_ref, home_ref, help_ref, w_ref, local,
+def whole_kernel(ny, nz, n_tp, slots, lengths_ref, splits_ref, helpers_ref, sent_ref, kv_ref, home_hbm, help_hbm, w_hbm, out_ref, home_ref, help_ref, w_ref, local,
                  got1, got2, back, stat, part, held, send1, recv1, send2, recv2, send3, recv3):
     n = ny * nz
     me = lax.axis_index("grp")
     col = lax.axis_index("tp")
-    rows = queries_ref.shape[0]
-    heads = queries_ref.shape[1] // 64
+    rows = sent_ref.shape[0]
+    heads = w_ref.shape[0] // 64
+    qw = heads * 64
     pairs = w_ref.shape[0] // 128
     width = out_ref.shape[1]
 
@@ -274,13 +274,13 @@
     low = lane < 64
     loads[0].wait()
     for r in range(rows):
-        kv = kv_ref[r : r + 1, :].astype(jnp.float32)
-        turned = pltpu.roll(kv, 64, 1)
-        fresh_k = jnp.where(low, kv, turned).astype(jnp.bfloat16)
-        fresh_v = jnp.where(low, turned, kv)
+        key = kv_ref[r, 0:1, :].astype(jnp.float32)
+        value = kv_ref[r, 1:2, :].astype(jnp.float32)
+        fresh_k = jnp.concatenate([key, key], axis=1).astype(jnp.bfloat16)
+        fresh_v = jnp.concatenate([value, value], axis=1)
         count = splits_ref[r].astype(jnp.float32)
         top, total, mixed = attend_tile(
-            widen(queries_ref[r : r + 1, :].astype(jnp.float32), heads),
+            widen(sent_ref[r : r + 1, :qw].astype(jnp.float32), heads),
             home_ref[r, 0, 0],
             home_ref[r, 1, 0],
             count,
@@ -303,7 +303,6 @@
     for k in range(slots):
         pick = jnp.where((pick_row == k) & (pick_col == helpers_ref[k] % rows), 1.0, pick)
     chosen = jnp.dot(pick.astype(jnp.bfloat16), block, preferred_element_type=jnp.float32)
-    qw = heads * 64
     for k in range(slots):
         count = chosen[k : k + 1, qw : qw + 1] * 32.0 + chosen[k : k + 1, qw + 1 : qw + 2]
         top, total, mixed = attend_tile(
@@ -397,7 +396,6 @@
         lane == 0, (count // 32)[:, None], jnp.where(lane == 1, (count % 32)[:, None], 0)
     ).astype(jnp.bfloat16)
     sent = jnp.concatenate([queries, code], axis=1)
-    kv = new_kv.reshape(row_count, 2 * new_kv.shape[2])
 
     out_cols = out_weight.shape[1] // n_tp
     vmem = pl.BlockSpec(memory_space=pltpu.VMEM)
@@ -406,7 +404,7 @@
     return pl.pallas_call(
         functools.partial(whole_kernel, ny, nz, n_tp, slots),
         out_shape=jax.ShapeDtypeStruct((row_count, out_cols), jnp.bfloat16),
-        in_specs=[smem] * 3 + [vmem] * 3 + [pl.BlockSpec(memory_space=pl.ANY)] * 3,
+        in_specs=[smem] * 3 + [vmem] * 2 + [pl.BlockSpec(memory_space=pl.ANY)] * 3,
         out_specs=vmem,
         scratch_shapes=[
             pltpu.VMEM(home_cache.shape, home_cache.dtype),
@@ -427,7 +425,7 @@
             pltpu.SemaphoreType.DMA((n_tp,)),
         ],
         compiler_params=pltpu.CompilerParams(collective_id=0, has_side_effects=True),
-    )(lengths, split_at, helper_req, sent, queries, kv, home_cache, help_cache, out_weight)
+    )(lengths, split_at, helper_req, sent, new_kv, home_cache, help_cache, out_weight)
 
 
 def grp_rows(mesh):

time: 65.7 us -> 64.2 us (0.977)
  local copies, waits for them, and re-layouts: 2.62 us -> 1.27 us
    reshape x1 -> x0, local copies, waits for them, and re-layouts: 1.35 us -> none  [per_device(): kv = new_kv.reshape(row_count, 2 * new_kv.shape[2])]
where the time goes in v9:
time: 64.2 us; the launch traced here: 63.9 us
  Pallas kernels  60.6 us (94%)
  other arithmetic  2.04 us (3%)
  local copies, waits for them, and re-layouts  1.27 us (2%)
    pallas_call x1, Pallas kernels, per_device(): pl.pallas_call(functools.partial(whole_kernel, ny, nz, n_tp, slots), out_...  60.6 us

profile of v9, /device:TPU:1, one launch (start us, length us, event | category | flops | bytes accessed | tf_op | source)
XLA Modules:
  0.0 63.9 jit_solution(8416729496370259659)
XLA Ops:
  0.0 0.7 %and_select_fusion.1 = (s32[8]{0:T(128)S(1)}, s32[8]{0:T(128)S(1)}) fusion(s32[8]{0:T(128)} %lengths_ref.1, s32[8]{0:T(128)} %splits_ref.1), kind=kLoop, calls=%fused_computation.3 | loop fusion | flops 128 | bytes 128 | tf_op jit(solution)/shard_map/jit(floor_divide)/jit(_where)/select_n | solution.py:396
  0.7 0.1 select_convert_fusion
  0.8 1.3 %pad_maximum_fusion.sent_ref = bf16[8,384]{1,0:T(8,128)(2,1)} fusion(bf16[8,128]{1,0:T(8,128)(2,1)S(1)} %select_convert_fusion, bf16[8,256]{1,0:T(8,128)(2,1)} %param.8), kind=kLoop, calls=%fused_computation | loop fusion | flops 12288 | bytes 12288 | tf_op jit(solution)/shard_map/concatenate | solution.py:398
  2.0 60.6 %shard_map.82 = bf16[8,256]{1,0:T(8,128)(2,1)} custom-call(s32[8]{0:T(128)} %lengths_ref.1, s32[8]{0:T(128)} %splits_ref.1, s32[4]{0:T(128)} %helpers_ref.1, bf16[8,384]{1,0:T(8,128)(2,1)} %pad_maximum_fusion.sent_ref, bf16[8,2,64]{2,1,0:T(2,128)(2,1)} %kv_ref.1, bf16[8,2,1,512,128]{4,3,2,1,0:T(8,128)(2,1)} %home_hbm.1, ...), custom_call_target="tpu_custom_call" | custom-call | tf_op jit(solution)/shard_map/pallas_call | solution.py:404
  62.7 1.3 %copy.10 = bf16[8,256]{1,0:T(8,128)(2,1)} copy(bf16[8,256]{1,0:T(8,128)(2,1)} %shard_map.82) | data formatting | bytes 8192
  (2 shorter events, 0.0 us)

commit v10 on v9

--- a/solution.py
+++ b/solution.py
@@ -134,12 +134,13 @@
 
 def far_first(i, size):
     half = size // 2
-    return jnp.where(i % 2 == 0, half + i // 2, half - (i + 1) // 2)
+    return half + i // 2 if i % 2 == 0 else half - (i + 1) // 2
 
 
 def fanout(ny, nz, me, col, src, dst, send, recv):
     my_y = me // nz
     my_z = me % nz
+    order = [(far_first(a, ny), far_first(b, nz)) for a in range(ny) for b in range(nz)][:-1]
 
     def copy(k, peer, slot):
         return pltpu.make_async_remote_copy(
@@ -151,33 +152,18 @@
             device_id_type=MESH,
         )
 
-    def offsets(k):
-        return far_first(k // nz, ny), far_first(k % nz, nz)
-
-    def to(k):
-        dy, dz = offsets(k)
-        return lax.rem(my_y + dy, ny) * nz + lax.rem(my_z + dz, nz)
-
-    def source(k):
-        dy, dz = offsets(k)
-        return lax.rem(my_y + ny - dy, ny) * nz + lax.rem(my_z + nz - dz, nz)
-
-    last = ny * nz - 1
-
-    def start(k, carry):
-        copy(k, to(k), me).start()
-        return carry
-
-    lax.fori_loop(0, last, start, 0)
+    targets = []
+    for k, (dy, dz) in enumerate(order):
+        peer = lax.rem(my_y + dy, ny) * nz + lax.rem(my_z + dz, nz)
+        out = copy(k, peer, me)
+        out.start()
+        targets.append(out)
 
     def finish():
-        def one(k, carry):
-            copy(k, to(k), me).wait_send()
-            s = source(k)
-            copy(k, s, s).wait_recv()
-            return carry
-
-        lax.fori_loop(0, last, one, 0)
+        for k, (dy, dz) in enumerate(order):
+            targets[k].wait_send()
+            source = lax.rem(my_y + (ny - dy), ny) * nz + lax.rem(my_z + (nz - dz), nz)
+            copy(k, source, source).wait_recv()
 
     return finish
 

time: 64.2 us -> 63.6 us (level)
  no operation moved by 1% of the time
where the time goes in v10:
time: 63.6 us; the launch traced here: 63.4 us
  Pallas kernels  60.1 us (94%)
  other arithmetic  2.04 us (3%)
  local copies, waits for them, and re-layouts  1.27 us (2%)
    pallas_call x1, Pallas kernels, per_device(): pl.pallas_call(functools.partial(whole_kernel, ny, nz, n_tp, slots), out_...  60.1 us
    concatenate x1, other arithmetic, per_device(): sent = jnp.concatenate([queries, code], axis=1)  1.27 us
    unnamed x1, local copies, waits for them, and re-layouts  1.27 us

profile of v10, /device:TPU:1, one launch (start us, length us, event | category | flops | bytes accessed | tf_op | source)
XLA Modules:
  0.0 63.4 jit_solution(1586976063402411604)
XLA Ops:
  0.0 0.7 %and_select_fusion.1 = (s32[8]{0:T(128)S(1)}, s32[8]{0:T(128)S(1)}) fusion(s32[8]{0:T(128)} %lengths_ref.1, s32[8]{0:T(128)} %splits_ref.1), kind=kLoop, calls=%fused_computation.3 | loop fusion | flops 128 | bytes 128 | tf_op jit(solution)/shard_map/jit(floor_divide)/jit(_where)/select_n | solution.py:382
  0.7 0.1 select_convert_fusion
  0.8 1.3 %pad_maximum_fusion.sent_ref = bf16[8,384]{1,0:T(8,128)(2,1)} fusion(bf16[8,128]{1,0:T(8,128)(2,1)S(1)} %select_convert_fusion, bf16[8,256]{1,0:T(8,128)(2,1)} %param.8), kind=kLoop, calls=%fused_computation | loop fusion | flops 12288 | bytes 12288 | tf_op jit(solution)/shard_map/concatenate | solution.py:384
  2.0 60.1 %shard_map.82 = bf16[8,256]{1,0:T(8,128)(2,1)} custom-call(s32[8]{0:T(128)} %lengths_ref.1, s32[8]{0:T(128)} %splits_ref.1, s32[4]{0:T(128)} %helpers_ref.1, bf16[8,384]{1,0:T(8,128)(2,1)} %pad_maximum_fusion.sent_ref, bf16[8,2,64]{2,1,0:T(2,128)(2,1)} %kv_ref.1, bf16[8,2,1,512,128]{4,3,2,1,0:T(8,128)(2,1)} %home_hbm.1, ...), custom_call_target="tpu_custom_call" | custom-call | tf_op jit(solution)/shard_map/pallas_call | solution.py:390
  62.1 1.3 %copy.10 = bf16[8,256]{1,0:T(8,128)(2,1)} copy(bf16[8,256]{1,0:T(8,128)(2,1)} %shard_map.82) | data formatting | bytes 8192
  (2 shorter events, 0.0 us)

commit v11 on v10

--- a/solution.py
+++ b/solution.py
@@ -236,12 +236,15 @@
 
     barrier = pltpu.get_barrier_semaphore()
 
-    def greet(k, carry):
-        peer = lax.rem(me + k, n)
-        pl.semaphore_signal(barrier, inc=1, device_id=(peer, col), device_id_type=MESH)
-        return carry
-
-    lax.fori_loop(1, n, greet, 0)
+    my_y = me // nz
+    my_z = me % nz
+    for a in range(ny):
+        for b in range(nz):
+            dy, dz = far_first(a, ny), far_first(b, nz)
+            if dy == 0 and dz == 0:
+                continue
+            peer = lax.rem(my_y + dy, ny) * nz + lax.rem(my_z + dz, nz)
+            pl.semaphore_signal(barrier, inc=1, device_id=(peer, col), device_id_type=MESH)
     for k in range(1, n_tp):
         peer = lax.rem(col + k, n_tp)
         pl.semaphore_signal(barrier, inc=1, device_id=(me, peer), device_id_type=MESH)

time: 63.6 us -> 63 us (level)
  Pallas kernels: 60.1 us -> 59.4 us
    pallas_call x1, Pallas kernels: 60.1 us -> 59.4 us  [per_device(): pl.pallas_call(functools.partial(whole_kernel, ny, nz, n_tp, slots), out_...]
where the time goes in v11:
time: 63 us; the launch traced here: 62.8 us
  Pallas kernels  59.4 us (94%)
  other arithmetic  2.04 us (3%)
  local copies, waits for them, and re-layouts  1.27 us (2%)
    pallas_call x1, Pallas kernels, per_device(): pl.pallas_call(functools.partial(whole_kernel, ny, nz, n_tp, slots), out_...  59.4 us
    concatenate x1, other arithmetic, per_device(): sent = jnp.concatenate([queries, code], axis=1)  1.27 us
    unnamed x1, local copies, waits for them, and re-layouts  1.27 us

profile of v11, /device:TPU:1, one launch (start us, length us, event | category | flops | bytes accessed | tf_op | source)
XLA Modules:
  0.0 62.8 jit_solution(889175593527683255)
XLA Ops:
  0.0 0.7 %and_select_fusion.1 = (s32[8]{0:T(128)S(1)}, s32[8]{0:T(128)S(1)}) fusion(s32[8]{0:T(128)} %lengths_ref.1, s32[8]{0:T(128)} %splits_ref.1), kind=kLoop, calls=%fused_computation.3 | loop fusion | flops 128 | bytes 128 | tf_op jit(solution)/shard_map/jit(floor_divide)/jit(_where)/select_n | solution.py:385
  0.7 0.1 select_convert_fusion
  0.8 1.3 %pad_maximum_fusion.sent_ref = bf16[8,384]{1,0:T(8,128)(2,1)} fusion(bf16[8,128]{1,0:T(8,128)(2,1)S(1)} %select_convert_fusion, bf16[8,256]{1,0:T(8,128)(2,1)} %param.8), kind=kLoop, calls=%fused_computation | loop fusion | flops 12288 | bytes 12288 | tf_op jit(solution)/shard_map/concatenate | solution.py:387
  2.0 59.4 %shard_map.82 = bf16[8,256]{1,0:T(8,128)(2,1)} custom-call(s32[8]{0:T(128)} %lengths_ref.1, s32[8]{0:T(128)} %splits_ref.1, s32[4]{0:T(128)} %helpers_ref.1, bf16[8,384]{1,0:T(8,128)(2,1)} %pad_maximum_fusion.sent_ref, bf16[8,2,64]{2,1,0:T(2,128)(2,1)} %kv_ref.1, bf16[8,2,1,512,128]{4,3,2,1,0:T(8,128)(2,1)} %home_hbm.1, ...), custom_call_target="tpu_custom_call" | custom-call | tf_op jit(solution)/shard_map/pallas_call | solution.py:393
  61.5 1.3 %copy.10 = bf16[8,256]{1,0:T(8,128)(2,1)} copy(bf16[8,256]{1,0:T(8,128)(2,1)} %shard_map.82) | data formatting | bytes 8192
  (2 shorter events, 0.0 us)

commit v12 on v11

--- a/solution.py
+++ b/solution.py
@@ -223,14 +223,25 @@
     return wide.astype(jnp.bfloat16)
 
 
-def whole_kernel(ny, nz, n_tp, slots, lengths_ref, splits_ref, helpers_ref, sent_ref, kv_ref, home_hbm, help_hbm, w_hbm, out_ref, home_ref, help_ref, w_ref, local,
+def whole_kernel(ny, nz, n_tp, slots, lengths_ref, splits_ref, helpers_ref, queries_ref, kv_ref,
+                 home_hbm, help_hbm, w_hbm, out_ref, sent_ref, home_ref, help_ref, w_ref, local,
                  got1, got2, back, stat, part, held, send1, recv1, send2, recv2, send3, recv3):
     n = ny * nz
     me = lax.axis_index("grp")
     col = lax.axis_index("tp")
-    rows = sent_ref.shape[0]
+    rows = queries_ref.shape[0]
     heads = w_ref.shape[0] // 64
     qw = heads * 64
+
+    code_row = lax.broadcasted_iota(jnp.int32, (rows, 128), 0)
+    code_lane = lax.broadcasted_iota(jnp.int32, (rows, 128), 1)
+    code = jnp.zeros((rows, 128), jnp.float32)
+    for r in range(rows):
+        count = lengths_ref[r] - splits_ref[r]
+        code = jnp.where((code_row == r) & (code_lane == 0), (count // 32).astype(jnp.float32), code)
+        code = jnp.where((code_row == r) & (code_lane == 1), (count % 32).astype(jnp.float32), code)
+    sent_ref[:, :qw] = queries_ref[...]
+    sent_ref[:, qw:] = code.astype(sent_ref.dtype)
     pairs = w_ref.shape[0] // 128
     width = out_ref.shape[1]
 
@@ -269,7 +280,7 @@
         fresh_v = jnp.concatenate([value, value], axis=1)
         count = splits_ref[r].astype(jnp.float32)
         top, total, mixed = attend_tile(
-            widen(sent_ref[r : r + 1, :qw].astype(jnp.float32), heads),
+            widen(queries_ref[r : r + 1, :].astype(jnp.float32), heads),
             home_ref[r, 0, 0],
             home_ref[r, 1, 0],
             count,
@@ -379,12 +390,7 @@
     pairs = width // 128
     lanes = 128
 
-    count = lengths - split_at
-    lane = jnp.arange(lanes)[None, :]
-    code = jnp.where(
-        lane == 0, (count // 32)[:, None], jnp.where(lane == 1, (count % 32)[:, None], 0)
-    ).astype(jnp.bfloat16)
-    sent = jnp.concatenate([queries, code], axis=1)
+    sent_shape = (row_count, width + lanes)
 
     out_cols = out_weight.shape[1] // n_tp
     vmem = pl.BlockSpec(memory_space=pltpu.VMEM)
@@ -396,11 +402,12 @@
         in_specs=[smem] * 3 + [vmem] * 2 + [pl.BlockSpec(memory_space=pl.ANY)] * 3,
         out_specs=vmem,
         scratch_shapes=[
+            pltpu.VMEM(sent_shape, jnp.bfloat16),
             pltpu.VMEM(home_cache.shape, home_cache.dtype),
             pltpu.VMEM(help_cache.shape, help_cache.dtype),
             pltpu.VMEM(out_weight.shape, out_weight.dtype),
             pltpu.SemaphoreType.DMA((3,)),
-            pltpu.VMEM((n_grp,) + sent.shape, jnp.bfloat16),
+            pltpu.VMEM((n_grp,) + sent_shape, jnp.bfloat16),
             pltpu.VMEM((n_grp, back_rows, lanes), jnp.float32),
             pltpu.VMEM((back_rows, lanes), jnp.float32),
             pltpu.VMEM((3, pairs, row_count, lanes), jnp.float32),
@@ -414,7 +421,7 @@
             pltpu.SemaphoreType.DMA((n_tp,)),
         ],
         compiler_params=pltpu.CompilerParams(collective_id=0, has_side_effects=True),
-    )(lengths, split_at, helper_req, sent, new_kv, home_cache, help_cache, out_weight)
+    )(lengths, split_at, helper_req, queries, new_kv, home_cache, help_cache, out_weight)
 
 
 def grp_rows(mesh):

time: 63 us -> 61 us (0.968)
  other arithmetic: 2.04 us -> 0 us
    concatenate x1 -> x0, other arithmetic: 1.27 us -> none  [per_device(): sent = jnp.concatenate([queries, code], axis=1)]
    select_n x2 -> x0, other arithmetic: 0.68 us -> none  [the longest x1 0.68 us: per_device(): count // 32]
where the time goes in v12:
time: 61 us; the launch traced here: 60.8 us
  Pallas kernels  59.5 us (98%)
  local copies, waits for them, and re-layouts  1.28 us (2%)
    pallas_call x1, Pallas kernels, per_device(): pl.pallas_call(functools.partial(whole_kernel, ny, nz, n_tp, slots), out_...  59.5 us
    unnamed x1, local copies, waits for them, and re-layouts  1.28 us

profile of v12, /device:TPU:1, one launch (start us, length us, event | category | flops | bytes accessed | tf_op | source)
XLA Modules:
  0.0 60.8 jit_solution(14259994677514181184)
XLA Ops:
  0.0 59.5 %shard_map.82 = bf16[8,256]{1,0:T(8,128)(2,1)} custom-call(s32[8]{0:T(128)} %lengths_ref.1, s32[8]{0:T(128)} %splits_ref.1, s32[4]{0:T(128)} %helpers_ref.1, bf16[8,256]{1,0:T(8,128)(2,1)} %queries_ref.1, bf16[8,2,64]{2,1,0:T(2,128)(2,1)} %kv_ref.1, bf16[8,2,1,512,128]{4,3,2,1,0:T(8,128)(2,1)} %home_hbm.1, bf16[4,2,1,512,128]{4,3,2,1,0:T(8,128)(2,1)} %help_hbm.1, ...), custom_call_target="tpu_custom_call" | custom-call | tf_op jit(solution)/shard_map/pallas_call | solution.py:399
  59.5 1.3 %copy.10 = bf16[8,256]{1,0:T(8,128)(2,1)} copy(bf16[8,256]{1,0:T(8,128)(2,1)} %shard_map.82) | data formatting | bytes 8192

commit v13 on v12

--- a/solution.py
+++ b/solution.py
@@ -398,7 +398,7 @@
     back_rows = 3 * slots * pairs
     return pl.pallas_call(
         functools.partial(whole_kernel, ny, nz, n_tp, slots),
-        out_shape=jax.ShapeDtypeStruct((row_count, out_cols), jnp.bfloat16),
+        out_shape=jax.ShapeDtypeStruct((row_count, out_cols), jnp.float32),
         in_specs=[smem] * 3 + [vmem] * 2 + [pl.BlockSpec(memory_space=pl.ANY)] * 3,
         out_specs=vmem,
         scratch_shapes=[
@@ -421,7 +421,7 @@
             pltpu.SemaphoreType.DMA((n_tp,)),
         ],
         compiler_params=pltpu.CompilerParams(collective_id=0, has_side_effects=True),
-    )(lengths, split_at, helper_req, queries, new_kv, home_cache, help_cache, out_weight)
+    )(lengths, split_at, helper_req, queries, new_kv, home_cache, help_cache, out_weight).astype(jnp.bfloat16)
 
 
 def grp_rows(mesh):

time: 61 us -> 61 us (level)
  other arithmetic: 0 us -> 1.29 us
  local copies, waits for them, and re-layouts: 1.28 us -> 0 us
    convert_element_type x0 -> x1, other arithmetic: none -> 1.29 us  [per_device(): return pl.pallas_call(functools.partial(whole_kernel, ny, nz, n_tp, slots...]
    unnamed x1 -> x0, local copies, waits for them, and re-layouts: 1.28 us -> none
where the time goes in v13:
time: 61 us; the launch traced here: 60.8 us
  Pallas kernels  59.5 us (98%)
  other arithmetic  1.29 us (2%)
    pallas_call x1, Pallas kernels, per_device(): pl.pallas_call(functools.partial(whole_kernel, ny, nz, n_tp, slots), out_...  59.5 us
    convert_element_type x1, other arithmetic, per_device(): return pl.pallas_call(functools.partial(whole_kernel, ny, nz, n_tp, slots...  1.29 us

profile of v13, /device:TPU:1, one launch (start us, length us, event | category | flops | bytes accessed | tf_op | source)
XLA Modules:
  0.0 60.8 jit_solution(6055697750294206187)
XLA Ops:
  0.0 59.5 %shard_map.82 = f32[8,256]{1,0:T(8,128)} custom-call(s32[8]{0:T(128)} %lengths_ref.1, s32[8]{0:T(128)} %splits_ref.1, s32[4]{0:T(128)} %helpers_ref.1, bf16[8,256]{1,0:T(8,128)(2,1)} %queries_ref.1, bf16[8,2,64]{2,1,0:T(2,128)(2,1)} %kv_ref.1, bf16[8,2,1,512,128]{4,3,2,1,0:T(8,128)(2,1)} %home_hbm.1, bf16[4,2,1,512,128]{4,3,2,1,0:T(8,128)(2,1)} %help_hbm.1, ...), custom_call_target="tpu_custom_call" | custom-call | tf_op jit(solution)/shard_map/pallas_call | solution.py:399
  59.5 1.3 %convert_element_type.3 = bf16[8,256]{1,0:T(8,128)(2,1)} convert(f32[8,256]{1,0:T(8,128)} %shard_map.82) | non-fusion elementwise | flops 2048 | bytes 12288 | tf_op jit(solution)/shard_map/convert_element_type | solution.py:424

commit v14 on v12

--- a/solution.py
+++ b/solution.py
@@ -303,6 +303,8 @@
     for k in range(slots):
         pick = jnp.where((pick_row == k) & (pick_col == helpers_ref[k] % rows), 1.0, pick)
     chosen = jnp.dot(pick.astype(jnp.bfloat16), block, preferred_element_type=jnp.float32)
+    stat_lane = lax.broadcasted_iota(jnp.int32, (1, 128), 1)
+    stat_row = jnp.zeros((1, 128), jnp.float32)
     for k in range(slots):
         count = chosen[k : k + 1, qw : qw + 1] * 32.0 + chosen[k : k + 1, qw + 1 : qw + 2]
         top, total, mixed = attend_tile(
@@ -311,8 +313,12 @@
         for h in range(pairs):
             u, m, l = pair_rows(top, total, mixed, h)
             back[k * pairs + h : k * pairs + h + 1, :] = u
-            back[(slots + k) * pairs + h : (slots + k) * pairs + h + 1, :] = m
-            back[(2 * slots + k) * pairs + h : (2 * slots + k) * pairs + h + 1, :] = l
+        for g in range(heads):
+            stat_row = jnp.where(stat_lane == k * heads + g, top[g : g + 1, :], stat_row)
+            stat_row = jnp.where(
+                stat_lane == (slots + k) * heads + g, total[g : g + 1, :], stat_row
+            )
+    back[slots * pairs : slots * pairs + 1, :] = stat_row
 
     wait2 = fanout(ny, nz, me, col, back, got2, send2, recv2)
 
@@ -331,19 +337,24 @@
 
     loads[2].wait()
     theirs = got2[partner]
+    stats = theirs[slots * pairs : slots * pairs + 1, :]
+    left = lax.broadcasted_iota(jnp.int32, (1, 128), 1) < 64
     acc = jnp.zeros(part.shape, jnp.float32)
     for h in range(pairs):
-
-        def pick_far(base):
-            x = fsel[:, 0:1] * theirs[base + h : base + h + 1, :]
-            for k in range(1, slots):
-                r0 = base + k * pairs + h
-                x = x + fsel[:, k : k + 1] * theirs[r0 : r0 + 1, :]
+        far_u = fsel[:, 0:1] * theirs[h : h + 1, :]
+        for k in range(1, slots):
+            far_u = far_u + fsel[:, k : k + 1] * theirs[k * pairs + h : k * pairs + h + 1, :]
+
+        def pick_stat(base):
+            x = None
+            for k in range(slots):
+                j = base + k * heads + 2 * h
+                val = jnp.where(left, stats[:, j : j + 1], stats[:, j + 1 : j + 2])
+                x = fsel[:, k : k + 1] * val if x is None else x + fsel[:, k : k + 1] * val
             return x
 
-        far_u = pick_far(0)
-        far_m = jnp.where(has > 0.0, pick_far(slots * pairs), -1e30)
-        far_l = pick_far(2 * slots * pairs)
+        far_m = jnp.where(has > 0.0, pick_stat(0), -1e30)
+        far_l = pick_stat(slots * heads)
         home_u = stat[0, h]
         home_m = stat[1, h]
         home_l = stat[2, h]
@@ -395,7 +406,7 @@
     out_cols = out_weight.shape[1] // n_tp
     vmem = pl.BlockSpec(memory_space=pltpu.VMEM)
     smem = pl.BlockSpec(memory_space=pltpu.SMEM)
-    back_rows = 3 * slots * pairs
+    back_rows = slots * pairs + 1
     return pl.pallas_call(
         functools.partial(whole_kernel, ny, nz, n_tp, slots),
         out_shape=jax.ShapeDtypeStruct((row_count, out_cols), jnp.bfloat16),

time: 61 us -> 50.5 us (0.83)
  Pallas kernels: 59.5 us -> 49.1 us
    pallas_call x1, Pallas kernels: 59.5 us -> 49.1 us  [per_device(): pl.pallas_call(functools.partial(whole_kernel, ny, nz, n_tp, slots), out_...]
where the time goes in v14:
time: 50.5 us; the launch traced here: 50.3 us
  Pallas kernels  49.1 us (97%)
  local copies, waits for them, and re-layouts  1.28 us (3%)
    pallas_call x1, Pallas kernels, per_device(): pl.pallas_call(functools.partial(whole_kernel, ny, nz, n_tp, slots), out_...  49.1 us
    unnamed x1, local copies, waits for them, and re-layouts  1.28 us

profile of v14, /device:TPU:1, one launch (start us, length us, event | category | flops | bytes accessed | tf_op | source)
XLA Modules:
  0.0 50.3 jit_solution(14577172043915658343)
XLA Ops:
  0.0 49.1 %shard_map.82 = bf16[8,256]{1,0:T(8,128)(2,1)} custom-call(s32[8]{0:T(128)} %lengths_ref.1, s32[8]{0:T(128)} %splits_ref.1, s32[4]{0:T(128)} %helpers_ref.1, bf16[8,256]{1,0:T(8,128)(2,1)} %queries_ref.1, bf16[8,2,64]{2,1,0:T(2,128)(2,1)} %kv_ref.1, bf16[8,2,1,512,128]{4,3,2,1,0:T(8,128)(2,1)} %home_hbm.1, bf16[4,2,1,512,128]{4,3,2,1,0:T(8,128)(2,1)} %help_hbm.1, ...), custom_call_target="tpu_custom_call" | custom-call | tf_op jit(solution)/shard_map/pallas_call | solution.py:410
  49.1 1.3 %copy.10 = bf16[8,256]{1,0:T(8,128)(2,1)} copy(bf16[8,256]{1,0:T(8,128)(2,1)} %shard_map.82) | data formatting | bytes 8192

commit v15 on v14

--- a/solution.py
+++ b/solution.py
@@ -207,13 +207,13 @@
     return u, m, l
 
 
-def widen(q, heads):
+def widen(pieces, heads):
     lane = lax.broadcasted_iota(jnp.int32, (2 * heads, 128), 1)
     row = lax.broadcasted_iota(jnp.int32, (2 * heads, 128), 0)
     low = lane < 64
     wide = jnp.zeros((2 * heads, 128), jnp.float32)
     for h in range(heads // 2):
-        a = q[:, h * 128 : (h + 1) * 128]
+        a = pieces[h]
         turned = pltpu.roll(a, 64, 1)
         g = 2 * h
         wide = jnp.where((row == g) & low, a, wide)
@@ -233,16 +233,29 @@
     heads = w_ref.shape[0] // 64
     qw = heads * 64
 
-    code_row = lax.broadcasted_iota(jnp.int32, (rows, 128), 0)
-    code_lane = lax.broadcasted_iota(jnp.int32, (rows, 128), 1)
-    code = jnp.zeros((rows, 128), jnp.float32)
+    pairs = heads // 2
+    pick_row = lax.broadcasted_iota(jnp.int32, (slots, rows), 0)
+    pick_col = lax.broadcasted_iota(jnp.int32, (slots, rows), 1)
+    code_lane = lax.broadcasted_iota(jnp.int32, (1, 128), 1)
+    pick = jnp.zeros((slots, rows), jnp.float32)
+    code = jnp.zeros((1, 128), jnp.float32)
+    rank = jnp.int32(0)
     for r in range(rows):
+        is_long = lengths_ref[r] > LONG_AT
         count = lengths_ref[r] - splits_ref[r]
-        code = jnp.where((code_row == r) & (code_lane == 0), (count // 32).astype(jnp.float32), code)
-        code = jnp.where((code_row == r) & (code_lane == 1), (count % 32).astype(jnp.float32), code)
-    sent_ref[:, :qw] = queries_ref[...]
-    sent_ref[:, qw:] = code.astype(sent_ref.dtype)
-    pairs = w_ref.shape[0] // 128
+        pick = jnp.where((pick_row == rank) & (pick_col == r) & is_long, 1.0, pick)
+        code = jnp.where((code_lane == rank) & is_long, (count // 32).astype(jnp.float32), code)
+        code = jnp.where(
+            (code_lane == slots + rank) & is_long, (count % 32).astype(jnp.float32), code
+        )
+        rank = rank + is_long.astype(jnp.int32)
+    long_q = jnp.dot(pick.astype(jnp.bfloat16), queries_ref[...], preferred_element_type=jnp.float32)
+    pay_row = lax.broadcasted_iota(jnp.int32, sent_ref.shape, 0)
+    pay = jnp.where(pay_row == slots * pairs, code, 0.0)
+    for k in range(slots):
+        for h in range(pairs):
+            pay = jnp.where(pay_row == k * pairs + h, long_q[k : k + 1, h * 128 : (h + 1) * 128], pay)
+    sent_ref[...] = pay.astype(sent_ref.dtype)
     width = out_ref.shape[1]
 
     barrier = pltpu.get_barrier_semaphore()
@@ -280,7 +293,7 @@
         fresh_v = jnp.concatenate([value, value], axis=1)
         count = splits_ref[r].astype(jnp.float32)
         top, total, mixed = attend_tile(
-            widen(queries_ref[r : r + 1, :].astype(jnp.float32), heads),
+            widen([queries_ref[r : r + 1, h * 128 : (h + 1) * 128].astype(jnp.float32) for h in range(pairs)], heads),
             home_ref[r, 0, 0],
             home_ref[r, 1, 0],
             count,
@@ -296,19 +309,15 @@
     loads[1].wait()
 
     partner = helpers_ref[0] // rows
-    block = got1[partner]
-    pick_row = lax.broadcasted_iota(jnp.int32, (slots, rows), 0)
-    pick_col = lax.broadcasted_iota(jnp.int32, (slots, rows), 1)
-    pick = jnp.zeros((slots, rows), jnp.float32)
-    for k in range(slots):
-        pick = jnp.where((pick_row == k) & (pick_col == helpers_ref[k] % rows), 1.0, pick)
-    chosen = jnp.dot(pick.astype(jnp.bfloat16), block, preferred_element_type=jnp.float32)
+    block = got1[partner].astype(jnp.float32)
+    codes = block[slots * pairs : slots * pairs + 1, :]
     stat_lane = lax.broadcasted_iota(jnp.int32, (1, 128), 1)
     stat_row = jnp.zeros((1, 128), jnp.float32)
     for k in range(slots):
-        count = chosen[k : k + 1, qw : qw + 1] * 32.0 + chosen[k : k + 1, qw + 1 : qw + 2]
+        count = codes[:, k : k + 1] * 32.0 + codes[:, slots + k : slots + k + 1]
+        pieces = [block[k * pairs + h : k * pairs + h + 1, :] for h in range(pairs)]
         top, total, mixed = attend_tile(
-            widen(chosen[k : k + 1, :qw], heads), help_ref[k, 0, 0], help_ref[k, 1, 0], count
+            widen(pieces, heads), help_ref[k, 0, 0], help_ref[k, 1, 0], count
         )
         for h in range(pairs):
             u, m, l = pair_rows(top, total, mixed, h)
@@ -401,7 +410,7 @@
     pairs = width // 128
     lanes = 128
 
-    sent_shape = (row_count, width + lanes)
+    sent_shape = (slots * pairs + 1, lanes)
 
     out_cols = out_weight.shape[1] // n_tp
     vmem = pl.BlockSpec(memory_space=pltpu.VMEM)

time: 50.5 us -> 47.7 us (0.945)
  Pallas kernels: 49.1 us -> 46.2 us
    pallas_call x1, Pallas kernels: 49.1 us -> 46.2 us  [per_device(): pl.pallas_call(functools.partial(whole_kernel, ny, nz, n_tp, slots), out_...]
where the time goes in v15:
time: 47.7 us; the launch traced here: 47.5 us
  Pallas kernels  46.2 us (97%)
  local copies, waits for them, and re-layouts  1.28 us (3%)
    pallas_call x1, Pallas kernels, per_device(): pl.pallas_call(functools.partial(whole_kernel, ny, nz, n_tp, slots), out_...  46.2 us
    unnamed x1, local copies, waits for them, and re-layouts  1.28 us

profile of v15, /device:TPU:1, one launch (start us, length us, event | category | flops | bytes accessed | tf_op | source)
XLA Modules:
  0.0 47.5 jit_solution(15290893261691234845)
XLA Ops:
  0.0 46.2 %shard_map.82 = bf16[8,256]{1,0:T(8,128)(2,1)} custom-call(s32[8]{0:T(128)} %lengths_ref.1, s32[8]{0:T(128)} %splits_ref.1, s32[4]{0:T(128)} %helpers_ref.1, bf16[8,256]{1,0:T(8,128)(2,1)} %queries_ref.1, bf16[8,2,64]{2,1,0:T(2,128)(2,1)} %kv_ref.1, bf16[8,2,1,512,128]{4,3,2,1,0:T(8,128)(2,1)} %home_hbm.1, bf16[4,2,1,512,128]{4,3,2,1,0:T(8,128)(2,1)} %help_hbm.1, ...), custom_call_target="tpu_custom_call" | custom-call | tf_op jit(solution)/shard_map/pallas_call | solution.py:419
  46.2 1.3 %copy.10 = bf16[8,256]{1,0:T(8,128)(2,1)} copy(bf16[8,256]{1,0:T(8,128)(2,1)} %shard_map.82) | data formatting | bytes 8192

commit v16 on v15

--- a/solution.py
+++ b/solution.py
@@ -321,13 +321,18 @@
         )
         for h in range(pairs):
             u, m, l = pair_rows(top, total, mixed, h)
-            back[k * pairs + h : k * pairs + h + 1, :] = u
+            back[k * pairs + h : k * pairs + h + 1, :] = u.astype(back.dtype)
+        n_st = slots * heads
         for g in range(heads):
-            stat_row = jnp.where(stat_lane == k * heads + g, top[g : g + 1, :], stat_row)
-            stat_row = jnp.where(
-                stat_lane == (slots + k) * heads + g, total[g : g + 1, :], stat_row
-            )
-    back[slots * pairs : slots * pairs + 1, :] = stat_row
+            for which, value in enumerate((top[g : g + 1, :], total[g : g + 1, :])):
+                hi = value.astype(jnp.bfloat16).astype(jnp.float32)
+                rest = value - hi
+                mid = rest.astype(jnp.bfloat16).astype(jnp.float32)
+                lo = (rest - mid).astype(jnp.bfloat16).astype(jnp.float32)
+                for part_i, piece in enumerate((hi, mid, lo)):
+                    at = (3 * which + part_i) * n_st + k * heads + g
+                    stat_row = jnp.where(stat_lane == at, piece, stat_row)
+    back[slots * pairs : slots * pairs + 1, :] = stat_row.astype(back.dtype)
 
     wait2 = fanout(ny, nz, me, col, back, got2, send2, recv2)
 
@@ -345,8 +350,19 @@
     wait2()
 
     loads[2].wait()
-    theirs = got2[partner]
-    stats = theirs[slots * pairs : slots * pairs + 1, :]
+    theirs = got2[partner].astype(jnp.float32)
+    packed = theirs[slots * pairs : slots * pairs + 1, :]
+    n_st = slots * heads
+
+    def joined(which):
+        base = 3 * which * n_st
+        return (
+            packed[:, base : base + n_st]
+            + packed[:, base + n_st : base + 2 * n_st]
+            + packed[:, base + 2 * n_st : base + 3 * n_st]
+        )
+
+    stats = jnp.concatenate([joined(0), joined(1)], axis=1)
     left = lax.broadcasted_iota(jnp.int32, (1, 128), 1) < 64
     acc = jnp.zeros(part.shape, jnp.float32)
     for h in range(pairs):
@@ -428,8 +444,8 @@
             pltpu.VMEM(out_weight.shape, out_weight.dtype),
             pltpu.SemaphoreType.DMA((3,)),
             pltpu.VMEM((n_grp,) + sent_shape, jnp.bfloat16),
-            pltpu.VMEM((n_grp, back_rows, lanes), jnp.float32),
-            pltpu.VMEM((back_rows, lanes), jnp.float32),
+            pltpu.VMEM((n_grp, back_rows, lanes), jnp.bfloat16),
+            pltpu.VMEM((back_rows, lanes), jnp.bfloat16),
             pltpu.VMEM((3, pairs, row_count, lanes), jnp.float32),
             pltpu.VMEM((row_count, out_weight.shape[1]), jnp.float32),
             pltpu.VMEM((n_tp, row_count, out_cols), jnp.float32),

time: 47.7 us -> 47.2 us (0.990)
  Pallas kernels: 46.2 us -> 45.7 us
    pallas_call x1, Pallas kernels: 46.2 us -> 45.7 us  [per_device(): pl.pallas_call(functools.partial(whole_kernel, ny, nz, n_tp, slots), out_...]
where the time goes in v16:
time: 47.2 us; the launch traced here: 47 us
  Pallas kernels  45.7 us (97%)
  local copies, waits for them, and re-layouts  1.28 us (3%)
    pallas_call x1, Pallas kernels, per_device(): pl.pallas_call(functools.partial(whole_kernel, ny, nz, n_tp, slots), out_...  45.7 us
    unnamed x1, local copies, waits for them, and re-layouts  1.28 us

profile of v16, /device:TPU:1, one launch (start us, length us, event | category | flops | bytes accessed | tf_op | source)
XLA Modules:
  0.0 47.0 jit_solution(6362714012695907279)
XLA Ops:
  0.0 45.7 %shard_map.82 = bf16[8,256]{1,0:T(8,128)(2,1)} custom-call(s32[8]{0:T(128)} %lengths_ref.1, s32[8]{0:T(128)} %splits_ref.1, s32[4]{0:T(128)} %helpers_ref.1, bf16[8,256]{1,0:T(8,128)(2,1)} %queries_ref.1, bf16[8,2,64]{2,1,0:T(2,128)(2,1)} %kv_ref.1, bf16[8,2,1,512,128]{4,3,2,1,0:T(8,128)(2,1)} %home_hbm.1, bf16[4,2,1,512,128]{4,3,2,1,0:T(8,128)(2,1)} %help_hbm.1, ...), custom_call_target="tpu_custom_call" | custom-call | tf_op jit(solution)/shard_map/pallas_call | solution.py:435
  45.7 1.3 %copy.10 = bf16[8,256]{1,0:T(8,128)(2,1)} copy(bf16[8,256]{1,0:T(8,128)(2,1)} %shard_map.82) | data formatting | bytes 8192

commit v17 on v15

--- a/solution.py
+++ b/solution.py
@@ -348,7 +348,7 @@
     theirs = got2[partner]
     stats = theirs[slots * pairs : slots * pairs + 1, :]
     left = lax.broadcasted_iota(jnp.int32, (1, 128), 1) < 64
-    acc = jnp.zeros(part.shape, jnp.float32)
+    mixes = []
     for h in range(pairs):
         far_u = fsel[:, 0:1] * theirs[h : h + 1, :]
         for k in range(1, slots):
@@ -371,12 +371,10 @@
         home_e = jnp.exp(home_m - top)
         far_e = jnp.exp(far_m - top)
         mix = (home_u * home_e + far_u * far_e) / (home_l * home_e + far_l * far_e)
-        acc = acc + jnp.dot(
-            mix.astype(jnp.bfloat16),
-            w_ref[h * 128 : (h + 1) * 128, :],
-            preferred_element_type=jnp.float32,
-        )
-    part[...] = acc
+        mixes.append(mix.astype(jnp.bfloat16))
+    part[...] = jnp.dot(
+        jnp.concatenate(mixes, axis=1), w_ref[...], preferred_element_type=jnp.float32
+    )
 
     sends = []
     for k in range(1, n_tp):

time: 47.7 us -> 47.7 us (level)
  no operation moved by 1% of the time
where the time goes in v17:
time: 47.7 us; the launch traced here: 47.5 us
  Pallas kernels  46.2 us (97%)
  local copies, waits for them, and re-layouts  1.28 us (3%)
    pallas_call x1, Pallas kernels, per_device(): pl.pallas_call(functools.partial(whole_kernel, ny, nz, n_tp, slots), out_...  46.2 us
    unnamed x1, local copies, waits for them, and re-layouts  1.28 us

profile of v17, /device:TPU:1, one launch (start us, length us, event | category | flops | bytes accessed | tf_op | source)
XLA Modules:
  0.0 47.5 jit_solution(2305551029262473487)
XLA Ops:
  0.0 46.2 %shard_map.82 = bf16[8,256]{1,0:T(8,128)(2,1)} custom-call(s32[8]{0:T(128)} %lengths_ref.1, s32[8]{0:T(128)} %splits_ref.1, s32[4]{0:T(128)} %helpers_ref.1, bf16[8,256]{1,0:T(8,128)(2,1)} %queries_ref.1, bf16[8,2,64]{2,1,0:T(2,128)(2,1)} %kv_ref.1, bf16[8,2,1,512,128]{4,3,2,1,0:T(8,128)(2,1)} %home_hbm.1, bf16[4,2,1,512,128]{4,3,2,1,0:T(8,128)(2,1)} %help_hbm.1, ...), custom_call_target="tpu_custom_call" | custom-call | tf_op jit(solution)/shard_map/pallas_call | solution.py:417
  46.2 1.3 %copy.10 = bf16[8,256]{1,0:T(8,128)(2,1)} copy(bf16[8,256]{1,0:T(8,128)(2,1)} %shard_map.82) | data formatting | bytes 8192

commit v18 on v17

--- a/solution.py
+++ b/solution.py
@@ -285,26 +285,29 @@
     wait1 = fanout(ny, nz, me, col, sent_ref, got1, send1, recv1)
     lane = lax.broadcasted_iota(jnp.int32, (1, 128), 1)
     low = lane < 64
+    def home_rows(first, last):
+        for r in range(first, last):
+            key = kv_ref[r, 0:1, :].astype(jnp.float32)
+            value = kv_ref[r, 1:2, :].astype(jnp.float32)
+            fresh_k = jnp.concatenate([key, key], axis=1).astype(jnp.bfloat16)
+            fresh_v = jnp.concatenate([value, value], axis=1)
+            count = splits_ref[r].astype(jnp.float32)
+            top, total, mixed = attend_tile(
+                widen([queries_ref[r : r + 1, h * 128 : (h + 1) * 128].astype(jnp.float32) for h in range(pairs)], heads),
+                home_ref[r, 0, 0],
+                home_ref[r, 1, 0],
+                count,
+                fresh_k,
+                fresh_v,
+            )
+            for h in range(pairs):
+                u, m, l = pair_rows(top, total, mixed, h)
+                stat[0, h, r : r + 1, :] = u
+                stat[1, h, r : r + 1, :] = m
+                stat[2, h, r : r + 1, :] = l
+
     loads[0].wait()
-    for r in range(rows):
-        key = kv_ref[r, 0:1, :].astype(jnp.float32)
-        value = kv_ref[r, 1:2, :].astype(jnp.float32)
-        fresh_k = jnp.concatenate([key, key], axis=1).astype(jnp.bfloat16)
-        fresh_v = jnp.concatenate([value, value], axis=1)
-        count = splits_ref[r].astype(jnp.float32)
-        top, total, mixed = attend_tile(
-            widen([queries_ref[r : r + 1, h * 128 : (h + 1) * 128].astype(jnp.float32) for h in range(pairs)], heads),
-            home_ref[r, 0, 0],
-            home_ref[r, 1, 0],
-            count,
-            fresh_k,
-            fresh_v,
-        )
-        for h in range(pairs):
-            u, m, l = pair_rows(top, total, mixed, h)
-            stat[0, h, r : r + 1, :] = u
-            stat[1, h, r : r + 1, :] = m
-            stat[2, h, r : r + 1, :] = l
+    home_rows(0, rows // 2)
     wait1()
     loads[1].wait()
 
@@ -330,6 +333,7 @@
     back[slots * pairs : slots * pairs + 1, :] = stat_row
 
     wait2 = fanout(ny, nz, me, col, back, got2, send2, recv2)
+    home_rows(rows // 2, rows)
 
     sel_row = lax.broadcasted_iota(jnp.int32, (rows, slots), 0)
     sel_col = lax.broadcasted_iota(jnp.int32, (rows, slots), 1)

time: 47.7 us -> 47.7 us (level)
  no operation moved by 1% of the time
where the time goes in v18:
time: 47.7 us; the launch traced here: 47.5 us
  Pallas kernels  46.2 us (97%)
  local copies, waits for them, and re-layouts  1.28 us (3%)
    pallas_call x1, Pallas kernels, per_device(): pl.pallas_call(functools.partial(whole_kernel, ny, nz, n_tp, slots), out_...  46.2 us
    unnamed x1, local copies, waits for them, and re-layouts  1.28 us

profile of v18, /device:TPU:1, one launch (start us, length us, event | category | flops | bytes accessed | tf_op | source)
XLA Modules:
  0.0 47.5 jit_solution(7228243198873668772)
XLA Ops:
  0.0 46.2 %shard_map.82 = bf16[8,256]{1,0:T(8,128)(2,1)} custom-call(s32[8]{0:T(128)} %lengths_ref.1, s32[8]{0:T(128)} %splits_ref.1, s32[4]{0:T(128)} %helpers_ref.1, bf16[8,256]{1,0:T(8,128)(2,1)} %queries_ref.1, bf16[8,2,64]{2,1,0:T(2,128)(2,1)} %kv_ref.1, bf16[8,2,1,512,128]{4,3,2,1,0:T(8,128)(2,1)} %home_hbm.1, bf16[4,2,1,512,128]{4,3,2,1,0:T(8,128)(2,1)} %help_hbm.1, ...), custom_call_target="tpu_custom_call" | custom-call | tf_op jit(solution)/shard_map/pallas_call | solution.py:421
  46.3 1.3 %copy.10 = bf16[8,256]{1,0:T(8,128)(2,1)} copy(bf16[8,256]{1,0:T(8,128)(2,1)} %shard_map.82) | data formatting | bytes 8192

commit v19 on v17

--- a/solution.py
+++ b/solution.py
@@ -372,16 +372,18 @@
         far_e = jnp.exp(far_m - top)
         mix = (home_u * home_e + far_u * far_e) / (home_l * home_e + far_l * far_e)
         mixes.append(mix.astype(jnp.bfloat16))
-    part[...] = jnp.dot(
+    projected = jnp.dot(
         jnp.concatenate(mixes, axis=1), w_ref[...], preferred_element_type=jnp.float32
     )
+    for j in range(n_tp):
+        part[j] = projected[:, j * width : (j + 1) * width]
 
     sends = []
     for k in range(1, n_tp):
         peer = lax.rem(col + k, n_tp)
         cols = pl.ds(pl.multiple_of(peer * width, width), width)
         copy = pltpu.make_async_remote_copy(
-            src_ref=part.at[:, cols],
+            src_ref=part.at[peer],
             dst_ref=held.at[k],
             send_sem=send3.at[k],
             recv_sem=recv3.at[k],
@@ -391,7 +393,7 @@
         copy.start()
         sends.append(copy)
     own = pl.ds(pl.multiple_of(col * width, width), width)
-    total = part[:, own]
+    total = part[col]
     for copy in sends:
         copy.wait_send()
         copy.wait_recv()
@@ -429,7 +431,7 @@
             pltpu.VMEM((n_grp, back_rows, lanes), jnp.float32),
             pltpu.VMEM((back_rows, lanes), jnp.float32),
             pltpu.VMEM((3, pairs, row_count, lanes), jnp.float32),
-            pltpu.VMEM((row_count, out_weight.shape[1]), jnp.float32),
+            pltpu.VMEM((n_tp, row_count, out_cols), jnp.float32),
             pltpu.VMEM((n_tp, row_count, out_cols), jnp.float32),
             pltpu.SemaphoreType.DMA((n_grp,)),
             pltpu.SemaphoreType.DMA((n_grp,)),

time: 47.7 us -> 47.7 us (level)
  no operation moved by 1% of the time
where the time goes in v19:
time: 47.7 us; the launch traced here: 47.5 us
  Pallas kernels  46.2 us (97%)
  local copies, waits for them, and re-layouts  1.28 us (3%)
    pallas_call x1, Pallas kernels, per_device(): pl.pallas_call(functools.partial(whole_kernel, ny, nz, n_tp, slots), out_...  46.2 us
    unnamed x1, local copies, waits for them, and re-layouts  1.28 us

profile of v19, /device:TPU:1, one launch (start us, length us, event | category | flops | bytes accessed | tf_op | source)
XLA Modules:
  0.0 47.5 jit_solution(12318242997015817304)
XLA Ops:
  0.0 46.2 %shard_map.82 = bf16[8,256]{1,0:T(8,128)(2,1)} custom-call(s32[8]{0:T(128)} %lengths_ref.1, s32[8]{0:T(128)} %splits_ref.1, s32[4]{0:T(128)} %helpers_ref.1, bf16[8,256]{1,0:T(8,128)(2,1)} %queries_ref.1, bf16[8,2,64]{2,1,0:T(2,128)(2,1)} %kv_ref.1, bf16[8,2,1,512,128]{4,3,2,1,0:T(8,128)(2,1)} %home_hbm.1, bf16[4,2,1,512,128]{4,3,2,1,0:T(8,128)(2,1)} %help_hbm.1, ...), custom_call_target="tpu_custom_call" | custom-call | tf_op jit(solution)/shard_map/pallas_call | solution.py:419
  46.2 1.3 %copy.10 = bf16[8,256]{1,0:T(8,128)(2,1)} copy(bf16[8,256]{1,0:T(8,128)(2,1)} %shard_map.82) | data formatting | bytes 8192
